TPU v7x, 32 devices: a whole 2x2x4 slice. The times are simulated.
32 devices in a mesh: seq: 16 (over z, x, core), ch: 2 (over y).
Axes of the slice: x: 2, y: 2, z: 4, core: 2. Of those that a mesh axis runs over, the one named last changes fastest.
Arguments:
- tokens: bfloat16 [131072, 1024], P('seq', 'ch'), may hold values from -6 to 6
- right_block: bfloat16 [1024, 1024], P('seq'), may hold values from -0.1875 to 0.1875
- twiddle: bfloat16 [128, 1024], P('seq'), may hold values from -4 to 4
- left_block: bfloat16 [128, 128], replicated, may hold values from -0.5 to 0.5
- gain: float32 [1024], replicated, may hold values from 0.1 to 1.9
- mix_weight: bfloat16 [4, 256, 256], replicated, may hold values from -0.375 to 0.375
Outputs:
- layer_out: bfloat16 [131072, 1024], P(('seq', 'ch'))
All inputs are finite; a program needn't handle non-finite values.
Results may differ from a plain program's by a relative error of at most 0.007.
Values may be sent and summed in bfloat16 or wider, within the bound.
No kernel may reach another device: no remote copies, remote signals or barrier semaphores. Data moves between devices by JAX's collectives and lax.ppermute only.
A program may use at most 128 MiB of HBM per device.

v0:
```python
import jax
import jax.numpy as jnp
from jax import lax
from jax.sharding import PartitionSpec as P


def body(tokens, right_block, twiddle, left_block, gain, mix_weight):
    row_width = right_block.shape[1]
    row_count = tokens.shape[0] // row_width
    local_width = tokens.shape[1]
    inputs = tokens.reshape(row_count, row_width, local_width)
    whole_right = lax.all_gather(right_block, "seq", axis=0, tiled=True)
    first_section = jnp.einsum(
        "abc,bk->akc", inputs, whole_right, preferred_element_type=jnp.float32
    )
    spread = (first_section * twiddle.astype(jnp.float32)[:, :, None]).astype(jnp.bfloat16)
    mixed_rows = jnp.einsum(
        "ij,jbc->ibc",
        left_block,
        lax.all_to_all(spread, "seq", split_axis=1, concat_axis=0, tiled=True),
        preferred_element_type=jnp.float32,
    ).astype(jnp.bfloat16)
    sequence_mixed = lax.all_to_all(mixed_rows, "seq", split_axis=0, concat_axis=1, tiled=True)
    gated = (sequence_mixed.astype(jnp.float32) * jax.nn.silu(inputs.astype(jnp.float32))).astype(
        jnp.bfloat16
    )
    ch_count = lax.axis_size("ch")
    pieces = gated.reshape(ch_count, row_count * row_width // ch_count, local_width)
    shard_piece = lax.all_to_all(pieces, "ch", split_axis=0, concat_axis=2, tiled=True)
    values = shard_piece.astype(jnp.float32)
    inverse_rms = lax.rsqrt(jnp.mean(values * values, axis=-1, keepdims=True) + 1e-05)
    normed = (values * inverse_rms * gain).astype(jnp.bfloat16)
    block_count = mix_weight.shape[0]
    block_width = mix_weight.shape[1]
    normed = normed.reshape(shard_piece.shape[0], shard_piece.shape[1], block_count, block_width)
    result = jnp.einsum("otki,kij->otkj", normed, mix_weight, preferred_element_type=jnp.float32)
    mixed_out = result.astype(jnp.bfloat16).reshape(shard_piece.shape)
    return mixed_out.reshape(mixed_out.shape[1], mixed_out.shape[2])


def solution(mesh):
    in_specs = (P("seq", "ch"), P("seq", None), P("seq", None), P(), P(), P())
    out_specs = P(("seq", "ch"), None)
    return jax.shard_map(body, mesh=mesh, in_specs=in_specs, out_specs=out_specs, check_vma=False)
```

profile of v0, /device:TPU:0, one launch (start us, length us, event | category | flops | bytes accessed | tf_op | source)
XLA Modules:
  0.0 688.7 jit_solution(9891246923339993870)
XLA Ops:
  6.5 0.0 copy-start
  6.5 0.0 all-gather.2.cloned.1.call-start
  6.5 0.7 all-gather.2.cloned.1.call-update
  7.3 0.7 convert_element_type.77
  8.0 45.7 %all-gather.2.cloned.1.call-done = bf16[1024,1024]{1,0:T(8,128)(2,1)} async-done(((bf16[64,1024]{1,0:T(8,128)(2,1)}), bf16[1024,1024]{1,0:T(8,128)(2,1)}) %all-gather.2.cloned.1.call-update) | async-done | bytes 2097168 | tf_op jit(solution)/shard_map/all_gather | solution.py:12
  53.7 14.9 %fusion.5 = bf16[8,1024,512]{2,1,0:T(8,128)(2,1)} fusion(bf16[8,1024,512]{2,1,0:T(8,128)(2,1)} %bitcast.44, f32[8,1024]{1,0:T(8,128)S(1)} %convert_element_type.77, bf16[1024,1024]{1,0:T(8,128)(2,1)} %all-gather.2.cloned.1.call-done), kind=kOutput, calls=%fused_computation.11 | convolution fusion | flops 8598323200 | bytes 18907136 | tf_op jit(solution)/shard_map/abc,bk->akc/dot_general | solution.py:13
  68.6 11.3 %copy.26 = bf16[8,1024,512]{2,0,1:T(8,128)(2,1)} copy(bf16[8,1024,512]{2,1,0:T(8,128)(2,1)} %fusion.5) | data formatting | bytes 16777216 | tf_op jit(solution)/shard_map/convert_element_type | solution.py:16
  79.9 186.7 %all_to_all.36 = bf16[8,1024,512]{2,0,1:T(8,128)(2,1)} all-to-all(bf16[8,1024,512]{2,0,1:T(8,128)(2,1)} %copy.26), channel_id=1, replica_groups=mesh['seq'=16,'ch'=2] {'seq'}, dimensions={1} | all-to-all | bytes 16777216 | tf_op jit(solution)/shard_map/all_to_all | solution.py:20
  266.6 0.0 copy-start.1
  266.6 10.3 %copy.28 = bf16[16,8,64,512]{3,2,1,0:T(8,128)(2,1)} copy(bf16[16,8,64,512]{3,1,2,0:T(8,128)(2,1)} %bitcast.42) | data formatting | bytes 16777216 | tf_op jit(solution)/shard_map/all_to_all | solution.py:20
  276.9 0.0 copy-done.1
  276.9 22.4 %convert_bitcast_fusion.2 = bf16[128,64,512]{0,2,1:T(8,128)(2,1)} fusion(bf16[128,64,512]{2,1,0:T(8,128)(2,1)} %bitcast.43, bf16[128,128]{1,0:T(8,128)(2,1)S(1)} %copy-done.1), kind=kOutput, calls=%fused_computation.19 | convolution fusion | flops 1077936128 | bytes 16809984 | tf_op jit(solution)/shard_map/ij,jbc->ibc/dot_general | solution.py:17
  299.3 12.6 %copy.30 = bf16[128,64,512]{2,1,0:T(8,128)(2,1)} copy(bf16[128,64,512]{0,2,1:T(8,128)(2,1)} %convert_bitcast_fusion.2) | data formatting | bytes 16777216 | tf_op jit(solution)/shard_map/convert_element_type | solution.py:22
  311.9 187.2 %all_to_all.37 = bf16[128,64,512]{2,1,0:T(8,128)(2,1)} all-to-all(bf16[128,64,512]{2,1,0:T(8,128)(2,1)} %copy.30), channel_id=1, replica_groups=mesh['seq'=16,'ch'=2] {'seq'}, dimensions={0} | all-to-all | bytes 16777216 | tf_op jit(solution)/shard_map/all_to_all | solution.py:23
  499.1 0.0 slice-start
  499.1 11.7 %convert_bitcast_fusion.1 = f32[8,16,64,512]{3,2,0,1:T(8,128)} fusion(bf16[16,8,64,512]{3,2,1,0:T(8,128)(2,1)} %bitcast.40), kind=kLoop, calls=%fused_computation.9 | loop fusion | flops 4194304 | bytes 25165824 | tf_op jit(solution)/shard_map/convert_element_type | solution.py:24
  510.9 0.0 slice-start.1
  510.9 7.1 %copy.31 = f32[8,16,64,512]{3,2,1,0:T(8,128)S(1)} copy(f32[8,16,64,512]{3,2,0,1:T(8,128)} %convert_bitcast_fusion.1) | data formatting | bytes 33554432 | tf_op jit(solution)/shard_map/convert_element_type | solution.py:24
  518.0 0.0 slice-done
  518.0 0.0 slice-done.1
  518.0 7.0 %fusion.6 = bf16[2,4096,512]{2,1,0:T(8,128)(2,1)} fusion(f32[2,4096,512]{2,1,0:T(8,128)S(1)} %bitcast.39, bf16[2,4096,512]{2,1,0:T(8,128)(2,1)S(1)} %bitcast.47), kind=kLoop, calls=%fused_computation.13 | loop fusion | flops 29360128 | bytes 33554432 | tf_op jit(solution)/shard_map/convert_element_type | solution.py:24
  525.0 0.0 copy-start.2
  525.0 7.3 %all-to-all-start.2 = ((bf16[2,4096,512]{2,1,0:T(8,128)(2,1)}), bf16[2,4096,512]{2,1,0:T(8,128)(2,1)}, u32[]{:S(2)}, u32[]{:S(2)}) async-start(bf16[2,4096,512]{2,1,0:T(8,128)(2,1)} %fusion.6), calls=%async_computation.2 | async-start | bytes 16777216 | tf_op jit(solution)/shard_map/all_to_all | solution.py:29
  532.4 0.0 copy-done.2
  532.4 93.7 %all-to-all-done.2 = bf16[2,4096,512]{2,1,0:T(8,128)(2,1)} async-done(((bf16[2,4096,512]{2,1,0:T(8,128)(2,1)}), bf16[2,4096,512]{2,1,0:T(8,128)(2,1)}, u32[]{:S(2)}, u32[]{:S(2)}) %all-to-all-start.2) | async-done | bytes 8388640 | tf_op jit(solution)/shard_map/all_to_all | solution.py:29
  626.1 5.1 fusion
  631.2 11.5 %convert_bitcast_fusion = f32[1,4096,2,512]{3,1,2,0:T(8,128)} fusion(bf16[2,4096,512]{2,1,0:T(8,128)(2,1)} %all-to-all-done.2), kind=kLoop, calls=%fused_computation.3 | loop fusion | flops 4194304 | bytes 25165824 | tf_op jit(solution)/shard_map/convert_element_type | solution.py:30
  642.7 17.6 %copy.32 = f32[1,4096,2,512]{1,3,2,0:T(8,128)} copy(f32[1,4096,2,512]{3,1,2,0:T(8,128)} %convert_bitcast_fusion) | data formatting | bytes 33554432 | tf_op jit(solution)/shard_map/convert_element_type | solution.py:30
  660.3 0.0 copy-done
  660.3 9.2 %fusion.12 = bf16[4,4096,256]{1,2,0:T(8,128)(2,1)} fusion(bf16[4,256,256]{2,1,0:T(8,128)(2,1)S(1)} %copy-done, f32[4096,4,256]{0,2,1:T(8,128)} %bitcast.38, f32[4,256]{1,0:T(4,128)S(1)} %mul.58, f32[4096]{0:T(1024)S(1)} %add_rsqrt_fusion), kind=kOutput, calls=%fused_computation.20 | convolution fusion | flops 2164260864 | bytes 25710592 | tf_op jit(solution)/shard_map/otki,kij->otkj/dot_general | solution.py:36
  669.5 11.9 %copy.35 = bf16[4096,1024]{1,0:T(8,128)(2,1)} copy(bf16[4096,1024]{0,1:T(8,128)(2,1)} %bitcast.41) | data formatting | bytes 16777216 | tf_op jit(solution)/shard_map/reshape;reshape | solution.py:38
  (3 shorter events, 0.0 us)
Async XLA Ops:
  6.5 653.8 %copy-start = (bf16[4,256,256]{2,1,0:T(8,128)(2,1)S(1)}, bf16[4,256,256]{2,1,0:T(8,128)(2,1)}, u32[]{:S(2)}) copy-start(bf16[4,256,256]{2,1,0:T(8,128)(2,1)} %param.11) | copy-start | bytes 1572868
  6.5 47.2 %all-gather.2.cloned.1.call-start = ((), (), s32[]{:S(2)}) async-start(), calls=%async_computation.3 | async-start | bytes 2228224 | tf_op jit(solution)/shard_map/all_gather | solution.py:12
  266.6 10.3 %copy-start.1 = (bf16[128,128]{1,0:T(8,128)(2,1)S(1)}, bf16[128,128]{1,0:T(8,128)(2,1)}, u32[]{:S(2)}) copy-start(bf16[128,128]{1,0:T(8,128)(2,1)} %param.9) | copy-start | bytes 98308
  499.1 18.9 %slice-start = ((s8[8388608]{0:T(1024)(128)(4,1)}), s8[4194304]{0:T(1024)(128)(4,1)S(1)}, s32[]{:S(2)}) async-start(s8[8388608]{0:T(1024)(128)(4,1)} %bitcast.45), calls=%async_computation.4 | async-start | bytes 8388608
  510.9 7.1 %slice-start.1 = ((s8[8388608]{0:T(1024)(128)(4,1)}), s8[4194304]{0:T(1024)(128)(4,1)S(1)}, s32[]{:S(2)}) async-start(s8[8388608]{0:T(1024)(128)(4,1)} %bitcast.45), calls=%async_computation.5 | async-start | bytes 8388608
  525.0 7.3 %copy-start.2 = (f32[1024]{0:T(1024)S(1)}, f32[1024]{0:T(1024)}, u32[]{:S(2)}) copy-start(f32[1024]{0:T(1024)} %param.10) | copy-start | bytes 12292
  525.0 101.1 %all-to-all-start.2 = ((bf16[2,4096,512]{2,1,0:T(8,128)(2,1)}), bf16[2,4096,512]{2,1,0:T(8,128)(2,1)}, u32[]{:S(2)}, u32[]{:S(2)}) async-start(bf16[2,4096,512]{2,1,0:T(8,128)(2,1)} %fusion.6), calls=%async_computation.2 | async-start | bytes 16777216 | tf_op jit(solution)/shard_map/all_to_all | solution.py:29
Sparse Core Ops, SparseCore 0:
  9.5 44.1 all-gather.1
where the time goes:
time: 697 us; the launch traced here: 689 us
  blocking collectives  374 us (54%)
  waiting for transfers between devices  140 us (20%)
  local copies, waits for them, and re-layouts  70.9 us (10%)
  matrix products  46.4 us (7%)
  other arithmetic  36.1 us (5%)
  between operations  13.9 us (2%)
  starting transfers between devices  7.33 us (1%)
    all_to_all x1, blocking collectives, body(): lax.all_to_all(mixed_rows, 'seq', split_axis=0, concat_axis=1, tiled=True)  187 us
    all_to_all x1, blocking collectives, body(): lax.all_to_all(spread, 'seq', split_axis=1, concat_axis=0, tiled=True)  187 us
    all_to_all x1, waiting for transfers between devices, body(): lax.all_to_all(pieces, 'ch', split_axis=0, concat_axis=2, tiled=True)  93.7 us
    all_gather x1, waiting for transfers between devices, body(): whole_right = lax.all_gather(right_block, 'seq', axis=0, tiled=True)  45.7 us
    dot_general x1, matrix products, body(): jnp.einsum('ij,jbc->ibc', left_block, lax.all_to_all(spread, 'seq', split...  22.4 us
    convert_element_type x1, local copies, waits for them, and re-layouts, body(): values = shard_piece.astype(jnp.float32)  17.6 us
    dot_general x1, matrix products, body(): jnp.einsum('abc,bk->akc', inputs, whole_right, preferred_element_type=jnp...  14.9 us
  transfers between devices with their start and end apart: 2, of which 2 were waited for; matrix products, arithmetic and copies ran while one was open for 0% of the time, Pallas kernels for 0%

commit v1 on v0

--- a/solution.py
+++ b/solution.py
@@ -1,10 +1,431 @@
+import functools
+
 import jax
 import jax.numpy as jnp
 from jax import lax
+from jax.experimental import pallas as pl
+from jax.experimental.pallas import tpu as pltpu
 from jax.sharding import PartitionSpec as P
 
 
-def body(tokens, right_block, twiddle, left_block, gain, mix_weight):
+ANY = pl.BlockSpec(memory_space=pl.ANY)
+VMEM = pl.BlockSpec(memory_space=pltpu.VMEM)
+LANES = 256
+CHUNKS = 2
+STEP = 16
+
+
+class Plan:
+    def __init__(self, tokens, right_block, twiddle, left_block, mix_weight):
+        self.seq = lax.axis_size("seq")
+        self.ch = lax.axis_size("ch")
+        self.width = right_block.shape[1]
+        self.rows = tokens.shape[0] // self.width
+        self.local = tokens.shape[1]
+        self.right_rows = right_block.shape[0]
+        self.all_rows = left_block.shape[0]
+        self.chunk = self.local // CHUNKS
+        self.own = self.chunk // self.seq
+        self.out_rows = self.rows // self.ch
+        self.channels = self.local * self.ch
+        self.mix = mix_weight.shape[1]
+        self.near = 1
+        while self.near * self.near < self.seq:
+            self.near *= 2
+        pad = self.right_rows + twiddle.shape[0]
+        self.gather_rows = pad + (-pad) % 16
+
+    def fits(self):
+        s, c = self.seq, self.ch
+        return (
+            s > 1
+            and s <= 16
+            and c > 1
+            and c <= 4
+            and s & (s - 1) == 0
+            and c & (c - 1) == 0
+            and self.own % 16 == 0
+            and self.own > 0
+            and self.chunk % 128 == 0
+            and self.rows % 8 == 0
+            and STEP % self.rows == 0
+            and self.rows % c == 0
+            and self.all_rows % STEP == 0
+            and self.right_rows % 16 == 0
+            and self.width % LANES == 0
+            and self.mix % 128 == 0
+            and self.chunk % self.mix == 0
+        )
+
+
+def prep_kernel(plan, split, x_ref, *rest):
+    c, s = plan.ch, plan.seq
+    count = s if split else 1
+    outs, shares, (turned, share_sem, piece_sem) = rest[:count], rest[count : count + c], rest[-3:]
+    me, y = lax.axis_index("seq"), lax.axis_index("ch")
+    a = pl.program_id(0)
+    value = x_ref[...].T
+    turned[a] = value
+    if not split:
+        outs[0][...] = value.reshape(s, 1, plan.own, plan.width)
+
+    def rows_of(m):
+        who = jnp.bitwise_xor(me, m)
+        return pl.ds(pl.multiple_of(who * plan.own, plan.own), plan.own)
+
+    if split:
+        for m in range(s):
+            pltpu.make_async_copy(
+                turned.at[a, rows_of(m), :], outs[m].at[a], piece_sem.at[m]
+            ).start()
+
+    @pl.when(a == plan.rows - 1)
+    def _():
+        copies = [
+            pltpu.make_async_copy(
+                turned.at[pl.ds(jnp.bitwise_xor(y, m) * plan.out_rows, plan.out_rows)],
+                shares[m],
+                share_sem.at[m],
+            )
+            for m in range(c)
+        ]
+        for copy in copies:
+            copy.start()
+        if split:
+            for m in range(s):
+                pltpu.make_async_copy(
+                    turned.at[:, rows_of(m), :], outs[m], piece_sem.at[m]
+                ).wait()
+        for copy in copies:
+            copy.wait()
+
+
+def prep(plan, tokens, chunk, split):
+    share = jax.ShapeDtypeStruct((plan.out_rows, plan.chunk, plan.width), jnp.bfloat16)
+    if split:
+        shape = (plan.rows, plan.own, plan.width)
+        count, spec = plan.seq, ANY
+    else:
+        shape = (plan.seq, plan.rows, plan.own, plan.width)
+        count = 1
+        spec = pl.BlockSpec((plan.seq, 1, plan.own, plan.width), lambda a: (0, a, 0, 0))
+    out = pl.pallas_call(
+        functools.partial(prep_kernel, plan, split),
+        out_shape=[jax.ShapeDtypeStruct(shape, jnp.bfloat16)] * count + [share] * plan.ch,
+        grid=(plan.rows,),
+        in_specs=[pl.BlockSpec((plan.width, plan.chunk), lambda a: (a, chunk))],
+        out_specs=[spec] * count + [ANY] * plan.ch,
+        scratch_shapes=[
+            pltpu.VMEM((plan.rows, plan.chunk, plan.width), jnp.bfloat16),
+            pltpu.SemaphoreType.DMA((plan.ch,)),
+            pltpu.SemaphoreType.DMA((plan.seq,)),
+        ],
+        cost_estimate=pl.CostEstimate(
+            flops=0,
+            bytes_accessed=6 * plan.rows * plan.chunk * plan.width,
+            transcendentals=0,
+        ),
+        name="prep",
+    )(tokens)
+    return out[:count], out[count:]
+
+
+def sections_kernel(plan, count, *refs):
+    near, far, own = plan.near, plan.seq // plan.near, plan.own
+    pieces, gathered, left = refs[:count], refs[count : count + near], refs[count + near]
+    out, x, right, twiddle, first, mixed, sem_x, sem_r, sem_t = refs[count + near + 1 :]
+    me = lax.axis_index("seq")
+    if count == 1:
+        copies = [pltpu.make_async_copy(pieces[0], x, sem_x.at[0])]
+    else:
+        copies = [
+            pltpu.make_async_copy(
+                pieces[m], x.at[pl.ds(jnp.bitwise_xor(me, m) * plan.rows, plan.rows)], sem_x.at[m]
+            )
+            for m in range(count)
+        ]
+    for m in range(near):
+        for n in range(far):
+            who = jnp.bitwise_xor(me, n * near + m)
+            at = pl.ds(pl.multiple_of(who * plan.right_rows, plan.right_rows), plan.right_rows)
+            source = gathered[m].at[n]
+            copies.append(
+                pltpu.make_async_copy(
+                    source.at[pl.ds(0, plan.right_rows)], right.at[at], sem_r.at[m * far + n]
+                )
+            )
+            copies.append(
+                pltpu.make_async_copy(
+                    source.at[pl.ds(plan.right_rows, plan.rows)],
+                    twiddle.at[who],
+                    sem_t.at[m * far + n],
+                )
+            )
+    kt = pl.program_id(0)
+
+    @pl.when(kt == 0)
+    def _():
+        for copy in copies:
+            copy.start()
+        for copy in copies:
+            copy.wait()
+
+    ks = pl.ds(pl.multiple_of(kt * LANES, LANES), LANES)
+
+    def section_one(t, carry):
+        rows = x[pl.ds(t * STEP, STEP)].reshape(STEP * own, plan.width)
+        value = jnp.dot(rows, right[:, ks], preferred_element_type=jnp.float32)
+        value = value.reshape(STEP, own, LANES)
+        group = STEP // plan.rows
+        factor = twiddle[pl.ds(t * group, group), :, ks].astype(jnp.float32)
+        value = value * factor.reshape(STEP, LANES)[:, None, :]
+        at = pl.ds(pl.multiple_of(t * STEP, STEP), STEP)
+        first[:, at, :] = jnp.swapaxes(value, 0, 1).astype(jnp.bfloat16)
+        return carry
+
+    lax.fori_loop(0, plan.all_rows // STEP, section_one, 0)
+    for q in range(own):
+        mixed[q] = jnp.dot(left[...], first[q], preferred_element_type=jnp.float32)
+
+    def turn(t, carry):
+        at = pl.ds(pl.multiple_of(t * STEP, STEP), STEP)
+        value = jnp.swapaxes(mixed[:, at, :], 0, 1)
+        out[pl.ds(t * STEP, STEP)] = value.astype(jnp.bfloat16)
+        return carry
+
+    lax.fori_loop(0, plan.all_rows // STEP, turn, 0)
+
+
+def sections(plan, pieces, gathered, left):
+    s, own, width, bf16 = plan.seq, plan.own, plan.width, jnp.bfloat16
+    flops = 2 * plan.all_rows * own * width * (width + plan.all_rows)
+    return pl.pallas_call(
+        functools.partial(sections_kernel, plan, len(pieces)),
+        out_shape=jax.ShapeDtypeStruct((plan.all_rows, own, width), bf16),
+        grid=(width // LANES,),
+        in_specs=[ANY] * (len(pieces) + len(gathered)) + [VMEM],
+        out_specs=pl.BlockSpec((plan.all_rows, own, LANES), lambda k: (0, 0, k)),
+        scratch_shapes=[
+            pltpu.VMEM((plan.all_rows, own, width), bf16),
+            pltpu.VMEM((s * plan.right_rows, width), bf16),
+            pltpu.VMEM((s, plan.rows, width), bf16),
+            pltpu.VMEM((own, plan.all_rows, LANES), bf16),
+            pltpu.VMEM((own, plan.all_rows, LANES), jnp.float32),
+            pltpu.SemaphoreType.DMA((s,)),
+            pltpu.SemaphoreType.DMA((s,)),
+            pltpu.SemaphoreType.DMA((s,)),
+        ],
+        cost_estimate=pl.CostEstimate(
+            flops=flops,
+            bytes_accessed=4 * plan.all_rows * own * width + 2 * width * width,
+            transcendentals=0,
+        ),
+        name="sections",
+    )(*pieces, *gathered, left)
+
+
+def load_chunk(plan, piece, shares, mixed, inputs, sem_m, sem_i):
+    s, c, own = plan.seq, plan.ch, plan.own
+    y = lax.axis_index("ch")
+    for r in range(plan.out_rows):
+        for n in range(c):
+            at = pl.ds(jnp.bitwise_xor(y, n) * plan.chunk, plan.chunk)
+            pltpu.make_async_copy(shares[n].at[r], inputs.at[r, at], sem_i.at[r]).start()
+        for m in range(s * c):
+            row = (m % c) * plan.chunk + (m // c) * own
+            pltpu.make_async_copy(
+                piece.at[m, r], mixed.at[r, pl.ds(row, own)], sem_m.at[r]
+            ).start()
+
+
+def gate_tile(plan, mixed, inputs, i, ks):
+    total = jnp.zeros((1, LANES), jnp.float32)
+    for j in range(plan.chunk * plan.ch // plan.mix):
+        rs = pl.ds(j * plan.mix, plan.mix)
+        value = mixed[i, rs, ks].astype(jnp.float32)
+        gate = inputs[i, rs, ks].astype(jnp.float32)
+        gated = (value * (gate / (1.0 + jnp.exp(-gate)))).astype(jnp.bfloat16)
+        mixed[i, rs, ks] = gated
+        gated = gated.astype(jnp.float32)
+        total = total + jnp.sum(gated * gated, axis=0, keepdims=True)
+    return total
+
+
+def columns(plan, chunk, j):
+    return (j * plan.mix // plan.chunk) * plan.local + chunk * plan.chunk + (
+        j * plan.mix % plan.chunk
+    )
+
+
+def turn_dot(value, weight):
+    return lax.dot_general(
+        value, weight, (((0,), (0,)), ((), ())), preferred_element_type=jnp.float32
+    )
+
+
+def gate_kernel(plan, *refs):
+    c = plan.ch
+    piece, shares = refs[0], refs[1 : 1 + c]
+    gain, weight, out, totals, mixed, inputs, sem_m, sem_i = refs[1 + c :]
+    i = pl.program_id(0)
+
+    @pl.when(i == 0)
+    def _():
+        load_chunk(plan, piece, shares, mixed, inputs, sem_m, sem_i)
+
+    pltpu.make_async_copy(inputs.at[i], inputs.at[i], sem_i.at[i]).wait()
+    pltpu.make_async_copy(mixed.at[i], mixed.at[i], sem_m.at[i]).wait()
+
+    def tile(kt, carry):
+        ks = pl.ds(pl.multiple_of(kt * LANES, LANES), LANES)
+        total = gate_tile(plan, mixed, inputs, i, ks)
+        totals[0, :, ks] = jnp.broadcast_to(total, (8, LANES))
+        for j in range(plan.chunk * c // plan.mix):
+            col = columns(plan, 0, j)
+            value = mixed[i, pl.ds(j * plan.mix, plan.mix), ks].astype(jnp.float32)
+            value = (value * gain[pl.ds(col, plan.mix), :]).astype(jnp.bfloat16)
+            out[ks, pl.ds(j * plan.mix, plan.mix)] = turn_dot(value, weight[col // plan.mix])
+        return carry
+
+    lax.fori_loop(0, plan.width // LANES, tile, 0)
+
+
+def final_kernel(plan, *refs):
+    c = plan.ch
+    piece, shares = refs[0], refs[1 : 1 + c]
+    held, before, gain, weight, out, mixed, inputs, sem_m, sem_i = refs[1 + c :]
+    i = pl.program_id(0)
+
+    @pl.when(i == 0)
+    def _():
+        load_chunk(plan, piece, shares, mixed, inputs, sem_m, sem_i)
+
+    pltpu.make_async_copy(inputs.at[i], inputs.at[i], sem_i.at[i]).wait()
+    pltpu.make_async_copy(mixed.at[i], mixed.at[i], sem_m.at[i]).wait()
+
+    def tile(kt, carry):
+        ks = pl.ds(pl.multiple_of(kt * LANES, LANES), LANES)
+        total = gate_tile(plan, mixed, inputs, i, ks) + before[0, pl.ds(0, 1), ks]
+        inverse = lax.rsqrt(total * (1.0 / plan.channels) + 1e-05)
+        for j in range(plan.chunk * c // plan.mix):
+            col = columns(plan, 1, j)
+            value = mixed[i, pl.ds(j * plan.mix, plan.mix), ks].astype(jnp.float32)
+            value = (value * inverse * gain[pl.ds(col, plan.mix), :]).astype(jnp.bfloat16)
+            result = turn_dot(value, weight[col // plan.mix])
+            out[ks, pl.ds(col, plan.mix)] = result.astype(jnp.bfloat16)
+        scale = jnp.broadcast_to(inverse, (128, LANES)).T
+        for j in range(plan.chunk * c // 128):
+            result = held[ks, pl.ds(j * 128, 128)] * scale
+            col = (j * 128 // plan.chunk) * plan.local + j * 128 % plan.chunk
+            out[ks, pl.ds(col, 128)] = result.astype(jnp.bfloat16)
+        return carry
+
+    lax.fori_loop(0, plan.width // LANES, tile, 0)
+
+
+def tail_scratch(plan):
+    shape = (plan.out_rows, plan.chunk * plan.ch, plan.width)
+    return [
+        pltpu.VMEM(shape, jnp.bfloat16),
+        pltpu.VMEM(shape, jnp.bfloat16),
+        pltpu.SemaphoreType.DMA((plan.out_rows,)),
+        pltpu.SemaphoreType.DMA((plan.out_rows,)),
+    ]
+
+
+def gate(plan, piece, shares, gain, weight):
+    size, part = plan.out_rows * plan.width, plan.chunk * plan.ch
+    return pl.pallas_call(
+        functools.partial(gate_kernel, plan),
+        out_shape=[
+            jax.ShapeDtypeStruct((size, part), jnp.float32),
+            jax.ShapeDtypeStruct((plan.out_rows, 8, plan.width), jnp.float32),
+        ],
+        grid=(plan.out_rows,),
+        in_specs=[ANY] * (1 + plan.ch) + [VMEM, VMEM],
+        out_specs=[
+            pl.BlockSpec((plan.width, part), lambda i: (i, 0)),
+            pl.BlockSpec((1, 8, plan.width), lambda i: (i, 0, 0)),
+        ],
+        scratch_shapes=tail_scratch(plan),
+        cost_estimate=pl.CostEstimate(
+            flops=2 * size * part * plan.mix,
+            bytes_accessed=8 * size * part,
+            transcendentals=size * part,
+        ),
+        name="gate",
+    )(piece, *shares, gain, weight)
+
+
+def final(plan, piece, shares, held, before, gain, weight):
+    size, part = plan.out_rows * plan.width, plan.chunk * plan.ch
+    return pl.pallas_call(
+        functools.partial(final_kernel, plan),
+        out_shape=jax.ShapeDtypeStruct((size, plan.channels), jnp.bfloat16),
+        grid=(plan.out_rows,),
+        in_specs=[ANY] * (1 + plan.ch)
+        + [
+            pl.BlockSpec((plan.width, part), lambda i: (i, 0)),
+            pl.BlockSpec((1, 8, plan.width), lambda i: (i, 0, 0)),
+            VMEM,
+            VMEM,
+        ],
+        out_specs=pl.BlockSpec((plan.width, plan.channels), lambda i: (i, 0)),
+        scratch_shapes=tail_scratch(plan),
+        cost_estimate=pl.CostEstimate(
+            flops=2 * size * part * plan.mix,
+            bytes_accessed=10 * size * part,
+            transcendentals=size * part,
+        ),
+        name="final",
+    )(piece, *shares, held, before, gain, weight)
+
+
+def swap(value, mask, axis):
+    count = lax.axis_size(axis)
+    return lax.ppermute(value, axis, [(i, i ^ mask) for i in range(count)])
+
+
+def exchange(value, axes):
+    return lax.all_to_all(value, axes, split_axis=0, concat_axis=0, tiled=True)
+
+
+def chunked_body(plan, tokens, right_block, twiddle, left_block, gain, mix_weight):
+    s, c, near, own = plan.seq, plan.ch, plan.near, plan.own
+    pad = plan.gather_rows - right_block.shape[0] - twiddle.shape[0]
+    zeros = jnp.zeros((pad, plan.width), jnp.bfloat16)
+    held = jnp.concatenate([right_block, twiddle, zeros], axis=0)[None]
+    gain = jnp.broadcast_to(gain[:, None], (plan.channels, LANES))
+    column = [held]
+    for n in range(1, s // near):
+        column.append(swap(held, n * near, "seq"))
+    column = jnp.concatenate(column, axis=0)
+    gathered = [column]
+    for m in range(1, near):
+        gathered.append(swap(column, m, "seq"))
+    arrived, shares = [], []
+    for k in range(CHUNKS):
+        pieces, share = prep(plan, tokens, k, k == 1)
+        if k == 0:
+            block = exchange(pieces[0], "seq")
+            arrived.append([block.reshape(plan.all_rows, own, plan.width)])
+        else:
+            arrived.append([pieces[0]] + [None] * (s - 1))
+            for m in reversed(range(1, s)):
+                arrived[k][m] = swap(pieces[m], m, "seq")
+        shares.append([share[0]])
+        for n in range(1, c):
+            shares[k].append(swap(share[n], n, "ch"))
+    landed = []
+    for k in range(CHUNKS):
+        out = sections(plan, arrived[k], gathered, left_block)
+        out = out.reshape(s * c, plan.out_rows, own, plan.width)
+        landed.append(exchange(out, ("seq", "ch")))
+    held, before = gate(plan, landed[0], shares[0], gain, mix_weight)
+    return final(plan, landed[1], shares[1], held, before, gain, mix_weight)
+
+
+def plain_body(tokens, right_block, twiddle, left_block, gain, mix_weight):
     row_width = right_block.shape[1]
     row_count = tokens.shape[0] // row_width
     local_width = tokens.shape[1]
@@ -38,6 +459,13 @@
     return mixed_out.reshape(mixed_out.shape[1], mixed_out.shape[2])
 
 
+def body(tokens, right_block, twiddle, left_block, gain, mix_weight):
+    plan = Plan(tokens, right_block, twiddle, left_block, mix_weight)
+    if plan.fits():
+        return chunked_body(plan, tokens, right_block, twiddle, left_block, gain, mix_weight)
+    return plain_body(tokens, right_block, twiddle, left_block, gain, mix_weight)
+
+
 def solution(mesh):
     in_specs = (P("seq", "ch"), P("seq", None), P("seq", None), P(), P(), P())
     out_specs = P(("seq", "ch"), None)

time: 697 us -> 544 us (0.78); the launches traced: 689 us -> 543 us
  blocking collectives: 374 us -> 0 us
  waiting for transfers between devices: 140 us -> 388 us
  Pallas kernels: 0 us -> 85.9 us
  local copies, waits for them, and re-layouts: 70.9 us -> 4.42 us
  starting transfers between devices: 7.33 us -> 64.4 us
  matrix products: 46.4 us -> 0 us
  other arithmetic: 36.1 us -> 0.17 us
  between operations: 13.9 us -> 0.29 us
    ppermute x0 -> x23, waiting for transfers between devices: none -> 388 us  [swap(): return lax.ppermute(value, axis, [(i, i ^ mask) for i in range(count)])]
    all_to_all x2 -> x0, blocking collectives: 374 us -> none  [the longest x1 187 us: body(): lax.all_to_all(mixed_rows, 'seq', split_axis=0, concat_axis=1, tiled=True)]
    all_to_all x1 -> x3, waiting for transfers between devices: 93.7 us -> 0.01 us  [exchange(): return lax.all_to_all(value, axes, split_axis=0, concat_axis=0, tiled=True)]
    pallas_call x0 -> x6, Pallas kernels: none -> 85.9 us  [the longest x2 39 us: sections(): pl.pallas_call(functools.partial(sections_kernel, plan, len(pieces)), out...]
    convert_element_type x4 -> x0, local copies, waits for them, and re-layouts: 48.6 us -> none  [the longest x1 17.6 us: body(): values = shard_piece.astype(jnp.float32)]
    dot_general x3 -> x0, matrix products: 46.4 us -> none  [the longest x1 22.4 us: body(): jnp.einsum('ij,jbc->ibc', left_block, lax.all_to_all(spread, 'seq', split...]
    all_gather x1 -> x0, waiting for transfers between devices: 45.7 us -> none  [body(): whole_right = lax.all_gather(right_block, 'seq', axis=0, tiled=True)]
    convert_element_type x4 -> x0, other arithmetic: 31 us -> none  [the longest x1 11.7 us: body(): sequence_mixed.astype(jnp.float32) * jax.nn.silu(inputs.astype(jnp.float32))]
  transfers between devices with their start and end apart: 2 -> 26, of which waited for: 2 -> 16; matrix products, arithmetic and copies ran while one was open for 0% -> 0% of each run, Pallas kernels for 0% -> 8%
where the time goes in v1:
time: 544 us; the launch traced here: 543 us
  waiting for transfers between devices  388 us (71%)
  Pallas kernels  85.9 us (16%)
  starting transfers between devices  64.4 us (12%)
    ppermute x23, waiting for transfers between devices, swap(): return lax.ppermute(value, axis, [(i, i ^ mask) for i in range(count)])  388 us
    pallas_call x2, Pallas kernels, sections(): pl.pallas_call(functools.partial(sections_kernel, plan, len(pieces)), out...  39 us
    all_to_all x3, starting transfers between devices, exchange(): return lax.all_to_all(value, axes, split_axis=0, concat_axis=0, tiled=True)  36.2 us
    ppermute x23, starting transfers between devices, swap(): return lax.ppermute(value, axis, [(i, i ^ mask) for i in range(count)])  28.2 us
    pallas_call x2, Pallas kernels, prep(): pl.pallas_call(functools.partial(prep_kernel, plan, split), out_shape=[ja...  18.4 us
    pallas_call x1, Pallas kernels, final(): pl.pallas_call(functools.partial(final_kernel, plan), out_shape=jax.Shape...  15.3 us
    pallas_call x1, Pallas kernels, gate(): pl.pallas_call(functools.partial(gate_kernel, plan), out_shape=[jax.Shape...  13.2 us
  transfers between devices with their start and end apart: 26, of which 16 were waited for; matrix products, arithmetic and copies ran while one was open for 0% of the time, Pallas kernels for 8%

profile of v1, /device:TPU:0, one launch (start us, length us, event | category | flops | bytes accessed | tf_op | source)
XLA Modules:
  0.0 542.9 jit_solution(10467960749979507241)
XLA Ops:
  0.0 9.6 %prep.3 = (bf16[16,8,16,1024]{3,2,1,0:T(8,128)(2,1)}, bf16[4,256,1024]{2,1,0:T(8,128)(2,1)}, bf16[4,256,1024]{2,1,0:T(8,128)(2,1)}) custom-call(bf16[8192,512]{1,0:T(8,128)(2,1)} %x_ref.3), custom_call_target="tpu_custom_call" | custom-call | bytes 12582912 | tf_op jit(solution)/shard_map/prep/pallas_call | solution.py:112
  9.6 7.6 %all-to-all-start.1 = ((bf16[16,8,16,1024]{3,2,1,0:T(8,128)(2,1)}), bf16[16,8,16,1024]{3,2,1,0:T(8,128)(2,1)}, u32[]{:S(2)}, u32[]{:S(2)}) async-start(bf16[16,8,16,1024]{3,2,1,0:T(8,128)(2,1)} %get-tuple-element.46), calls=%async_computation.1 | async-start | bytes 8388608 | tf_op jit(solution)/shard_map/all_to_all | solution.py:390
  17.4 3.7 collective-permute-start.17
  21.9 72.0 %collective-permute-done.17 = bf16[1,80,1024]{2,1,0:T(8,128)(2,1)S(1)} collective-permute-done((bf16[1,80,1024]{2,1,0:T(8,128)(2,1)S(1)}, bf16[1,80,1024]{2,1,0:T(8,128)(2,1)S(1)}, u32[]{:S(2)}, u32[]{:S(2)}) %collective-permute-start.17) | collective-permute-done | bytes 163872 | tf_op jit(solution)/shard_map/ppermute | solution.py:386
  93.8 31.4 %collective-permute-done.16 = bf16[1,80,1024]{2,1,0:T(8,128)(2,1)S(1)} collective-permute-done((bf16[1,80,1024]{2,1,0:T(8,128)(2,1)S(1)}, bf16[1,80,1024]{2,1,0:T(8,128)(2,1)S(1)}, u32[]{:S(2)}, u32[]{:S(2)}) %collective-permute-start.16) | collective-permute-done | bytes 163872 | tf_op jit(solution)/shard_map/ppermute | solution.py:386
  127.3 15.1 %collective-permute-done.20.refs_19_.refs_4_ = bf16[4,80,1024]{2,1,0:T(8,128)(2,1)S(1)} collective-permute-done((bf16[4,80,1024]{2,1,0:T(8,128)(2,1)S(1)}, bf16[4,80,1024]{2,1,0:T(8,128)(2,1)S(1)}, u32[]{:S(2)}, u32[]{:S(2)}) %collective-permute-start.20) | collective-permute-done | bytes 655392 | tf_op jit(solution)/shard_map/ppermute | solution.py:386
  142.4 14.1 %collective-permute-done.19.refs_18_.refs_3_ = bf16[4,80,1024]{2,1,0:T(8,128)(2,1)S(1)} collective-permute-done((bf16[4,80,1024]{2,1,0:T(8,128)(2,1)S(1)}, bf16[4,80,1024]{2,1,0:T(8,128)(2,1)S(1)}, u32[]{:S(2)}, u32[]{:S(2)}) %collective-permute-start.19) | collective-permute-done | bytes 655392 | tf_op jit(solution)/shard_map/ppermute | solution.py:386
  157.5 19.6 %sections.3 = bf16[128,16,1024]{2,1,0:T(8,128)(2,1)} custom-call(bf16[128,16,1024]{2,1,0:T(8,128)(2,1)} %bitcast.2.refs_0_, bf16[4,80,1024]{2,1,0:T(8,128)(2,1)} %copy-done.1, bf16[4,80,1024]{2,1,0:T(8,128)(2,1)} %copy-done.7, bf16[4,80,1024]{2,1,0:T(8,128)(2,1)} %copy-done.6, bf16[4,80,1024]{2,1,0:T(8,128)(2,1)} %copy-done.5, bf16[128,128]{1,0:T(8,128)(2,1)} %refs_5_.1), custom_call_target="tpu_custom_call" | custom-call | flops 4831838208 | bytes 10485760 | tf_op jit(solution)/shard_map/sections/pallas_call | solution.py:202
  177.2 3.6 all-to-all-start.2
  180.8 8.8 %prep.2 = (bf16[8,16,1024]{2,1,0:T(8,128)(2,1)}, bf16[8,16,1024]{2,1,0:T(8,128)(2,1)}, bf16[8,16,1024]{2,1,0:T(8,128)(2,1)}, bf16[8,16,1024]{2,1,0:T(8,128)(2,1)...) custom-call(bf16[8192,512]{1,0:T(8,128)(2,1)} %x_ref.3), custom_call_target="tpu_custom_call" | custom-call | bytes 12582912 | tf_op jit(solution)/shard_map/prep/pallas_call | solution.py:112
  193.3 2.6 collective-permute-start.5
  195.8 22.9 %collective-permute-done.1.refs_2_ = bf16[8,16,1024]{2,1,0:T(8,128)(2,1)S(1)} collective-permute-done((bf16[8,16,1024]{2,1,0:T(8,128)(2,1)}, bf16[8,16,1024]{2,1,0:T(8,128)(2,1)S(1)}, u32[]{:S(2)}, u32[]{:S(2)}) %collective-permute-start.1) | collective-permute-done | bytes 262176 | tf_op jit(solution)/shard_map/ppermute | solution.py:386
  218.7 8.8 %collective-permute-done.2.refs_3_ = bf16[8,16,1024]{2,1,0:T(8,128)(2,1)S(1)} collective-permute-done((bf16[8,16,1024]{2,1,0:T(8,128)(2,1)}, bf16[8,16,1024]{2,1,0:T(8,128)(2,1)S(1)}, u32[]{:S(2)}, u32[]{:S(2)}) %collective-permute-start.2) | collective-permute-done | bytes 262176 | tf_op jit(solution)/shard_map/ppermute | solution.py:386
  227.5 28.9 %collective-permute-done.3.refs_4_ = bf16[8,16,1024]{2,1,0:T(8,128)(2,1)S(1)} collective-permute-done((bf16[8,16,1024]{2,1,0:T(8,128)(2,1)}, bf16[8,16,1024]{2,1,0:T(8,128)(2,1)S(1)}, u32[]{:S(2)}, u32[]{:S(2)}) %collective-permute-start.3) | collective-permute-done | bytes 262176 | tf_op jit(solution)/shard_map/ppermute | solution.py:386
  256.4 2.0 collective-permute-start.8
  258.5 3.6 collective-permute-done.4.refs_5_
  262.1 3.1 collective-permute-start.9
  265.2 5.2 collective-permute-done.5.refs_6_
  270.4 1.7 collective-permute-start.10
  272.2 3.9 collective-permute-done.6.refs_7_
  276.1 5.1 collective-permute-start.11
  281.2 28.9 %collective-permute-done.7.refs_8_ = bf16[8,16,1024]{2,1,0:T(8,128)(2,1)S(1)} collective-permute-done((bf16[8,16,1024]{2,1,0:T(8,128)(2,1)}, bf16[8,16,1024]{2,1,0:T(8,128)(2,1)S(1)}, u32[]{:S(2)}, u32[]{:S(2)}) %collective-permute-start.7) | collective-permute-done | bytes 262176 | tf_op jit(solution)/shard_map/ppermute | solution.py:386
  310.1 10.1 %collective-permute-done.8.refs_9_ = bf16[8,16,1024]{2,1,0:T(8,128)(2,1)S(1)} collective-permute-done((bf16[8,16,1024]{2,1,0:T(8,128)(2,1)}, bf16[8,16,1024]{2,1,0:T(8,128)(2,1)S(1)}, u32[]{:S(2)}, u32[]{:S(2)}) %collective-permute-start.8) | collective-permute-done | bytes 262176 | tf_op jit(solution)/shard_map/ppermute | solution.py:386
  321.8 11.6 %collective-permute-done.9.refs_10_ = bf16[8,16,1024]{2,1,0:T(8,128)(2,1)S(1)} collective-permute-done((bf16[8,16,1024]{2,1,0:T(8,128)(2,1)}, bf16[8,16,1024]{2,1,0:T(8,128)(2,1)S(1)}, u32[]{:S(2)}, u32[]{:S(2)}) %collective-permute-start.9) | collective-permute-done | bytes 262176 | tf_op jit(solution)/shard_map/ppermute | solution.py:386
  333.4 10.1 %collective-permute-done.10.refs_11_ = bf16[8,16,1024]{2,1,0:T(8,128)(2,1)S(1)} collective-permute-done((bf16[8,16,1024]{2,1,0:T(8,128)(2,1)}, bf16[8,16,1024]{2,1,0:T(8,128)(2,1)S(1)}, u32[]{:S(2)}, u32[]{:S(2)}) %collective-permute-start.10) | collective-permute-done | bytes 262176 | tf_op jit(solution)/shard_map/ppermute | solution.py:386
  344.3 19.4 %sections.2 = bf16[128,16,1024]{2,1,0:T(8,128)(2,1)} custom-call(bf16[8,16,1024]{2,1,0:T(8,128)(2,1)} %get-tuple-element.28.refs_0_, bf16[8,16,1024]{2,1,0:T(8,128)(2,1)} %copy-done.8, bf16[8,16,1024]{2,1,0:T(8,128)(2,1)} %copy-done.9, bf16[8,16,1024]{2,1,0:T(8,128)(2,1)} %copy-done.10, bf16[8,16,1024]{2,1,0:T(8,128)(2,1)} %copy-done.11, ...), custom_call_target="tpu_custom_call" | custom-call | flops 4831838208 | bytes 10485760 | tf_op jit(solution)/shard_map/sections/pallas_call | solution.py:202
  363.8 25.0 %all-to-all-start = ((bf16[32,4,16,1024]{3,2,1,0:T(8,128)(2,1)}), bf16[32,4,16,1024]{3,2,1,0:T(8,128)(2,1)}, u32[]{:S(2)}, u32[]{:S(2)}) async-start(bf16[32,4,16,1024]{3,2,1,0:T(8,128)(2,1)} %bitcast.6), calls=%async_computation | async-start | bytes 8388608 | tf_op jit(solution)/shard_map/all_to_all | solution.py:390
  388.8 1.8 collective-permute-start.22
  390.9 91.2 %collective-permute-done.22.refs_2_ = bf16[4,256,1024]{2,1,0:T(8,128)(2,1)} collective-permute-done((bf16[4,256,1024]{2,1,0:T(8,128)(2,1)}, bf16[4,256,1024]{2,1,0:T(8,128)(2,1)}, u32[]{:S(2)}, u32[]{:S(2)}) %collective-permute-start.22) | collective-permute-done | bytes 2097184 | tf_op jit(solution)/shard_map/ppermute | solution.py:386
  483.2 13.2 %gate.1 = (f32[4096,512]{1,0:T(8,128)}, f32[4,8,1024]{2,1,0:T(8,128)}) custom-call(bf16[32,4,16,1024]{3,2,1,0:T(8,128)(2,1)} %all-to-all-done.2.refs_0_, bf16[4,256,1024]{2,1,0:T(8,128)(2,1)} %get-tuple-element.47.refs_1_, bf16[4,256,1024]{2,1,0:T(8,128)(2,1)} %collective-permute-done.22.refs_2_, f32[1024,256]{1,0:T(8,128)} %broadcast_in_dim.14.refs_3_.refs_5_, ...), custom_call_target="tpu_custom_call" | custom-call | flops 1073741824 | bytes 16777216 | tf_op jit(solution)/shard_map/gate/pallas_call | solution.py:338
  496.4 29.9 %collective-permute-done.21.refs_2_ = bf16[4,256,1024]{2,1,0:T(8,128)(2,1)S(1)} collective-permute-done((bf16[4,256,1024]{2,1,0:T(8,128)(2,1)}, bf16[4,256,1024]{2,1,0:T(8,128)(2,1)S(1)}, u32[]{:S(2)}, u32[]{:S(2)}) %collective-permute-start.21) | collective-permute-done | bytes 2097184 | tf_op jit(solution)/shard_map/ppermute | solution.py:386
  527.6 15.3 %final.1 = bf16[4096,1024]{1,0:T(8,128)(2,1)} custom-call(bf16[32,4,16,1024]{3,2,1,0:T(8,128)(2,1)} %all-to-all-done.refs_0_, bf16[4,256,1024]{2,1,0:T(8,128)(2,1)} %get-tuple-element.44.refs_1_, bf16[4,256,1024]{2,1,0:T(8,128)(2,1)} %copy-done, f32[4096,512]{1,0:T(8,128)} %get-tuple-element.49.refs_3_, f32[4,8,1024]{2,1,0:T(8,128)} %get-tuple-element.50.refs_4_, ...), custom_call_target="tpu_custom_call" | custom-call | flops 1073741824 | bytes 20971520 | tf_op jit(solution)/shard_map/final/pallas_call | solution.py:362
  (73 shorter events, 12.8 us)
Async XLA Ops:
  9.6 146.9 %all-to-all-start.1 = ((bf16[16,8,16,1024]{3,2,1,0:T(8,128)(2,1)}), bf16[16,8,16,1024]{3,2,1,0:T(8,128)(2,1)}, u32[]{:S(2)}, u32[]{:S(2)}) async-start(bf16[16,8,16,1024]{3,2,1,0:T(8,128)(2,1)} %get-tuple-element.46), calls=%async_computation.1 | async-start | bytes 8388608 | tf_op jit(solution)/shard_map/all_to_all | solution.py:390
  17.4 76.4 %collective-permute-start.17 = (bf16[1,80,1024]{2,1,0:T(8,128)(2,1)S(1)}, bf16[1,80,1024]{2,1,0:T(8,128)(2,1)S(1)}, u32[]{:S(2)}, u32[]{:S(2)}) collective-permute-start(bf16[1,80,1024]{2,1,0:T(8,128)(2,1)S(1)} %maximum_bitcast_fusion), channel_id=1, source_target_pairs={{0,24},{2,26},{4,28},{6,30},{8,16},{10,18},{12,20},{14,22},{16,8},... | collective-permute-start | bytes 491528 | tf_op jit(solution)/shard_map/ppermute | solution.py:386
  21.1 104.1 %collective-permute-start.16 = (bf16[1,80,1024]{2,1,0:T(8,128)(2,1)S(1)}, bf16[1,80,1024]{2,1,0:T(8,128)(2,1)S(1)}, u32[]{:S(2)}, u32[]{:S(2)}) collective-permute-start(bf16[1,80,1024]{2,1,0:T(8,128)(2,1)S(1)} %maximum_bitcast_fusion), channel_id=1, source_target_pairs={{0,16},{2,18},{4,20},{6,22},{8,24},{10,26},{12,28},{14,30},{16,0},... | collective-permute-start | bytes 491528 | tf_op jit(solution)/shard_map/ppermute | solution.py:386
  21.1 104.1 %collective-permute-start.15 = (bf16[1,80,1024]{2,1,0:T(8,128)(2,1)S(1)}, bf16[1,80,1024]{2,1,0:T(8,128)(2,1)S(1)}, u32[]{:S(2)}, u32[]{:S(2)}) collective-permute-start(bf16[1,80,1024]{2,1,0:T(8,128)(2,1)S(1)} %maximum_bitcast_fusion), channel_id=1, source_target_pairs={{0,8},{2,10},{4,12},{6,14},{8,0},{10,2},{12,4},{14,6},{16,24},{18,... | collective-permute-start | bytes 491528 | tf_op jit(solution)/shard_map/ppermute | solution.py:386
  125.3 17.1 %collective-permute-start.20 = (bf16[4,80,1024]{2,1,0:T(8,128)(2,1)S(1)}, bf16[4,80,1024]{2,1,0:T(8,128)(2,1)S(1)}, u32[]{:S(2)}, u32[]{:S(2)}) collective-permute-start(bf16[4,80,1024]{2,1,0:T(8,128)(2,1)S(1)} %pad_maximum_fusion.refs_16_.refs_1_), channel_id=1, source_target_pairs={{0,6},{2,4},{4,2},{6,0},{8,14},{10,12},{12,10},{14,8},{16,22},{18,... | collective-permute-start | bytes 1966088 | tf_op jit(solution)/shard_map/ppermute | solution.py:386
  126.0 30.5 %collective-permute-start.19 = (bf16[4,80,1024]{2,1,0:T(8,128)(2,1)S(1)}, bf16[4,80,1024]{2,1,0:T(8,128)(2,1)S(1)}, u32[]{:S(2)}, u32[]{:S(2)}) collective-permute-start(bf16[4,80,1024]{2,1,0:T(8,128)(2,1)S(1)} %pad_maximum_fusion.refs_16_.refs_1_), channel_id=1, source_target_pairs={{0,4},{2,6},{4,0},{6,2},{8,12},{10,14},{12,8},{14,10},{16,20},{18,... | collective-permute-start | bytes 1966088 | tf_op jit(solution)/shard_map/ppermute | solution.py:386
  126.9 29.5 %collective-permute-start.18 = (bf16[4,80,1024]{2,1,0:T(8,128)(2,1)S(1)}, bf16[4,80,1024]{2,1,0:T(8,128)(2,1)S(1)}, u32[]{:S(2)}, u32[]{:S(2)}) collective-permute-start(bf16[4,80,1024]{2,1,0:T(8,128)(2,1)S(1)} %pad_maximum_fusion.refs_16_.refs_1_), channel_id=1, source_target_pairs={{0,2},{2,0},{4,6},{6,4},{8,10},{10,8},{12,14},{14,12},{16,18},{18,... | collective-permute-start | bytes 1966088 | tf_op jit(solution)/shard_map/ppermute | solution.py:386
  177.2 186.6 %all-to-all-start.2 = ((bf16[32,4,16,1024]{3,2,1,0:T(8,128)(2,1)}), bf16[32,4,16,1024]{3,2,1,0:T(8,128)(2,1)}, u32[]{:S(2)}, u32[]{:S(2)}) async-start(bf16[32,4,16,1024]{3,2,1,0:T(8,128)(2,1)} %bitcast.5), calls=%async_computation.2 | async-start | bytes 8388608 | tf_op jit(solution)/shard_map/all_to_all | solution.py:390
  189.6 3.6 collective-permute-start
  189.7 29.0 %collective-permute-start.1 = (bf16[8,16,1024]{2,1,0:T(8,128)(2,1)}, bf16[8,16,1024]{2,1,0:T(8,128)(2,1)S(1)}, u32[]{:S(2)}, u32[]{:S(2)}) collective-permute-start(bf16[8,16,1024]{2,1,0:T(8,128)(2,1)} %get-tuple-element.30), channel_id=1, source_target_pairs={{0,4},{2,6},{4,0},{6,2},{8,12},{10,14},{12,8},{14,10},{16,20},{18,... | collective-permute-start | bytes 786440 | tf_op jit(solution)/shard_map/ppermute | solution.py:386
  191.4 36.2 %collective-permute-start.2 = (bf16[8,16,1024]{2,1,0:T(8,128)(2,1)}, bf16[8,16,1024]{2,1,0:T(8,128)(2,1)S(1)}, u32[]{:S(2)}, u32[]{:S(2)}) collective-permute-start(bf16[8,16,1024]{2,1,0:T(8,128)(2,1)} %get-tuple-element.31), channel_id=1, source_target_pairs={{0,6},{2,4},{4,2},{6,0},{8,14},{10,12},{12,10},{14,8},{16,22},{18,... | collective-permute-start | bytes 786440 | tf_op jit(solution)/shard_map/ppermute | solution.py:386
  191.5 64.9 %collective-permute-start.3 = (bf16[8,16,1024]{2,1,0:T(8,128)(2,1)}, bf16[8,16,1024]{2,1,0:T(8,128)(2,1)S(1)}, u32[]{:S(2)}, u32[]{:S(2)}) collective-permute-start(bf16[8,16,1024]{2,1,0:T(8,128)(2,1)} %get-tuple-element.32), channel_id=1, source_target_pairs={{0,8},{2,10},{4,12},{6,14},{8,0},{10,2},{12,4},{14,6},{16,24},{18,... | collective-permute-start | bytes 786440 | tf_op jit(solution)/shard_map/ppermute | solution.py:386
  193.2 68.9 %collective-permute-start.4 = (bf16[8,16,1024]{2,1,0:T(8,128)(2,1)}, bf16[8,16,1024]{2,1,0:T(8,128)(2,1)S(1)}, u32[]{:S(2)}, u32[]{:S(2)}) collective-permute-start(bf16[8,16,1024]{2,1,0:T(8,128)(2,1)} %get-tuple-element.33), channel_id=1, source_target_pairs={{0,10},{2,8},{4,14},{6,12},{8,2},{10,0},{12,6},{14,4},{16,26},{18,... | collective-permute-start | bytes 786440 | tf_op jit(solution)/shard_map/ppermute | solution.py:386
  193.3 150.2 %copy-start.8 = (bf16[8,16,1024]{2,1,0:T(8,128)(2,1)}, bf16[8,16,1024]{2,1,0:T(8,128)(2,1)S(1)}, u32[]{:S(2)}) copy-start(bf16[8,16,1024]{2,1,0:T(8,128)(2,1)S(1)} %collective-permute-done.refs_1_) | copy-start | bytes 786436
  193.3 77.2 %collective-permute-start.5 = (bf16[8,16,1024]{2,1,0:T(8,128)(2,1)}, bf16[8,16,1024]{2,1,0:T(8,128)(2,1)S(1)}, u32[]{:S(2)}, u32[]{:S(2)}) collective-permute-start(bf16[8,16,1024]{2,1,0:T(8,128)(2,1)} %get-tuple-element.34), channel_id=1, source_target_pairs={{0,12},{2,14},{4,8},{6,10},{8,4},{10,6},{12,0},{14,2},{16,28},{18,... | collective-permute-start | bytes 786440 | tf_op jit(solution)/shard_map/ppermute | solution.py:386
  218.7 124.8 %copy-start.9 = (bf16[8,16,1024]{2,1,0:T(8,128)(2,1)}, bf16[8,16,1024]{2,1,0:T(8,128)(2,1)S(1)}, u32[]{:S(2)}) copy-start(bf16[8,16,1024]{2,1,0:T(8,128)(2,1)S(1)} %collective-permute-done.1.refs_2_) | copy-start | bytes 786436
  218.7 57.4 %collective-permute-start.6 = (bf16[8,16,1024]{2,1,0:T(8,128)(2,1)}, bf16[8,16,1024]{2,1,0:T(8,128)(2,1)S(1)}, u32[]{:S(2)}, u32[]{:S(2)}) collective-permute-start(bf16[8,16,1024]{2,1,0:T(8,128)(2,1)} %get-tuple-element.35), channel_id=1, source_target_pairs={{0,14},{2,12},{4,10},{6,8},{8,6},{10,4},{12,2},{14,0},{16,30},{18,... | collective-permute-start | bytes 786440 | tf_op jit(solution)/shard_map/ppermute | solution.py:386
  227.5 116.0 %copy-start.10 = (bf16[8,16,1024]{2,1,0:T(8,128)(2,1)}, bf16[8,16,1024]{2,1,0:T(8,128)(2,1)S(1)}, u32[]{:S(2)}) copy-start(bf16[8,16,1024]{2,1,0:T(8,128)(2,1)S(1)} %collective-permute-done.2.refs_3_) | copy-start | bytes 786436
  227.5 82.6 %collective-permute-start.7 = (bf16[8,16,1024]{2,1,0:T(8,128)(2,1)}, bf16[8,16,1024]{2,1,0:T(8,128)(2,1)S(1)}, u32[]{:S(2)}, u32[]{:S(2)}) collective-permute-start(bf16[8,16,1024]{2,1,0:T(8,128)(2,1)} %get-tuple-element.36), channel_id=1, source_target_pairs={{0,16},{2,18},{4,20},{6,22},{8,24},{10,26},{12,28},{14,30},{16,0},... | collective-permute-start | bytes 786440 | tf_op jit(solution)/shard_map/ppermute | solution.py:386
  256.4 87.1 %copy-start.11 = (bf16[8,16,1024]{2,1,0:T(8,128)(2,1)}, bf16[8,16,1024]{2,1,0:T(8,128)(2,1)S(1)}, u32[]{:S(2)}) copy-start(bf16[8,16,1024]{2,1,0:T(8,128)(2,1)S(1)} %collective-permute-done.3.refs_4_) | copy-start | bytes 786436
  256.4 63.8 %collective-permute-start.8 = (bf16[8,16,1024]{2,1,0:T(8,128)(2,1)}, bf16[8,16,1024]{2,1,0:T(8,128)(2,1)S(1)}, u32[]{:S(2)}, u32[]{:S(2)}) collective-permute-start(bf16[8,16,1024]{2,1,0:T(8,128)(2,1)} %get-tuple-element.37), channel_id=1, source_target_pairs={{0,18},{2,16},{4,22},{6,20},{8,26},{10,24},{12,30},{14,28},{16,2},... | collective-permute-start | bytes 786440 | tf_op jit(solution)/shard_map/ppermute | solution.py:386
  262.1 81.5 %copy-start.12 = (bf16[8,16,1024]{2,1,0:T(8,128)(2,1)}, bf16[8,16,1024]{2,1,0:T(8,128)(2,1)S(1)}, u32[]{:S(2)}) copy-start(bf16[8,16,1024]{2,1,0:T(8,128)(2,1)S(1)} %collective-permute-done.4.refs_5_) | copy-start | bytes 786436
  262.1 71.3 %collective-permute-start.9 = (bf16[8,16,1024]{2,1,0:T(8,128)(2,1)}, bf16[8,16,1024]{2,1,0:T(8,128)(2,1)S(1)}, u32[]{:S(2)}, u32[]{:S(2)}) collective-permute-start(bf16[8,16,1024]{2,1,0:T(8,128)(2,1)} %get-tuple-element.38), channel_id=1, source_target_pairs={{0,20},{2,22},{4,16},{6,18},{8,28},{10,30},{12,24},{14,26},{16,4},... | collective-permute-start | bytes 786440 | tf_op jit(solution)/shard_map/ppermute | solution.py:386
  270.4 73.0 %collective-permute-start.10 = (bf16[8,16,1024]{2,1,0:T(8,128)(2,1)}, bf16[8,16,1024]{2,1,0:T(8,128)(2,1)S(1)}, u32[]{:S(2)}, u32[]{:S(2)}) collective-permute-start(bf16[8,16,1024]{2,1,0:T(8,128)(2,1)} %get-tuple-element.39), channel_id=1, source_target_pairs={{0,22},{2,20},{4,18},{6,16},{8,30},{10,28},{12,26},{14,24},{16,6},... | collective-permute-start | bytes 786440 | tf_op jit(solution)/shard_map/ppermute | solution.py:386
  276.1 67.4 %collective-permute-start.11 = (bf16[8,16,1024]{2,1,0:T(8,128)(2,1)}, bf16[8,16,1024]{2,1,0:T(8,128)(2,1)S(1)}, u32[]{:S(2)}, u32[]{:S(2)}) collective-permute-start(bf16[8,16,1024]{2,1,0:T(8,128)(2,1)} %get-tuple-element.40), channel_id=1, source_target_pairs={{0,24},{2,26},{4,28},{6,30},{8,16},{10,18},{12,20},{14,22},{16,8},... | collective-permute-start | bytes 786440 | tf_op jit(solution)/shard_map/ppermute | solution.py:386
  310.1 33.4 %collective-permute-start.12 = (bf16[8,16,1024]{2,1,0:T(8,128)(2,1)}, bf16[8,16,1024]{2,1,0:T(8,128)(2,1)S(1)}, u32[]{:S(2)}, u32[]{:S(2)}) collective-permute-start(bf16[8,16,1024]{2,1,0:T(8,128)(2,1)} %get-tuple-element.41), channel_id=1, source_target_pairs={{0,26},{2,24},{4,30},{6,28},{8,18},{10,16},{12,22},{14,20},{16,10}... | collective-permute-start | bytes 786440 | tf_op jit(solution)/shard_map/ppermute | solution.py:386
  320.2 23.3 %collective-permute-start.13 = (bf16[8,16,1024]{2,1,0:T(8,128)(2,1)}, bf16[8,16,1024]{2,1,0:T(8,128)(2,1)}, u32[]{:S(2)}, u32[]{:S(2)}) collective-permute-start(bf16[8,16,1024]{2,1,0:T(8,128)(2,1)} %get-tuple-element.42), channel_id=1, source_target_pairs={{0,28},{2,30},{4,24},{6,26},{8,20},{10,22},{12,16},{14,18},{16,12}... | collective-permute-start | bytes 786440 | tf_op jit(solution)/shard_map/ppermute | solution.py:386
  333.4 10.1 %collective-permute-start.14 = (bf16[8,16,1024]{2,1,0:T(8,128)(2,1)}, bf16[8,16,1024]{2,1,0:T(8,128)(2,1)}, u32[]{:S(2)}, u32[]{:S(2)}) collective-permute-start(bf16[8,16,1024]{2,1,0:T(8,128)(2,1)} %get-tuple-element.43), channel_id=1, source_target_pairs={{0,30},{2,28},{4,26},{6,24},{8,22},{10,20},{12,18},{14,16},{16,14}... | collective-permute-start | bytes 786440 | tf_op jit(solution)/shard_map/ppermute | solution.py:386
  363.8 118.3 %copy-start.4 = (f32[1024]{0:T(1024)S(1)}, f32[1024]{0:T(1024)}, u32[]{:S(2)}) copy-start(f32[1024]{0:T(1024)} %param.10) | copy-start | bytes 12292
  363.8 162.5 %all-to-all-start = ((bf16[32,4,16,1024]{3,2,1,0:T(8,128)(2,1)}), bf16[32,4,16,1024]{3,2,1,0:T(8,128)(2,1)}, u32[]{:S(2)}, u32[]{:S(2)}) async-start(bf16[32,4,16,1024]{3,2,1,0:T(8,128)(2,1)} %bitcast.6), calls=%async_computation | async-start | bytes 8388608 | tf_op jit(solution)/shard_map/all_to_all | solution.py:390
  388.8 93.3 %collective-permute-start.22 = (bf16[4,256,1024]{2,1,0:T(8,128)(2,1)}, bf16[4,256,1024]{2,1,0:T(8,128)(2,1)}, u32[]{:S(2)}, u32[]{:S(2)}) collective-permute-start(bf16[4,256,1024]{2,1,0:T(8,128)(2,1)} %get-tuple-element.48), channel_id=1, source_target_pairs={{0,1},{1,0},{2,3},{3,2},{4,5},{5,4},{6,7},{7,6},{8,9},{9,8},{10,11... | collective-permute-start | bytes 6291464 | tf_op jit(solution)/shard_map/ppermute | solution.py:386
  390.5 135.8 %collective-permute-start.21 = (bf16[4,256,1024]{2,1,0:T(8,128)(2,1)}, bf16[4,256,1024]{2,1,0:T(8,128)(2,1)S(1)}, u32[]{:S(2)}, u32[]{:S(2)}) collective-permute-start(bf16[4,256,1024]{2,1,0:T(8,128)(2,1)} %get-tuple-element.45), channel_id=1, source_target_pairs={{0,1},{1,0},{2,3},{3,2},{4,5},{5,4},{6,7},{7,6},{8,9},{9,8},{10,11... | collective-permute-start | bytes 6291464 | tf_op jit(solution)/shard_map/ppermute | solution.py:386
  (15 other events, 274.0 us)

commit v2 on v1

--- a/solution.py
+++ b/solution.py
@@ -58,67 +58,69 @@
         )
 
 
-def prep_kernel(plan, split, x_ref, *rest):
-    c, s = plan.ch, plan.seq
+def prep_kernel(plan, chunk, split, x_ref, *rest):
+    s = plan.seq
     count = s if split else 1
-    outs, shares, (turned, share_sem, piece_sem) = rest[:count], rest[count : count + c], rest[-3:]
+    outs, shares = rest[:count], rest[count:-5]
+    given, turned, in_sem, out_sem, share_sem = rest[-5:]
     me, y = lax.axis_index("seq"), lax.axis_index("ch")
-    a = pl.program_id(0)
-    value = x_ref[...].T
-    turned[a] = value
-    if not split:
-        outs[0][...] = value.reshape(s, 1, plan.own, plan.width)
-
-    def rows_of(m):
-        who = jnp.bitwise_xor(me, m)
-        return pl.ds(pl.multiple_of(who * plan.own, plan.own), plan.own)
-
+    loads = [
+        pltpu.make_async_copy(
+            x_ref.at[pl.ds(a * plan.width, plan.width), pl.ds(chunk * plan.chunk, plan.chunk)],
+            given.at[a],
+            in_sem.at[a],
+        )
+        for a in range(plan.rows)
+    ]
+    for load in loads:
+        load.start()
+    stores = []
+    for a in range(plan.rows):
+        loads[a].wait()
+        turned[a] = given[a].T.reshape(s, plan.own, plan.width)
+        if split:
+            for m in range(s):
+                pltpu.make_async_copy(
+                    turned.at[a, jnp.bitwise_xor(me, m)], outs[m].at[a], out_sem.at[m]
+                ).start()
+        else:
+            stores.append(
+                pltpu.make_async_copy(turned.at[a], outs[0].at[:, a], out_sem.at[a])
+            )
+            stores[-1].start()
+    for m in range(len(shares)):
+        at = pl.ds(jnp.bitwise_xor(y, m) * plan.out_rows, plan.out_rows)
+        stores.append(pltpu.make_async_copy(turned.at[at], shares[m], share_sem.at[m]))
+        stores[-1].start()
     if split:
         for m in range(s):
             pltpu.make_async_copy(
-                turned.at[a, rows_of(m), :], outs[m].at[a], piece_sem.at[m]
-            ).start()
-
-    @pl.when(a == plan.rows - 1)
-    def _():
-        copies = [
-            pltpu.make_async_copy(
-                turned.at[pl.ds(jnp.bitwise_xor(y, m) * plan.out_rows, plan.out_rows)],
-                shares[m],
-                share_sem.at[m],
-            )
-            for m in range(c)
-        ]
-        for copy in copies:
-            copy.start()
-        if split:
-            for m in range(s):
-                pltpu.make_async_copy(
-                    turned.at[:, rows_of(m), :], outs[m], piece_sem.at[m]
-                ).wait()
-        for copy in copies:
-            copy.wait()
+                turned.at[:, jnp.bitwise_xor(me, m)], outs[m], out_sem.at[m]
+            ).wait()
+    for store in stores:
+        store.wait()
 
 
 def prep(plan, tokens, chunk, split):
-    share = jax.ShapeDtypeStruct((plan.out_rows, plan.chunk, plan.width), jnp.bfloat16)
+    bf16 = jnp.bfloat16
     if split:
-        shape = (plan.rows, plan.own, plan.width)
-        count, spec = plan.seq, ANY
+        shapes = [jax.ShapeDtypeStruct((plan.rows, plan.own, plan.width), bf16)] * plan.seq
+        shape = (plan.out_rows, plan.seq, plan.own, plan.width)
+        shapes += [jax.ShapeDtypeStruct(shape, bf16)] * plan.ch
     else:
         shape = (plan.seq, plan.rows, plan.own, plan.width)
-        count = 1
-        spec = pl.BlockSpec((plan.seq, 1, plan.own, plan.width), lambda a: (0, a, 0, 0))
+        shapes = [jax.ShapeDtypeStruct(shape, bf16)]
     out = pl.pallas_call(
-        functools.partial(prep_kernel, plan, split),
-        out_shape=[jax.ShapeDtypeStruct(shape, jnp.bfloat16)] * count + [share] * plan.ch,
-        grid=(plan.rows,),
-        in_specs=[pl.BlockSpec((plan.width, plan.chunk), lambda a: (a, chunk))],
-        out_specs=[spec] * count + [ANY] * plan.ch,
+        functools.partial(prep_kernel, plan, chunk, split),
+        out_shape=shapes,
+        in_specs=[ANY],
+        out_specs=[ANY] * len(shapes),
         scratch_shapes=[
-            pltpu.VMEM((plan.rows, plan.chunk, plan.width), jnp.bfloat16),
+            pltpu.VMEM((plan.rows, plan.width, plan.chunk), bf16),
+            pltpu.VMEM((plan.rows, plan.seq, plan.own, plan.width), bf16),
+            pltpu.SemaphoreType.DMA((plan.rows,)),
+            pltpu.SemaphoreType.DMA((max(plan.seq, plan.rows),)),
             pltpu.SemaphoreType.DMA((plan.ch,)),
-            pltpu.SemaphoreType.DMA((plan.seq,)),
         ],
         cost_estimate=pl.CostEstimate(
             flops=0,
@@ -127,7 +129,16 @@
         ),
         name="prep",
     )(tokens)
-    return out[:count], out[count:]
+    if split:
+        shape = (plan.out_rows, plan.chunk, plan.width)
+        return out[: plan.seq], [share.reshape(shape) for share in out[plan.seq :]]
+    return out[0], [own_rows(plan, out[0], n) for n in range(plan.ch)]
+
+
+def own_rows(plan, block, mask):
+    start = jnp.bitwise_xor(lax.axis_index("ch"), mask) * plan.out_rows
+    part = lax.dynamic_slice_in_dim(block, start, plan.out_rows, axis=1)
+    return part.transpose(1, 0, 2, 3).reshape(plan.out_rows, plan.chunk, plan.width)
 
 
 def sections_kernel(plan, count, *refs):
@@ -224,37 +235,34 @@
     )(*pieces, *gathered, left)
 
 
-def load_chunk(plan, piece, shares, mixed, inputs, sem_m, sem_i):
-    s, c, own = plan.seq, plan.ch, plan.own
+def load_piece(plan, piece, mixed, sem):
+    for r in range(plan.out_rows):
+        for m in range(plan.seq * plan.ch):
+            row = (m % plan.ch) * plan.chunk + (m // plan.ch) * plan.own
+            pltpu.make_async_copy(
+                piece.at[m, r], mixed.at[r, pl.ds(row, plan.own)], sem.at[r]
+            ).start()
+
+
+def load_shares(plan, shares, inputs, sem):
     y = lax.axis_index("ch")
     for r in range(plan.out_rows):
-        for n in range(c):
+        for n in range(plan.ch):
             at = pl.ds(jnp.bitwise_xor(y, n) * plan.chunk, plan.chunk)
-            pltpu.make_async_copy(shares[n].at[r], inputs.at[r, at], sem_i.at[r]).start()
-        for m in range(s * c):
-            row = (m % c) * plan.chunk + (m // c) * own
-            pltpu.make_async_copy(
-                piece.at[m, r], mixed.at[r, pl.ds(row, own)], sem_m.at[r]
-            ).start()
-
-
-def gate_tile(plan, mixed, inputs, i, ks):
-    total = jnp.zeros((1, LANES), jnp.float32)
-    for j in range(plan.chunk * plan.ch // plan.mix):
-        rs = pl.ds(j * plan.mix, plan.mix)
-        value = mixed[i, rs, ks].astype(jnp.float32)
-        gate = inputs[i, rs, ks].astype(jnp.float32)
-        gated = (value * (gate / (1.0 + jnp.exp(-gate)))).astype(jnp.bfloat16)
-        mixed[i, rs, ks] = gated
-        gated = gated.astype(jnp.float32)
-        total = total + jnp.sum(gated * gated, axis=0, keepdims=True)
-    return total
-
-
-def columns(plan, chunk, j):
-    return (j * plan.mix // plan.chunk) * plan.local + chunk * plan.chunk + (
-        j * plan.mix % plan.chunk
-    )
+            pltpu.make_async_copy(shares[n].at[r], inputs.at[r, at], sem.at[r]).start()
+
+
+def wait_row(buffer, sem, r):
+    pltpu.make_async_copy(buffer.at[r], buffer.at[r], sem.at[r]).wait()
+
+
+def column(plan, chunk, j):
+    row = j * plan.mix
+    return (row // plan.chunk) * plan.local + chunk * plan.chunk + row % plan.chunk
+
+
+def silu(value):
+    return value / (1.0 + jnp.exp(-value))
 
 
 def turn_dot(value, weight):
@@ -265,120 +273,139 @@
 
 def gate_kernel(plan, *refs):
     c = plan.ch
-    piece, shares = refs[0], refs[1 : 1 + c]
-    gain, weight, out, totals, mixed, inputs, sem_m, sem_i = refs[1 + c :]
+    piece, shares, later = refs[0], refs[1 : 1 + c], refs[1 + c : 1 + 2 * c]
+    gain, weight, out, gates, totals = refs[1 + 2 * c : 6 + 2 * c]
+    mixed, inputs, after, sem_m, sem_i, sem_a = refs[6 + 2 * c :]
     i = pl.program_id(0)
 
     @pl.when(i == 0)
     def _():
-        load_chunk(plan, piece, shares, mixed, inputs, sem_m, sem_i)
-
-    pltpu.make_async_copy(inputs.at[i], inputs.at[i], sem_i.at[i]).wait()
-    pltpu.make_async_copy(mixed.at[i], mixed.at[i], sem_m.at[i]).wait()
+        load_shares(plan, later, after, sem_a)
+        load_shares(plan, shares, inputs, sem_i)
+        load_piece(plan, piece, mixed, sem_m)
+
+    wait_row(after, sem_a, i)
+    wait_row(inputs, sem_i, i)
+    wait_row(mixed, sem_m, i)
 
     def tile(kt, carry):
         ks = pl.ds(pl.multiple_of(kt * LANES, LANES), LANES)
-        total = gate_tile(plan, mixed, inputs, i, ks)
+        total = jnp.zeros((1, LANES), jnp.float32)
+        for j in range(plan.chunk * c // plan.mix):
+            rs = pl.ds(j * plan.mix, plan.mix)
+            gates[0, rs, ks] = silu(after[i, rs, ks].astype(jnp.float32)).astype(jnp.bfloat16)
+            value = mixed[i, rs, ks].astype(jnp.float32)
+            value = value * silu(inputs[i, rs, ks].astype(jnp.float32))
+            value = value.astype(jnp.bfloat16).astype(jnp.float32)
+            total = total + jnp.sum(value * value, axis=0, keepdims=True)
+            col = column(plan, 0, j)
+            value = (value * gain[pl.ds(col, plan.mix), :]).astype(jnp.bfloat16)
+            out[ks, rs] = turn_dot(value, weight[col // plan.mix]).astype(jnp.bfloat16)
         totals[0, :, ks] = jnp.broadcast_to(total, (8, LANES))
-        for j in range(plan.chunk * c // plan.mix):
-            col = columns(plan, 0, j)
-            value = mixed[i, pl.ds(j * plan.mix, plan.mix), ks].astype(jnp.float32)
-            value = (value * gain[pl.ds(col, plan.mix), :]).astype(jnp.bfloat16)
-            out[ks, pl.ds(j * plan.mix, plan.mix)] = turn_dot(value, weight[col // plan.mix])
         return carry
 
     lax.fori_loop(0, plan.width // LANES, tile, 0)
 
 
 def final_kernel(plan, *refs):
-    c = plan.ch
-    piece, shares = refs[0], refs[1 : 1 + c]
-    held, before, gain, weight, out, mixed, inputs, sem_m, sem_i = refs[1 + c :]
-    i = pl.program_id(0)
-
-    @pl.when(i == 0)
-    def _():
-        load_chunk(plan, piece, shares, mixed, inputs, sem_m, sem_i)
-
-    pltpu.make_async_copy(inputs.at[i], inputs.at[i], sem_i.at[i]).wait()
-    pltpu.make_async_copy(mixed.at[i], mixed.at[i], sem_m.at[i]).wait()
-
-    def tile(kt, carry):
-        ks = pl.ds(pl.multiple_of(kt * LANES, LANES), LANES)
-        total = gate_tile(plan, mixed, inputs, i, ks) + before[0, pl.ds(0, 1), ks]
-        inverse = lax.rsqrt(total * (1.0 / plan.channels) + 1e-05)
-        for j in range(plan.chunk * c // plan.mix):
-            col = columns(plan, 1, j)
-            value = mixed[i, pl.ds(j * plan.mix, plan.mix), ks].astype(jnp.float32)
-            value = (value * inverse * gain[pl.ds(col, plan.mix), :]).astype(jnp.bfloat16)
-            result = turn_dot(value, weight[col // plan.mix])
-            out[ks, pl.ds(col, plan.mix)] = result.astype(jnp.bfloat16)
-        scale = jnp.broadcast_to(inverse, (128, LANES)).T
-        for j in range(plan.chunk * c // 128):
-            result = held[ks, pl.ds(j * 128, 128)] * scale
-            col = (j * 128 // plan.chunk) * plan.local + j * 128 % plan.chunk
-            out[ks, pl.ds(col, 128)] = result.astype(jnp.bfloat16)
-        return carry
-
-    lax.fori_loop(0, plan.width // LANES, tile, 0)
-
-
-def tail_scratch(plan):
-    shape = (plan.out_rows, plan.chunk * plan.ch, plan.width)
-    return [
-        pltpu.VMEM(shape, jnp.bfloat16),
-        pltpu.VMEM(shape, jnp.bfloat16),
-        pltpu.SemaphoreType.DMA((plan.out_rows,)),
-        pltpu.SemaphoreType.DMA((plan.out_rows,)),
-    ]
-
-
-def gate(plan, piece, shares, gain, weight):
+    piece, gates, held, before, gain, weight, result = refs[:7]
+    mixed, inputs, left, out, sem_m, sem_i, sem_h, sem_o = refs[7:]
+    c, width = plan.ch, plan.width
+    for r in range(plan.out_rows):
+        pltpu.make_async_copy(gates.at[r], inputs.at[r], sem_i.at[r]).start()
+        at = pl.ds(r * width, width)
+        pltpu.make_async_copy(held.at[at], left.at[r], sem_h.at[r]).start()
+    load_piece(plan, piece, mixed, sem_m)
+    stores = []
+    for r in range(plan.out_rows):
+        wait_row(mixed, sem_m, r)
+        wait_row(inputs, sem_i, r)
+        wait_row(left, sem_h, r)
+
+        def tile(kt, carry):
+            ks = pl.ds(pl.multiple_of(kt * LANES, LANES), LANES)
+            total = before[r, pl.ds(0, 1), ks]
+            parts = []
+            for j in range(plan.chunk * c // plan.mix):
+                rs = pl.ds(j * plan.mix, plan.mix)
+                value = mixed[r, rs, ks].astype(jnp.float32)
+                value = value * inputs[r, rs, ks].astype(jnp.float32)
+                total = total + jnp.sum(value * value, axis=0, keepdims=True)
+                col = column(plan, 1, j)
+                value = (value * gain[pl.ds(col, plan.mix), :]).astype(jnp.bfloat16)
+                parts.append((col, turn_dot(value, weight[col // plan.mix])))
+            inverse = lax.rsqrt(total * (1.0 / plan.channels) + 1e-05)
+            scale = jnp.broadcast_to(inverse, (128, LANES)).T
+            for col, part in parts:
+                for q in range(plan.mix // 128):
+                    value = part[:, q * 128 : (q + 1) * 128] * scale
+                    out[r, ks, pl.ds(col + q * 128, 128)] = value.astype(jnp.bfloat16)
+            for j in range(plan.chunk * c // 128):
+                value = left[r, ks, pl.ds(j * 128, 128)].astype(jnp.float32) * scale
+                col = (j * 128 // plan.chunk) * plan.local + j * 128 % plan.chunk
+                out[r, ks, pl.ds(col, 128)] = value.astype(jnp.bfloat16)
+            return carry
+
+        lax.fori_loop(0, width // LANES, tile, 0)
+        stores.append(
+            pltpu.make_async_copy(out.at[r], result.at[pl.ds(r * width, width)], sem_o.at[r])
+        )
+        stores[-1].start()
+    for store in stores:
+        store.wait()
+
+
+def gate(plan, piece, shares, later, gain, weight):
     size, part = plan.out_rows * plan.width, plan.chunk * plan.ch
+    shape, bf16 = (plan.out_rows, part, plan.width), jnp.bfloat16
+    sem = pltpu.SemaphoreType.DMA((plan.out_rows,))
     return pl.pallas_call(
         functools.partial(gate_kernel, plan),
         out_shape=[
-            jax.ShapeDtypeStruct((size, part), jnp.float32),
+            jax.ShapeDtypeStruct((size, part), bf16),
+            jax.ShapeDtypeStruct(shape, bf16),
             jax.ShapeDtypeStruct((plan.out_rows, 8, plan.width), jnp.float32),
         ],
         grid=(plan.out_rows,),
-        in_specs=[ANY] * (1 + plan.ch) + [VMEM, VMEM],
+        in_specs=[ANY] * (1 + 2 * plan.ch) + [VMEM, VMEM],
         out_specs=[
             pl.BlockSpec((plan.width, part), lambda i: (i, 0)),
+            pl.BlockSpec((1, part, plan.width), lambda i: (i, 0, 0)),
             pl.BlockSpec((1, 8, plan.width), lambda i: (i, 0, 0)),
         ],
-        scratch_shapes=tail_scratch(plan),
-        cost_estimate=pl.CostEstimate(
-            flops=2 * size * part * plan.mix,
-            bytes_accessed=8 * size * part,
-            transcendentals=size * part,
-        ),
-        name="gate",
-    )(piece, *shares, gain, weight)
-
-
-def final(plan, piece, shares, held, before, gain, weight):
-    size, part = plan.out_rows * plan.width, plan.chunk * plan.ch
-    return pl.pallas_call(
-        functools.partial(final_kernel, plan),
-        out_shape=jax.ShapeDtypeStruct((size, plan.channels), jnp.bfloat16),
-        grid=(plan.out_rows,),
-        in_specs=[ANY] * (1 + plan.ch)
-        + [
-            pl.BlockSpec((plan.width, part), lambda i: (i, 0)),
-            pl.BlockSpec((1, 8, plan.width), lambda i: (i, 0, 0)),
-            VMEM,
-            VMEM,
-        ],
-        out_specs=pl.BlockSpec((plan.width, plan.channels), lambda i: (i, 0)),
-        scratch_shapes=tail_scratch(plan),
+        scratch_shapes=[pltpu.VMEM(shape, bf16)] * 3 + [sem] * 3,
         cost_estimate=pl.CostEstimate(
             flops=2 * size * part * plan.mix,
             bytes_accessed=10 * size * part,
-            transcendentals=size * part,
+            transcendentals=2 * size * part,
+        ),
+        name="gate",
+    )(piece, *shares, *later, gain, weight)
+
+
+def final(plan, piece, gates, held, before, gain, weight):
+    size, part = plan.out_rows * plan.width, plan.chunk * plan.ch
+    shape, bf16 = (plan.out_rows, part, plan.width), jnp.bfloat16
+    sem = pltpu.SemaphoreType.DMA((plan.out_rows,))
+    return pl.pallas_call(
+        functools.partial(final_kernel, plan),
+        out_shape=jax.ShapeDtypeStruct((size, plan.channels), bf16),
+        in_specs=[ANY] * 3 + [VMEM] * 3,
+        out_specs=ANY,
+        scratch_shapes=[
+            pltpu.VMEM(shape, bf16),
+            pltpu.VMEM(shape, bf16),
+            pltpu.VMEM((plan.out_rows, plan.width, part), bf16),
+            pltpu.VMEM((plan.out_rows, plan.width, plan.channels), bf16),
+        ]
+        + [sem] * 4,
+        cost_estimate=pl.CostEstimate(
+            flops=2 * size * part * plan.mix,
+            bytes_accessed=10 * size * part,
+            transcendentals=0,
         ),
         name="final",
-    )(piece, *shares, held, before, gain, weight)
+    )(piece, gates, held, before, gain, weight)
 
 
 def swap(value, mask, axis):
@@ -407,7 +434,7 @@
     for k in range(CHUNKS):
         pieces, share = prep(plan, tokens, k, k == 1)
         if k == 0:
-            block = exchange(pieces[0], "seq")
+            block = exchange(pieces, "seq")
             arrived.append([block.reshape(plan.all_rows, own, plan.width)])
         else:
             arrived.append([pieces[0]] + [None] * (s - 1))
@@ -421,8 +448,8 @@
         out = sections(plan, arrived[k], gathered, left_block)
         out = out.reshape(s * c, plan.out_rows, own, plan.width)
         landed.append(exchange(out, ("seq", "ch")))
-    held, before = gate(plan, landed[0], shares[0], gain, mix_weight)
-    return final(plan, landed[1], shares[1], held, before, gain, mix_weight)
+    held, gates, before = gate(plan, landed[0], *shares, gain, mix_weight)
+    return final(plan, landed[1], gates, held, before, gain, mix_weight)
 
 
 def plain_body(tokens, right_block, twiddle, left_block, gain, mix_weight):

time: 544 us -> 550 us (1.011)
  waiting for transfers between devices: 388 us -> 400 us
  Pallas kernels: 85.9 us -> 75.5 us
    ppermute x23, waiting for transfers between devices: 388 us -> 400 us  [swap(): return lax.ppermute(value, axis, [(i, i ^ mask) for i in range(count)])]
    pallas_call x2, Pallas kernels: 18.4 us -> 8.74 us  [prep(): pl.pallas_call(functools.partial(prep_kernel, plan, chunk, split), out_sh...]
  transfers between devices with their start and end apart: 26 -> 26, of which waited for: 16 -> 16; matrix products, arithmetic and copies ran while one was open for 0% -> 1% of each run, Pallas kernels for 8% -> 7%
where the time goes in v2:
time: 550 us; the launch traced here: 549 us
  waiting for transfers between devices  400 us (73%)
  Pallas kernels  75.5 us (14%)
  starting transfers between devices  65.3 us (12%)
  local copies, waits for them, and re-layouts  7.52 us (1%)
    ppermute x23, waiting for transfers between devices, swap(): return lax.ppermute(value, axis, [(i, i ^ mask) for i in range(count)])  400 us
    pallas_call x2, Pallas kernels, sections(): pl.pallas_call(functools.partial(sections_kernel, plan, len(pieces)), out...  39 us
    all_to_all x3, starting transfers between devices, exchange(): return lax.all_to_all(value, axes, split_axis=0, concat_axis=0, tiled=True)  36.2 us
    ppermute x23, starting transfers between devices, swap(): return lax.ppermute(value, axis, [(i, i ^ mask) for i in range(count)])  29.1 us
    pallas_call x1, Pallas kernels, gate(): pl.pallas_call(functools.partial(gate_kernel, plan), out_shape=[jax.Shape...  15.5 us
    pallas_call x1, Pallas kernels, final(): pl.pallas_call(functools.partial(final_kernel, plan), out_shape=jax.Shape...  12.2 us
  transfers between devices with their start and end apart: 26, of which 16 were waited for; matrix products, arithmetic and copies ran while one was open for 1% of the time, Pallas kernels for 7%

profile of v2, /device:TPU:0, one launch (start us, length us, event | category | flops | bytes accessed | tf_op | source)
XLA Modules:
  0.0 549.3 jit_solution(1994854370024169015)
XLA Ops:
  0.0 3.6 prep.3
  3.7 7.6 %all-to-all-start.1 = ((bf16[16,8,16,1024]{3,2,1,0:T(8,128)(2,1)}), bf16[16,8,16,1024]{3,2,1,0:T(8,128)(2,1)}, u32[]{:S(2)}, u32[]{:S(2)}) async-start(bf16[16,8,16,1024]{3,2,1,0:T(8,128)(2,1)} %prep.3), calls=%async_computation.1 | async-start | bytes 8388608 | tf_op jit(solution)/shard_map/all_to_all | solution.py:417
  11.4 3.7 collective-permute-start.17
  15.9 72.0 %collective-permute-done.17 = bf16[1,80,1024]{2,1,0:T(8,128)(2,1)S(1)} collective-permute-done((bf16[1,80,1024]{2,1,0:T(8,128)(2,1)S(1)}, bf16[1,80,1024]{2,1,0:T(8,128)(2,1)S(1)}, u32[]{:S(2)}, u32[]{:S(2)}) %collective-permute-start.17) | collective-permute-done | bytes 163872 | tf_op jit(solution)/shard_map/ppermute | solution.py:413
  87.9 31.4 %collective-permute-done.16 = bf16[1,80,1024]{2,1,0:T(8,128)(2,1)S(1)} collective-permute-done((bf16[1,80,1024]{2,1,0:T(8,128)(2,1)S(1)}, bf16[1,80,1024]{2,1,0:T(8,128)(2,1)S(1)}, u32[]{:S(2)}, u32[]{:S(2)}) %collective-permute-start.16) | collective-permute-done | bytes 163872 | tf_op jit(solution)/shard_map/ppermute | solution.py:413
  121.3 15.1 %collective-permute-done.20.refs_19_.refs_4_ = bf16[4,80,1024]{2,1,0:T(8,128)(2,1)S(1)} collective-permute-done((bf16[4,80,1024]{2,1,0:T(8,128)(2,1)S(1)}, bf16[4,80,1024]{2,1,0:T(8,128)(2,1)S(1)}, u32[]{:S(2)}, u32[]{:S(2)}) %collective-permute-start.20) | collective-permute-done | bytes 655392 | tf_op jit(solution)/shard_map/ppermute | solution.py:413
  136.4 14.1 %collective-permute-done.19.refs_18_.refs_3_ = bf16[4,80,1024]{2,1,0:T(8,128)(2,1)S(1)} collective-permute-done((bf16[4,80,1024]{2,1,0:T(8,128)(2,1)S(1)}, bf16[4,80,1024]{2,1,0:T(8,128)(2,1)S(1)}, u32[]{:S(2)}, u32[]{:S(2)}) %collective-permute-start.19) | collective-permute-done | bytes 655392 | tf_op jit(solution)/shard_map/ppermute | solution.py:413
  151.6 19.6 %sections.3 = bf16[128,16,1024]{2,1,0:T(8,128)(2,1)} custom-call(bf16[128,16,1024]{2,1,0:T(8,128)(2,1)} %bitcast.2.refs_0_, bf16[4,80,1024]{2,1,0:T(8,128)(2,1)} %copy-done.1, bf16[4,80,1024]{2,1,0:T(8,128)(2,1)} %copy-done.8, bf16[4,80,1024]{2,1,0:T(8,128)(2,1)} %copy-done.7, bf16[4,80,1024]{2,1,0:T(8,128)(2,1)} %copy-done.6, bf16[128,128]{1,0:T(8,128)(2,1)} %refs_5_.2), custom_call_target="tpu_custom_call" | custom-call | flops 4831838208 | bytes 10485760 | tf_op jit(solution)/shard_map/sections/pallas_call | solution.py:213
  171.2 3.6 all-to-all-start.2
  174.8 5.1 prep.2
  183.6 2.6 collective-permute-start.5
  186.1 26.6 %collective-permute-done.1.refs_2_ = bf16[8,16,1024]{2,1,0:T(8,128)(2,1)S(1)} collective-permute-done((bf16[8,16,1024]{2,1,0:T(8,128)(2,1)}, bf16[8,16,1024]{2,1,0:T(8,128)(2,1)S(1)}, u32[]{:S(2)}, u32[]{:S(2)}) %collective-permute-start.1) | collective-permute-done | bytes 262176 | tf_op jit(solution)/shard_map/ppermute | solution.py:413
  212.7 8.8 %collective-permute-done.2.refs_3_ = bf16[8,16,1024]{2,1,0:T(8,128)(2,1)S(1)} collective-permute-done((bf16[8,16,1024]{2,1,0:T(8,128)(2,1)}, bf16[8,16,1024]{2,1,0:T(8,128)(2,1)S(1)}, u32[]{:S(2)}, u32[]{:S(2)}) %collective-permute-start.2) | collective-permute-done | bytes 262176 | tf_op jit(solution)/shard_map/ppermute | solution.py:413
  221.5 28.9 %collective-permute-done.3.refs_4_ = bf16[8,16,1024]{2,1,0:T(8,128)(2,1)S(1)} collective-permute-done((bf16[8,16,1024]{2,1,0:T(8,128)(2,1)}, bf16[8,16,1024]{2,1,0:T(8,128)(2,1)S(1)}, u32[]{:S(2)}, u32[]{:S(2)}) %collective-permute-start.3) | collective-permute-done | bytes 262176 | tf_op jit(solution)/shard_map/ppermute | solution.py:413
  250.4 2.0 collective-permute-start.8
  252.5 3.6 collective-permute-done.4.refs_5_
  256.1 3.1 collective-permute-start.9
  259.2 5.2 collective-permute-done.5.refs_6_
  266.2 3.9 collective-permute-done.6.refs_7_
  270.0 5.1 collective-permute-start.11
  275.2 28.9 %collective-permute-done.7.refs_8_ = bf16[8,16,1024]{2,1,0:T(8,128)(2,1)S(1)} collective-permute-done((bf16[8,16,1024]{2,1,0:T(8,128)(2,1)}, bf16[8,16,1024]{2,1,0:T(8,128)(2,1)S(1)}, u32[]{:S(2)}, u32[]{:S(2)}) %collective-permute-start.7) | collective-permute-done | bytes 262176 | tf_op jit(solution)/shard_map/ppermute | solution.py:413
  304.1 10.1 %collective-permute-done.8.refs_9_ = bf16[8,16,1024]{2,1,0:T(8,128)(2,1)S(1)} collective-permute-done((bf16[8,16,1024]{2,1,0:T(8,128)(2,1)}, bf16[8,16,1024]{2,1,0:T(8,128)(2,1)S(1)}, u32[]{:S(2)}, u32[]{:S(2)}) %collective-permute-start.8) | collective-permute-done | bytes 262176 | tf_op jit(solution)/shard_map/ppermute | solution.py:413
  315.8 11.6 %collective-permute-done.9.refs_10_ = bf16[8,16,1024]{2,1,0:T(8,128)(2,1)S(1)} collective-permute-done((bf16[8,16,1024]{2,1,0:T(8,128)(2,1)}, bf16[8,16,1024]{2,1,0:T(8,128)(2,1)S(1)}, u32[]{:S(2)}, u32[]{:S(2)}) %collective-permute-start.9) | collective-permute-done | bytes 262176 | tf_op jit(solution)/shard_map/ppermute | solution.py:413
  327.4 10.1 %collective-permute-done.10.refs_11_ = bf16[8,16,1024]{2,1,0:T(8,128)(2,1)S(1)} collective-permute-done((bf16[8,16,1024]{2,1,0:T(8,128)(2,1)}, bf16[8,16,1024]{2,1,0:T(8,128)(2,1)S(1)}, u32[]{:S(2)}, u32[]{:S(2)}) %collective-permute-start.10) | collective-permute-done | bytes 262176 | tf_op jit(solution)/shard_map/ppermute | solution.py:413
  338.3 19.4 %sections.2 = bf16[128,16,1024]{2,1,0:T(8,128)(2,1)} custom-call(bf16[8,16,1024]{2,1,0:T(8,128)(2,1)} %get-tuple-element.26.refs_0_, bf16[8,16,1024]{2,1,0:T(8,128)(2,1)} %copy-done.9, bf16[8,16,1024]{2,1,0:T(8,128)(2,1)} %copy-done.10, bf16[8,16,1024]{2,1,0:T(8,128)(2,1)} %copy-done.11, bf16[8,16,1024]{2,1,0:T(8,128)(2,1)} %copy-done.12, ...), custom_call_target="tpu_custom_call" | custom-call | flops 4831838208 | bytes 10485760 | tf_op jit(solution)/shard_map/sections/pallas_call | solution.py:213
  357.8 25.0 %all-to-all-start = ((bf16[32,4,16,1024]{3,2,1,0:T(8,128)(2,1)}), bf16[32,4,16,1024]{3,2,1,0:T(8,128)(2,1)}, u32[]{:S(2)}, u32[]{:S(2)}) async-start(bf16[32,4,16,1024]{3,2,1,0:T(8,128)(2,1)} %bitcast.15), calls=%async_computation | async-start | bytes 8388608 | tf_op jit(solution)/shard_map/all_to_all | solution.py:417
  382.8 2.7 dynamic-slice_bitcast_fusion
  385.7 1.8 collective-permute-start.21
  390.3 85.6 %collective-permute-done.21.refs_2_ = bf16[4,256,1024]{2,1,0:T(8,128)(2,1)S(1)} collective-permute-done((bf16[4,256,1024]{2,1,0:T(8,128)(2,1)S(1)}, bf16[4,256,1024]{2,1,0:T(8,128)(2,1)S(1)}, u32[]{:S(2)}, u32[]{:S(2)}) %collective-permute-start.21) | collective-permute-done | bytes 2097184 | tf_op jit(solution)/shard_map/ppermute | solution.py:413
  475.9 44.5 %collective-permute-done.22.refs_4_ = bf16[4,256,1024]{2,1,0:T(8,128)(2,1)} collective-permute-done((bf16[4,256,1024]{2,1,0:T(8,128)(2,1)S(1)}, bf16[4,256,1024]{2,1,0:T(8,128)(2,1)}, u32[]{:S(2)}, u32[]{:S(2)}) %collective-permute-start.22) | collective-permute-done | bytes 2097184 | tf_op jit(solution)/shard_map/ppermute | solution.py:413
  521.5 15.5 %gate.1 = (bf16[4096,512]{1,0:T(8,128)(2,1)}, bf16[4,512,1024]{2,1,0:T(8,128)(2,1)}, f32[4,8,1024]{2,1,0:T(8,128)}) custom-call(bf16[32,4,16,1024]{3,2,1,0:T(8,128)(2,1)} %all-to-all-done.2.refs_0_, bf16[4,256,1024]{2,1,0:T(8,128)(2,1)} %bitcast.13, bf16[4,256,1024]{2,1,0:T(8,128)(2,1)} %copy-done, bf16[4,256,1024]{2,1,0:T(8,128)(2,1)} %bitcast.16, ...), custom_call_target="tpu_custom_call" | custom-call | flops 1073741824 | bytes 20971520 | tf_op jit(solution)/shard_map/gate/pallas_call | solution.py:362
  537.1 12.2 %final.1 = bf16[4096,1024]{1,0:T(8,128)(2,1)} custom-call(bf16[32,4,16,1024]{3,2,1,0:T(8,128)(2,1)} %all-to-all-done.refs_0_, bf16[4,512,1024]{2,1,0:T(8,128)(2,1)} %get-tuple-element.44.refs_1_, bf16[4096,512]{1,0:T(8,128)(2,1)} %get-tuple-element.45.refs_2_, f32[4,8,1024]{2,1,0:T(8,128)} %get-tuple-element.46.refs_3_, ...), custom_call_target="tpu_custom_call" | custom-call | flops 1073741824 | bytes 20971520 | tf_op jit(solution)/shard_map/final/pallas_call | solution.py:390
  (78 shorter events, 15.8 us)
Async XLA Ops:
  3.7 146.9 %all-to-all-start.1 = ((bf16[16,8,16,1024]{3,2,1,0:T(8,128)(2,1)}), bf16[16,8,16,1024]{3,2,1,0:T(8,128)(2,1)}, u32[]{:S(2)}, u32[]{:S(2)}) async-start(bf16[16,8,16,1024]{3,2,1,0:T(8,128)(2,1)} %prep.3), calls=%async_computation.1 | async-start | bytes 8388608 | tf_op jit(solution)/shard_map/all_to_all | solution.py:417
  11.4 76.4 %collective-permute-start.17 = (bf16[1,80,1024]{2,1,0:T(8,128)(2,1)S(1)}, bf16[1,80,1024]{2,1,0:T(8,128)(2,1)S(1)}, u32[]{:S(2)}, u32[]{:S(2)}) collective-permute-start(bf16[1,80,1024]{2,1,0:T(8,128)(2,1)S(1)} %maximum_bitcast_fusion), channel_id=1, source_target_pairs={{0,24},{2,26},{4,28},{6,30},{8,16},{10,18},{12,20},{14,22},{16,8},... | collective-permute-start | bytes 491528 | tf_op jit(solution)/shard_map/ppermute | solution.py:413
  15.2 104.1 %collective-permute-start.16 = (bf16[1,80,1024]{2,1,0:T(8,128)(2,1)S(1)}, bf16[1,80,1024]{2,1,0:T(8,128)(2,1)S(1)}, u32[]{:S(2)}, u32[]{:S(2)}) collective-permute-start(bf16[1,80,1024]{2,1,0:T(8,128)(2,1)S(1)} %maximum_bitcast_fusion), channel_id=1, source_target_pairs={{0,16},{2,18},{4,20},{6,22},{8,24},{10,26},{12,28},{14,30},{16,0},... | collective-permute-start | bytes 491528 | tf_op jit(solution)/shard_map/ppermute | solution.py:413
  15.2 104.1 %collective-permute-start.15 = (bf16[1,80,1024]{2,1,0:T(8,128)(2,1)S(1)}, bf16[1,80,1024]{2,1,0:T(8,128)(2,1)S(1)}, u32[]{:S(2)}, u32[]{:S(2)}) collective-permute-start(bf16[1,80,1024]{2,1,0:T(8,128)(2,1)S(1)} %maximum_bitcast_fusion), channel_id=1, source_target_pairs={{0,8},{2,10},{4,12},{6,14},{8,0},{10,2},{12,4},{14,6},{16,24},{18,... | collective-permute-start | bytes 491528 | tf_op jit(solution)/shard_map/ppermute | solution.py:413
  119.4 17.1 %collective-permute-start.20 = (bf16[4,80,1024]{2,1,0:T(8,128)(2,1)S(1)}, bf16[4,80,1024]{2,1,0:T(8,128)(2,1)S(1)}, u32[]{:S(2)}, u32[]{:S(2)}) collective-permute-start(bf16[4,80,1024]{2,1,0:T(8,128)(2,1)S(1)} %pad_maximum_fusion.refs_16_.refs_1_), channel_id=1, source_target_pairs={{0,6},{2,4},{4,2},{6,0},{8,14},{10,12},{12,10},{14,8},{16,22},{18,... | collective-permute-start | bytes 1966088 | tf_op jit(solution)/shard_map/ppermute | solution.py:413
  120.0 30.5 %collective-permute-start.19 = (bf16[4,80,1024]{2,1,0:T(8,128)(2,1)S(1)}, bf16[4,80,1024]{2,1,0:T(8,128)(2,1)S(1)}, u32[]{:S(2)}, u32[]{:S(2)}) collective-permute-start(bf16[4,80,1024]{2,1,0:T(8,128)(2,1)S(1)} %pad_maximum_fusion.refs_16_.refs_1_), channel_id=1, source_target_pairs={{0,4},{2,6},{4,0},{6,2},{8,12},{10,14},{12,8},{14,10},{16,20},{18,... | collective-permute-start | bytes 1966088 | tf_op jit(solution)/shard_map/ppermute | solution.py:413
  121.0 29.5 %collective-permute-start.18 = (bf16[4,80,1024]{2,1,0:T(8,128)(2,1)S(1)}, bf16[4,80,1024]{2,1,0:T(8,128)(2,1)S(1)}, u32[]{:S(2)}, u32[]{:S(2)}) collective-permute-start(bf16[4,80,1024]{2,1,0:T(8,128)(2,1)S(1)} %pad_maximum_fusion.refs_16_.refs_1_), channel_id=1, source_target_pairs={{0,2},{2,0},{4,6},{6,4},{8,10},{10,8},{12,14},{14,12},{16,18},{18,... | collective-permute-start | bytes 1966088 | tf_op jit(solution)/shard_map/ppermute | solution.py:413
  171.2 186.6 %all-to-all-start.2 = ((bf16[32,4,16,1024]{3,2,1,0:T(8,128)(2,1)}), bf16[32,4,16,1024]{3,2,1,0:T(8,128)(2,1)}, u32[]{:S(2)}, u32[]{:S(2)}) async-start(bf16[32,4,16,1024]{3,2,1,0:T(8,128)(2,1)} %bitcast.14), calls=%async_computation.2 | async-start | bytes 8388608 | tf_op jit(solution)/shard_map/all_to_all | solution.py:417
  179.9 3.6 collective-permute-start
  180.0 32.7 %collective-permute-start.1 = (bf16[8,16,1024]{2,1,0:T(8,128)(2,1)}, bf16[8,16,1024]{2,1,0:T(8,128)(2,1)S(1)}, u32[]{:S(2)}, u32[]{:S(2)}) collective-permute-start(bf16[8,16,1024]{2,1,0:T(8,128)(2,1)} %get-tuple-element.28), channel_id=1, source_target_pairs={{0,4},{2,6},{4,0},{6,2},{8,12},{10,14},{12,8},{14,10},{16,20},{18,... | collective-permute-start | bytes 786440 | tf_op jit(solution)/shard_map/ppermute | solution.py:413
  181.7 39.9 %collective-permute-start.2 = (bf16[8,16,1024]{2,1,0:T(8,128)(2,1)}, bf16[8,16,1024]{2,1,0:T(8,128)(2,1)S(1)}, u32[]{:S(2)}, u32[]{:S(2)}) collective-permute-start(bf16[8,16,1024]{2,1,0:T(8,128)(2,1)} %get-tuple-element.29), channel_id=1, source_target_pairs={{0,6},{2,4},{4,2},{6,0},{8,14},{10,12},{12,10},{14,8},{16,22},{18,... | collective-permute-start | bytes 786440 | tf_op jit(solution)/shard_map/ppermute | solution.py:413
  181.8 68.6 %collective-permute-start.3 = (bf16[8,16,1024]{2,1,0:T(8,128)(2,1)}, bf16[8,16,1024]{2,1,0:T(8,128)(2,1)S(1)}, u32[]{:S(2)}, u32[]{:S(2)}) collective-permute-start(bf16[8,16,1024]{2,1,0:T(8,128)(2,1)} %get-tuple-element.30), channel_id=1, source_target_pairs={{0,8},{2,10},{4,12},{6,14},{8,0},{10,2},{12,4},{14,6},{16,24},{18,... | collective-permute-start | bytes 786440 | tf_op jit(solution)/shard_map/ppermute | solution.py:413
  183.5 72.6 %collective-permute-start.4 = (bf16[8,16,1024]{2,1,0:T(8,128)(2,1)}, bf16[8,16,1024]{2,1,0:T(8,128)(2,1)S(1)}, u32[]{:S(2)}, u32[]{:S(2)}) collective-permute-start(bf16[8,16,1024]{2,1,0:T(8,128)(2,1)} %get-tuple-element.31), channel_id=1, source_target_pairs={{0,10},{2,8},{4,14},{6,12},{8,2},{10,0},{12,6},{14,4},{16,26},{18,... | collective-permute-start | bytes 786440 | tf_op jit(solution)/shard_map/ppermute | solution.py:413
  183.6 153.9 %copy-start.9 = (bf16[8,16,1024]{2,1,0:T(8,128)(2,1)}, bf16[8,16,1024]{2,1,0:T(8,128)(2,1)S(1)}, u32[]{:S(2)}) copy-start(bf16[8,16,1024]{2,1,0:T(8,128)(2,1)S(1)} %collective-permute-done.refs_1_) | copy-start | bytes 786436
  183.6 80.9 %collective-permute-start.5 = (bf16[8,16,1024]{2,1,0:T(8,128)(2,1)}, bf16[8,16,1024]{2,1,0:T(8,128)(2,1)S(1)}, u32[]{:S(2)}, u32[]{:S(2)}) collective-permute-start(bf16[8,16,1024]{2,1,0:T(8,128)(2,1)} %get-tuple-element.32), channel_id=1, source_target_pairs={{0,12},{2,14},{4,8},{6,10},{8,4},{10,6},{12,0},{14,2},{16,28},{18,... | collective-permute-start | bytes 786440 | tf_op jit(solution)/shard_map/ppermute | solution.py:413
  212.7 124.8 %copy-start.10 = (bf16[8,16,1024]{2,1,0:T(8,128)(2,1)}, bf16[8,16,1024]{2,1,0:T(8,128)(2,1)S(1)}, u32[]{:S(2)}) copy-start(bf16[8,16,1024]{2,1,0:T(8,128)(2,1)S(1)} %collective-permute-done.1.refs_2_) | copy-start | bytes 786436
  212.7 57.4 %collective-permute-start.6 = (bf16[8,16,1024]{2,1,0:T(8,128)(2,1)}, bf16[8,16,1024]{2,1,0:T(8,128)(2,1)S(1)}, u32[]{:S(2)}, u32[]{:S(2)}) collective-permute-start(bf16[8,16,1024]{2,1,0:T(8,128)(2,1)} %get-tuple-element.33), channel_id=1, source_target_pairs={{0,14},{2,12},{4,10},{6,8},{8,6},{10,4},{12,2},{14,0},{16,30},{18,... | collective-permute-start | bytes 786440 | tf_op jit(solution)/shard_map/ppermute | solution.py:413
  221.5 116.0 %copy-start.11 = (bf16[8,16,1024]{2,1,0:T(8,128)(2,1)}, bf16[8,16,1024]{2,1,0:T(8,128)(2,1)S(1)}, u32[]{:S(2)}) copy-start(bf16[8,16,1024]{2,1,0:T(8,128)(2,1)S(1)} %collective-permute-done.2.refs_3_) | copy-start | bytes 786436
  221.5 82.6 %collective-permute-start.7 = (bf16[8,16,1024]{2,1,0:T(8,128)(2,1)}, bf16[8,16,1024]{2,1,0:T(8,128)(2,1)S(1)}, u32[]{:S(2)}, u32[]{:S(2)}) collective-permute-start(bf16[8,16,1024]{2,1,0:T(8,128)(2,1)} %get-tuple-element.34), channel_id=1, source_target_pairs={{0,16},{2,18},{4,20},{6,22},{8,24},{10,26},{12,28},{14,30},{16,0},... | collective-permute-start | bytes 786440 | tf_op jit(solution)/shard_map/ppermute | solution.py:413
  250.4 87.1 %copy-start.12 = (bf16[8,16,1024]{2,1,0:T(8,128)(2,1)}, bf16[8,16,1024]{2,1,0:T(8,128)(2,1)S(1)}, u32[]{:S(2)}) copy-start(bf16[8,16,1024]{2,1,0:T(8,128)(2,1)S(1)} %collective-permute-done.3.refs_4_) | copy-start | bytes 786436
  250.4 63.8 %collective-permute-start.8 = (bf16[8,16,1024]{2,1,0:T(8,128)(2,1)}, bf16[8,16,1024]{2,1,0:T(8,128)(2,1)S(1)}, u32[]{:S(2)}, u32[]{:S(2)}) collective-permute-start(bf16[8,16,1024]{2,1,0:T(8,128)(2,1)} %get-tuple-element.35), channel_id=1, source_target_pairs={{0,18},{2,16},{4,22},{6,20},{8,26},{10,24},{12,30},{14,28},{16,2},... | collective-permute-start | bytes 786440 | tf_op jit(solution)/shard_map/ppermute | solution.py:413
  256.1 81.5 %copy-start.13 = (bf16[8,16,1024]{2,1,0:T(8,128)(2,1)}, bf16[8,16,1024]{2,1,0:T(8,128)(2,1)S(1)}, u32[]{:S(2)}) copy-start(bf16[8,16,1024]{2,1,0:T(8,128)(2,1)S(1)} %collective-permute-done.4.refs_5_) | copy-start | bytes 786436
  256.1 71.3 %collective-permute-start.9 = (bf16[8,16,1024]{2,1,0:T(8,128)(2,1)}, bf16[8,16,1024]{2,1,0:T(8,128)(2,1)S(1)}, u32[]{:S(2)}, u32[]{:S(2)}) collective-permute-start(bf16[8,16,1024]{2,1,0:T(8,128)(2,1)} %get-tuple-element.36), channel_id=1, source_target_pairs={{0,20},{2,22},{4,16},{6,18},{8,28},{10,30},{12,24},{14,26},{16,4},... | collective-permute-start | bytes 786440 | tf_op jit(solution)/shard_map/ppermute | solution.py:413
  264.4 73.0 %collective-permute-start.10 = (bf16[8,16,1024]{2,1,0:T(8,128)(2,1)}, bf16[8,16,1024]{2,1,0:T(8,128)(2,1)S(1)}, u32[]{:S(2)}, u32[]{:S(2)}) collective-permute-start(bf16[8,16,1024]{2,1,0:T(8,128)(2,1)} %get-tuple-element.37), channel_id=1, source_target_pairs={{0,22},{2,20},{4,18},{6,16},{8,30},{10,28},{12,26},{14,24},{16,6},... | collective-permute-start | bytes 786440 | tf_op jit(solution)/shard_map/ppermute | solution.py:413
  270.0 67.4 %collective-permute-start.11 = (bf16[8,16,1024]{2,1,0:T(8,128)(2,1)}, bf16[8,16,1024]{2,1,0:T(8,128)(2,1)S(1)}, u32[]{:S(2)}, u32[]{:S(2)}) collective-permute-start(bf16[8,16,1024]{2,1,0:T(8,128)(2,1)} %get-tuple-element.38), channel_id=1, source_target_pairs={{0,24},{2,26},{4,28},{6,30},{8,16},{10,18},{12,20},{14,22},{16,8},... | collective-permute-start | bytes 786440 | tf_op jit(solution)/shard_map/ppermute | solution.py:413
  304.1 33.4 %collective-permute-start.12 = (bf16[8,16,1024]{2,1,0:T(8,128)(2,1)}, bf16[8,16,1024]{2,1,0:T(8,128)(2,1)S(1)}, u32[]{:S(2)}, u32[]{:S(2)}) collective-permute-start(bf16[8,16,1024]{2,1,0:T(8,128)(2,1)} %get-tuple-element.39), channel_id=1, source_target_pairs={{0,26},{2,24},{4,30},{6,28},{8,18},{10,16},{12,22},{14,20},{16,10}... | collective-permute-start | bytes 786440 | tf_op jit(solution)/shard_map/ppermute | solution.py:413
  314.2 23.3 %collective-permute-start.13 = (bf16[8,16,1024]{2,1,0:T(8,128)(2,1)}, bf16[8,16,1024]{2,1,0:T(8,128)(2,1)}, u32[]{:S(2)}, u32[]{:S(2)}) collective-permute-start(bf16[8,16,1024]{2,1,0:T(8,128)(2,1)} %get-tuple-element.40), channel_id=1, source_target_pairs={{0,28},{2,30},{4,24},{6,26},{8,20},{10,22},{12,16},{14,18},{16,12}... | collective-permute-start | bytes 786440 | tf_op jit(solution)/shard_map/ppermute | solution.py:413
  327.4 10.1 %collective-permute-start.14 = (bf16[8,16,1024]{2,1,0:T(8,128)(2,1)}, bf16[8,16,1024]{2,1,0:T(8,128)(2,1)}, u32[]{:S(2)}, u32[]{:S(2)}) collective-permute-start(bf16[8,16,1024]{2,1,0:T(8,128)(2,1)} %get-tuple-element.41), channel_id=1, source_target_pairs={{0,30},{2,28},{4,26},{6,24},{8,22},{10,20},{12,18},{14,16},{16,14}... | collective-permute-start | bytes 786440 | tf_op jit(solution)/shard_map/ppermute | solution.py:413
  357.8 179.3 %all-to-all-start = ((bf16[32,4,16,1024]{3,2,1,0:T(8,128)(2,1)}), bf16[32,4,16,1024]{3,2,1,0:T(8,128)(2,1)}, u32[]{:S(2)}, u32[]{:S(2)}) async-start(bf16[32,4,16,1024]{3,2,1,0:T(8,128)(2,1)} %bitcast.15), calls=%async_computation | async-start | bytes 8388608 | tf_op jit(solution)/shard_map/all_to_all | solution.py:417
  385.4 134.9 %copy-start.4 = (f32[1024]{0:T(1024)S(1)}, f32[1024]{0:T(1024)}, u32[]{:S(2)}) copy-start(f32[1024]{0:T(1024)} %param.10) | copy-start | bytes 12292
  385.7 90.2 %collective-permute-start.21 = (bf16[4,256,1024]{2,1,0:T(8,128)(2,1)S(1)}, bf16[4,256,1024]{2,1,0:T(8,128)(2,1)S(1)}, u32[]{:S(2)}, u32[]{:S(2)}) collective-permute-start(bf16[4,256,1024]{2,1,0:T(8,128)(2,1)S(1)} %bitcast.17), channel_id=1, source_target_pairs={{0,1},{1,0},{2,3},{3,2},{4,5},{5,4},{6,7},{7,6},{8,9},{9,8},{10,11... | collective-permute-start | bytes 6291464 | tf_op jit(solution)/shard_map/ppermute | solution.py:413
  387.5 132.9 %collective-permute-start.22 = (bf16[4,256,1024]{2,1,0:T(8,128)(2,1)S(1)}, bf16[4,256,1024]{2,1,0:T(8,128)(2,1)}, u32[]{:S(2)}, u32[]{:S(2)}) collective-permute-start(bf16[4,256,1024]{2,1,0:T(8,128)(2,1)S(1)} %bitcast.18), channel_id=1, source_target_pairs={{0,1},{1,0},{2,3},{3,2},{4,5},{5,4},{6,7},{7,6},{8,9},{9,8},{10,11... | collective-permute-start | bytes 6291464 | tf_op jit(solution)/shard_map/ppermute | solution.py:413
  (16 other events, 320.3 us)

commit v3 on v2

--- a/solution.py
+++ b/solution.py
@@ -29,6 +29,7 @@
         self.out_rows = self.rows // self.ch
         self.channels = self.local * self.ch
         self.mix = mix_weight.shape[1]
+        self.half = self.seq // 2
         self.near = 1
         while self.near * self.near < self.seq:
             self.near *= 2
@@ -141,11 +142,14 @@
     return part.transpose(1, 0, 2, 3).reshape(plan.out_rows, plan.chunk, plan.width)
 
 
-def sections_kernel(plan, count, *refs):
+def sections_kernel(plan, count, split, *refs):
     near, far, own = plan.near, plan.seq // plan.near, plan.own
     pieces, gathered, left = refs[:count], refs[count : count + near], refs[count + near]
-    out, x, right, twiddle, first, mixed, sem_x, sem_r, sem_t = refs[count + near + 1 :]
-    me = lax.axis_index("seq")
+    parts = 1 + plan.half * plan.ch if split else 1
+    outs = refs[count + near + 1 : count + near + 1 + parts]
+    x, right, twiddle, first, mixed, sem_x, sem_r, sem_t, *more = refs[count + near + 1 + parts :]
+    out, sem_o = more if split else (outs[0], None)
+    me, y = lax.axis_index("seq"), lax.axis_index("ch")
     if count == 1:
         copies = [pltpu.make_async_copy(pieces[0], x, sem_x.at[0])]
     else:
@@ -201,21 +205,61 @@
     def turn(t, carry):
         at = pl.ds(pl.multiple_of(t * STEP, STEP), STEP)
         value = jnp.swapaxes(mixed[:, at, :], 0, 1)
-        out[pl.ds(t * STEP, STEP)] = value.astype(jnp.bfloat16)
+        if split:
+            out[pl.ds(t * STEP, STEP), :, ks] = value.astype(jnp.bfloat16)
+        else:
+            out[pl.ds(t * STEP, STEP)] = value.astype(jnp.bfloat16)
         return carry
 
     lax.fori_loop(0, plan.all_rows // STEP, turn, 0)
-
-
-def sections(plan, pieces, gathered, left):
+    if split:
+
+        @pl.when(kt == plan.width // LANES - 1)
+        def _():
+            half = plan.half
+            stores = []
+            for m in range(half):
+                for n in range(plan.ch):
+                    row = jnp.bitwise_xor(me, half + m) * plan.rows
+                    row = row + jnp.bitwise_xor(y, n) * plan.out_rows
+                    stores.append(
+                        pltpu.make_async_copy(
+                            out.at[pl.ds(row, plan.out_rows)],
+                            outs[1 + m * plan.ch + n],
+                            sem_o.at[1 + m * plan.ch + n],
+                        )
+                    )
+            rows = half * plan.rows
+            stores.append(
+                pltpu.make_async_copy(
+                    out.at[pl.ds((me // half) * rows, rows)], outs[0], sem_o.at[0]
+                )
+            )
+            for store in stores:
+                store.start()
+            for store in stores:
+                store.wait()
+
+
+def sections(plan, pieces, gathered, left, split):
     s, own, width, bf16 = plan.seq, plan.own, plan.width, jnp.bfloat16
     flops = 2 * plan.all_rows * own * width * (width + plan.all_rows)
+    scratch = []
+    if split:
+        shapes = [jax.ShapeDtypeStruct((plan.half * plan.rows, own, width), bf16)]
+        shapes += [jax.ShapeDtypeStruct((plan.out_rows, own, width), bf16)] * (plan.half * plan.ch)
+        specs = [ANY] * len(shapes)
+        scratch.append(pltpu.VMEM((plan.all_rows, own, width), bf16))
+        scratch.append(pltpu.SemaphoreType.DMA((len(shapes),)))
+    else:
+        shapes = jax.ShapeDtypeStruct((plan.all_rows, own, width), bf16)
+        specs = pl.BlockSpec((plan.all_rows, own, LANES), lambda k: (0, 0, k))
     return pl.pallas_call(
-        functools.partial(sections_kernel, plan, len(pieces)),
-        out_shape=jax.ShapeDtypeStruct((plan.all_rows, own, width), bf16),
+        functools.partial(sections_kernel, plan, len(pieces), split),
+        out_shape=shapes,
         grid=(width // LANES,),
         in_specs=[ANY] * (len(pieces) + len(gathered)) + [VMEM],
-        out_specs=pl.BlockSpec((plan.all_rows, own, LANES), lambda k: (0, 0, k)),
+        out_specs=specs,
         scratch_shapes=[
             pltpu.VMEM((plan.all_rows, own, width), bf16),
             pltpu.VMEM((s * plan.right_rows, width), bf16),
@@ -225,6 +269,7 @@
             pltpu.SemaphoreType.DMA((s,)),
             pltpu.SemaphoreType.DMA((s,)),
             pltpu.SemaphoreType.DMA((s,)),
+            *scratch,
         ],
         cost_estimate=pl.CostEstimate(
             flops=flops,
@@ -244,6 +289,22 @@
             ).start()
 
 
+def load_halves(plan, block, pieces, mixed, sem):
+    me, y = lax.axis_index("seq"), lax.axis_index("ch")
+    half, own = plan.half, plan.own
+    for r in range(plan.out_rows):
+        for m in range(half * plan.ch):
+            row = (m % plan.ch) * plan.chunk + ((me // half) * half + m // plan.ch) * own
+            pltpu.make_async_copy(
+                block.at[m, r], mixed.at[r, pl.ds(pl.multiple_of(row, own), own)], sem.at[r]
+            ).start()
+            who = jnp.bitwise_xor(me, half + m // plan.ch)
+            row = jnp.bitwise_xor(y, m % plan.ch) * plan.chunk + who * own
+            pltpu.make_async_copy(
+                pieces[m].at[r], mixed.at[r, pl.ds(pl.multiple_of(row, own), own)], sem.at[r]
+            ).start()
+
+
 def load_shares(plan, shares, inputs, sem):
     y = lax.axis_index("ch")
     for r in range(plan.out_rows):
@@ -273,16 +334,18 @@
 
 def gate_kernel(plan, *refs):
     c = plan.ch
-    piece, shares, later = refs[0], refs[1 : 1 + c], refs[1 + c : 1 + 2 * c]
-    gain, weight, out, gates, totals = refs[1 + 2 * c : 6 + 2 * c]
-    mixed, inputs, after, sem_m, sem_i, sem_a = refs[6 + 2 * c :]
+    count = 1 + plan.half * c
+    block, pieces, refs = refs[0], refs[1:count], refs[count:]
+    shares, later = refs[:c], refs[c : 2 * c]
+    gain, weight, out, gates, totals = refs[2 * c : 5 + 2 * c]
+    mixed, inputs, after, sem_m, sem_i, sem_a = refs[5 + 2 * c :]
     i = pl.program_id(0)
 
     @pl.when(i == 0)
     def _():
         load_shares(plan, later, after, sem_a)
         load_shares(plan, shares, inputs, sem_i)
-        load_piece(plan, piece, mixed, sem_m)
+        load_halves(plan, block, pieces, mixed, sem_m)
 
     wait_row(after, sem_a, i)
     wait_row(inputs, sem_i, i)
@@ -355,7 +418,7 @@
         store.wait()
 
 
-def gate(plan, piece, shares, later, gain, weight):
+def gate(plan, pieces, shares, later, gain, weight):
     size, part = plan.out_rows * plan.width, plan.chunk * plan.ch
     shape, bf16 = (plan.out_rows, part, plan.width), jnp.bfloat16
     sem = pltpu.SemaphoreType.DMA((plan.out_rows,))
@@ -367,7 +430,7 @@
             jax.ShapeDtypeStruct((plan.out_rows, 8, plan.width), jnp.float32),
         ],
         grid=(plan.out_rows,),
-        in_specs=[ANY] * (1 + 2 * plan.ch) + [VMEM, VMEM],
+        in_specs=[ANY] * (len(pieces) + 2 * plan.ch) + [VMEM, VMEM],
         out_specs=[
             pl.BlockSpec((plan.width, part), lambda i: (i, 0)),
             pl.BlockSpec((1, part, plan.width), lambda i: (i, 0, 0)),
@@ -380,7 +443,7 @@
             transcendentals=2 * size * part,
         ),
         name="gate",
-    )(piece, *shares, *later, gain, weight)
+    )(*pieces, *shares, *later, gain, weight)
 
 
 def final(plan, piece, gates, held, before, gain, weight):
@@ -443,13 +506,28 @@
         shares.append([share[0]])
         for n in range(1, c):
             shares[k].append(swap(share[n], n, "ch"))
-    landed = []
-    for k in range(CHUNKS):
-        out = sections(plan, arrived[k], gathered, left_block)
-        out = out.reshape(s * c, plan.out_rows, own, plan.width)
-        landed.append(exchange(out, ("seq", "ch")))
-    held, gates, before = gate(plan, landed[0], *shares, gain, mix_weight)
-    return final(plan, landed[1], gates, held, before, gain, mix_weight)
+    half = plan.half
+    block, *pieces = sections(plan, arrived[0], gathered, left_block, True)
+    block = block.reshape(half * c, plan.out_rows, own, plan.width)
+    groups = [[h * half * c + i for i in range(half * c)] for h in range(2)]
+    landed = [
+        lax.all_to_all(
+            block, ("seq", "ch"), 0, 0, axis_index_groups=groups, tiled=True
+        )
+    ]
+    for m in range(half):
+        for n in range(c):
+            landed.append(cross(pieces[m * c + n], half + m, n, s, c))
+    out = sections(plan, arrived[1], gathered, left_block, False)
+    out = out.reshape(s * c, plan.out_rows, own, plan.width)
+    last = exchange(out, ("seq", "ch"))
+    held, gates, before = gate(plan, landed, *shares, gain, mix_weight)
+    return final(plan, last, gates, held, before, gain, mix_weight)
+
+
+def cross(value, seq_mask, ch_mask, s, c):
+    pairs = [(i * c + j, (i ^ seq_mask) * c + (j ^ ch_mask)) for i in range(s) for j in range(c)]
+    return lax.ppermute(value, ("seq", "ch"), pairs)
 
 
 def plain_body(tokens, right_block, twiddle, left_block, gain, mix_weight):

time: 550 us -> 589 us (1.071)
  the two profiles are of different devices: /device:TPU:0 before, /device:TPU:19 now
where the time goes in v3:
time: 589 us; the launch traced here: 588 us
  waiting for transfers between devices  407 us (69%)
  starting transfers between devices  94.9 us (16%)
  Pallas kernels  77.1 us (13%)
  local copies, waits for them, and re-layouts  8.3 us (1%)
    ppermute x23, waiting for transfers between devices, swap(): return lax.ppermute(value, axis, [(i, i ^ mask) for i in range(count)])  370 us
    pallas_call x2, Pallas kernels, sections(): pl.pallas_call(functools.partial(sections_kernel, plan, len(pieces), spli...  40.2 us
    ppermute x23, starting transfers between devices, swap(): return lax.ppermute(value, axis, [(i, i ^ mask) for i in range(count)])  39.8 us
    ppermute x16, starting transfers between devices, cross(): return lax.ppermute(value, ('seq', 'ch'), pairs)  37.9 us
    ppermute x16, waiting for transfers between devices, cross(): return lax.ppermute(value, ('seq', 'ch'), pairs)  37.1 us
    pallas_call x1, Pallas kernels, gate(): pl.pallas_call(functools.partial(gate_kernel, plan), out_shape=[jax.Shape...  15.8 us
    pallas_call x1, Pallas kernels, final(): pl.pallas_call(functools.partial(final_kernel, plan), out_shape=jax.Shape...  12.2 us
  transfers between devices with their start and end apart: 42, of which 23 were waited for; matrix products, arithmetic and copies ran while one was open for 1% of the time, Pallas kernels for 7%

profile of v3, /device:TPU:19, one launch (start us, length us, event | category | flops | bytes accessed | tf_op | source)
XLA Modules:
  0.0 588.5 jit_solution(8105961799859157983)
XLA Ops:
  0.0 3.7 prep.3
  3.7 6.6 %all-to-all-start.1 = ((bf16[16,8,16,1024]{3,2,1,0:T(8,128)(2,1)}), bf16[16,8,16,1024]{3,2,1,0:T(8,128)(2,1)}, u32[]{:S(2)}, u32[]{:S(2)}) async-start(bf16[16,8,16,1024]{3,2,1,0:T(8,128)(2,1)} %prep.3), calls=%async_computation.1 | async-start | bytes 8388608 | tf_op jit(solution)/shard_map/all_to_all | solution.py:480
  13.8 98.1 %collective-permute-done.17 = bf16[1,80,1024]{2,1,0:T(8,128)(2,1)S(1)} collective-permute-done((bf16[1,80,1024]{2,1,0:T(8,128)(2,1)S(1)}, bf16[1,80,1024]{2,1,0:T(8,128)(2,1)S(1)}, u32[]{:S(2)}, u32[]{:S(2)}) %collective-permute-start.17) | collective-permute-done | bytes 163872 | tf_op jit(solution)/shard_map/ppermute | solution.py:476
  117.0 14.7 %collective-permute-done.20.refs_19_.refs_4_ = bf16[4,80,1024]{2,1,0:T(8,128)(2,1)S(1)} collective-permute-done((bf16[4,80,1024]{2,1,0:T(8,128)(2,1)S(1)}, bf16[4,80,1024]{2,1,0:T(8,128)(2,1)S(1)}, u32[]{:S(2)}, u32[]{:S(2)}) %collective-permute-start.20) | collective-permute-done | bytes 655392 | tf_op jit(solution)/shard_map/ppermute | solution.py:476
  131.7 14.0 %collective-permute-done.19.refs_18_.refs_3_ = bf16[4,80,1024]{2,1,0:T(8,128)(2,1)S(1)} collective-permute-done((bf16[4,80,1024]{2,1,0:T(8,128)(2,1)S(1)}, bf16[4,80,1024]{2,1,0:T(8,128)(2,1)S(1)}, u32[]{:S(2)}, u32[]{:S(2)}) %collective-permute-start.19) | collective-permute-done | bytes 655392 | tf_op jit(solution)/shard_map/ppermute | solution.py:476
  146.8 20.8 %sections.3 = (bf16[64,16,1024]{2,1,0:T(8,128)(2,1)}, bf16[4,16,1024]{2,1,0:T(8,128)(2,1)}, bf16[4,16,1024]{2,1,0:T(8,128)(2,1)}, bf16[4,16,1024]{2,1,0:T(8,128)...) custom-call(bf16[128,16,1024]{2,1,0:T(8,128)(2,1)} %bitcast.2.refs_0, ...), custom_call_target="tpu_custom_call" | custom-call | flops 4831838208 | bytes 10485760 | tf_op jit(solution)/shard_map/sections/pallas_call | solution.py:257
  167.6 6.1 %all-to-all-start.2 = ((bf16[16,4,16,1024]{3,2,1,0:T(8,128)(2,1)}), bf16[16,4,16,1024]{3,2,1,0:T(8,128)(2,1)S(1)}, u32[]{:S(2)}, u32[]{:S(2)}) async-start(bf16[16,4,16,1024]{3,2,1,0:T(8,128)(2,1)} %bitcast.16), calls=%async_computation.2 | async-start | bytes 4194304 | tf_op jit(solution)/shard_map/all_to_all | solution.py:514
  173.7 5.2 prep.2
  184.0 21.9 %collective-permute-done.1.refs_2_ = bf16[8,16,1024]{2,1,0:T(8,128)(2,1)S(1)} collective-permute-done((bf16[8,16,1024]{2,1,0:T(8,128)(2,1)}, bf16[8,16,1024]{2,1,0:T(8,128)(2,1)S(1)}, u32[]{:S(2)}, u32[]{:S(2)}) %collective-permute-start.1) | collective-permute-done | bytes 262176 | tf_op jit(solution)/shard_map/ppermute | solution.py:476
  205.9 3.5 collective-permute-start.6
  209.4 13.4 %collective-permute-done.2.refs_3_ = bf16[8,16,1024]{2,1,0:T(8,128)(2,1)S(1)} collective-permute-done((bf16[8,16,1024]{2,1,0:T(8,128)(2,1)}, bf16[8,16,1024]{2,1,0:T(8,128)(2,1)S(1)}, u32[]{:S(2)}, u32[]{:S(2)}) %collective-permute-start.2) | collective-permute-done | bytes 262176 | tf_op jit(solution)/shard_map/ppermute | solution.py:476
  230.7 27.2 %collective-permute-done.7.refs_8_ = bf16[8,16,1024]{2,1,0:T(8,128)(2,1)} collective-permute-done((bf16[8,16,1024]{2,1,0:T(8,128)(2,1)}, bf16[8,16,1024]{2,1,0:T(8,128)(2,1)}, u32[]{:S(2)}, u32[]{:S(2)}) %collective-permute-start.7) | collective-permute-done | bytes 262176 | tf_op jit(solution)/shard_map/ppermute | solution.py:476
  260.0 3.6 collective-permute-done.8.refs_9_
  266.9 7.9 %collective-permute-done.9.refs_10_ = bf16[8,16,1024]{2,1,0:T(8,128)(2,1)} collective-permute-done((bf16[8,16,1024]{2,1,0:T(8,128)(2,1)}, bf16[8,16,1024]{2,1,0:T(8,128)(2,1)}, u32[]{:S(2)}, u32[]{:S(2)}) %collective-permute-start.9) | collective-permute-done | bytes 262176 | tf_op jit(solution)/shard_map/ppermute | solution.py:476
  274.8 9.8 %collective-permute-start.14 = (bf16[8,16,1024]{2,1,0:T(8,128)(2,1)}, bf16[8,16,1024]{2,1,0:T(8,128)(2,1)}, u32[]{:S(2)}, u32[]{:S(2)}) collective-permute-start(bf16[8,16,1024]{2,1,0:T(8,128)(2,1)} %get-tuple-element.58), channel_id=1, source_target_pairs={{0,30},{2,28},{4,26},{6,24},{8,22},{10,20},{12,18},{14,16},{16,14}... | collective-permute-start | bytes 786440 | tf_op jit(solution)/shard_map/ppermute | solution.py:476
  286.1 13.6 %collective-permute-done.11.refs_12_ = bf16[8,16,1024]{2,1,0:T(8,128)(2,1)} collective-permute-done((bf16[8,16,1024]{2,1,0:T(8,128)(2,1)}, bf16[8,16,1024]{2,1,0:T(8,128)(2,1)}, u32[]{:S(2)}, u32[]{:S(2)}) %collective-permute-start.11) | collective-permute-done | bytes 262176 | tf_op jit(solution)/shard_map/ppermute | solution.py:476
  299.6 5.6 collective-permute-done.12.refs_13_
  305.2 7.3 %collective-permute-done.13.refs_14_ = bf16[8,16,1024]{2,1,0:T(8,128)(2,1)} collective-permute-done((bf16[8,16,1024]{2,1,0:T(8,128)(2,1)}, bf16[8,16,1024]{2,1,0:T(8,128)(2,1)}, u32[]{:S(2)}, u32[]{:S(2)}) %collective-permute-start.13) | collective-permute-done | bytes 262176 | tf_op jit(solution)/shard_map/ppermute | solution.py:476
  312.6 5.6 collective-permute-done.14.refs_15_
  318.2 19.5 %sections.2 = bf16[128,16,1024]{2,1,0:T(8,128)(2,1)} custom-call(bf16[8,16,1024]{2,1,0:T(8,128)(2,1)} %get-tuple-element.43.refs_0_, bf16[8,16,1024]{2,1,0:T(8,128)(2,1)} %copy-done.27, bf16[8,16,1024]{2,1,0:T(8,128)(2,1)} %copy-done.28, bf16[8,16,1024]{2,1,0:T(8,128)(2,1)} %copy-done.29, bf16[8,16,1024]{2,1,0:T(8,128)(2,1)} %copy-done.30, ...), custom_call_target="tpu_custom_call" | custom-call | flops 4831838208 | bytes 10485760 | tf_op jit(solution)/shard_map/sections/pallas_call | solution.py:257
  339.0 4.6 all-to-all-start
  353.2 85.6 %collective-permute-done.37.refs_18_ = bf16[4,256,1024]{2,1,0:T(8,128)(2,1)S(1)} collective-permute-done((bf16[4,256,1024]{2,1,0:T(8,128)(2,1)S(1)}, bf16[4,256,1024]{2,1,0:T(8,128)(2,1)S(1)}, u32[]{:S(2)}, u32[]{:S(2)}) %collective-permute-start.37) | collective-permute-done | bytes 2097184 | tf_op jit(solution)/shard_map/ppermute | solution.py:476
  438.8 47.6 %collective-permute-done.38.refs_20_ = bf16[4,256,1024]{2,1,0:T(8,128)(2,1)S(1)} collective-permute-done((bf16[4,256,1024]{2,1,0:T(8,128)(2,1)S(1)}, bf16[4,256,1024]{2,1,0:T(8,128)(2,1)S(1)}, u32[]{:S(2)}, u32[]{:S(2)}) %collective-permute-start.38) | collective-permute-done | bytes 2097184 | tf_op jit(solution)/shard_map/ppermute | solution.py:476
  490.9 3.5 collective-permute-start.28
  494.7 7.9 %collective-permute-done.25.refs_5_ = bf16[4,16,1024]{2,1,0:T(8,128)(2,1)S(1)} collective-permute-done((bf16[4,16,1024]{2,1,0:T(8,128)(2,1)S(1)}, bf16[4,16,1024]{2,1,0:T(8,128)(2,1)S(1)}, u32[]{:S(2)}, u32[]{:S(2)}) %collective-permute-start.25) | collective-permute-done | bytes 131104 | tf_op jit(solution)/shard_map/ppermute | solution.py:530
  511.7 5.2 collective-permute-done.28.refs_8_
  516.8 7.5 %collective-permute-start.33 = (bf16[4,16,1024]{2,1,0:T(8,128)(2,1)S(1)}, bf16[4,16,1024]{2,1,0:T(8,128)(2,1)S(1)}, u32[]{:S(2)}, u32[]{:S(2)}) collective-permute-start(bf16[4,16,1024]{2,1,0:T(8,128)(2,1)S(1)} %copy-done.35), channel_id=1, source_target_pairs={{0,28},{1,29},{2,30},{3,31},{4,24},{5,25},{6,26},{7,27},{8,20},{9,... | collective-permute-start | bytes 393224 | tf_op jit(solution)/shard_map/ppermute | solution.py:530
  527.3 4.6 collective-permute-start.35
  531.9 11.1 %collective-permute-done.31.refs_11_ = bf16[4,16,1024]{2,1,0:T(8,128)(2,1)S(1)} collective-permute-done((bf16[4,16,1024]{2,1,0:T(8,128)(2,1)S(1)}, bf16[4,16,1024]{2,1,0:T(8,128)(2,1)S(1)}, u32[]{:S(2)}, u32[]{:S(2)}) %collective-permute-start.31) | collective-permute-done | bytes 131104 | tf_op jit(solution)/shard_map/ppermute | solution.py:530
  546.1 4.2 collective-permute-done.33.refs_13_
  560.4 15.8 %gate.1 = (bf16[4096,512]{1,0:T(8,128)(2,1)}, bf16[4,512,1024]{2,1,0:T(8,128)(2,1)}, f32[4,8,1024]{2,1,0:T(8,128)}) custom-call(bf16[16,4,16,1024]{3,2,1,0:T(8,128)(2,1)} %copy-done, bf16[4,16,1024]{2,1,0:T(8,128)(2,1)} %copy-done.4, bf16[4,16,1024]{2,1,0:T(8,128)(2,1)} %copy-done.5, bf16[4,16,1024]{2,1,0:T(8,128)(2,1)} %copy-done.6, ...), custom_call_target="tpu_custom_call" | custom-call | flops 1073741824 | bytes 20971520 | tf_op jit(solution)/shard_map/gate/pallas_call | solution.py:425
  576.1 12.2 %final.1 = bf16[4096,1024]{1,0:T(8,128)(2,1)} custom-call(bf16[32,4,16,1024]{3,2,1,0:T(8,128)(2,1)} %all-to-all-done.refs_0_, bf16[4,512,1024]{2,1,0:T(8,128)(2,1)} %get-tuple-element.78.refs_1_, bf16[4096,512]{1,0:T(8,128)(2,1)} %get-tuple-element.79.refs_2_, f32[4,8,1024]{2,1,0:T(8,128)} %get-tuple-element.80.refs_3_, ...), custom_call_target="tpu_custom_call" | custom-call | flops 1073741824 | bytes 20971520 | tf_op jit(solution)/shard_map/final/pallas_call | solution.py:453
  (162 shorter events, 70.1 us)
Async XLA Ops:
  3.7 142.0 %all-to-all-start.1 = ((bf16[16,8,16,1024]{3,2,1,0:T(8,128)(2,1)}), bf16[16,8,16,1024]{3,2,1,0:T(8,128)(2,1)}, u32[]{:S(2)}, u32[]{:S(2)}) async-start(bf16[16,8,16,1024]{3,2,1,0:T(8,128)(2,1)} %prep.3), calls=%async_computation.1 | async-start | bytes 8388608 | tf_op jit(solution)/shard_map/all_to_all | solution.py:480
  10.5 101.4 %collective-permute-start.17 = (bf16[1,80,1024]{2,1,0:T(8,128)(2,1)S(1)}, bf16[1,80,1024]{2,1,0:T(8,128)(2,1)S(1)}, u32[]{:S(2)}, u32[]{:S(2)}) collective-permute-start(bf16[1,80,1024]{2,1,0:T(8,128)(2,1)S(1)} %maximum_bitcast_fusion), channel_id=1, source_target_pairs={{0,24},{2,26},{4,28},{6,30},{8,16},{10,18},{12,20},{14,22},{16,8},... | collective-permute-start | bytes 491528 | tf_op jit(solution)/shard_map/ppermute | solution.py:476
  10.8 103.7 %collective-permute-start.16 = (bf16[1,80,1024]{2,1,0:T(8,128)(2,1)S(1)}, bf16[1,80,1024]{2,1,0:T(8,128)(2,1)S(1)}, u32[]{:S(2)}, u32[]{:S(2)}) collective-permute-start(bf16[1,80,1024]{2,1,0:T(8,128)(2,1)S(1)} %maximum_bitcast_fusion), channel_id=1, source_target_pairs={{0,16},{2,18},{4,20},{6,22},{8,24},{10,26},{12,28},{14,30},{16,0},... | collective-permute-start | bytes 491528 | tf_op jit(solution)/shard_map/ppermute | solution.py:476
  13.8 100.7 %collective-permute-start.15 = (bf16[1,80,1024]{2,1,0:T(8,128)(2,1)S(1)}, bf16[1,80,1024]{2,1,0:T(8,128)(2,1)S(1)}, u32[]{:S(2)}, u32[]{:S(2)}) collective-permute-start(bf16[1,80,1024]{2,1,0:T(8,128)(2,1)S(1)} %maximum_bitcast_fusion), channel_id=1, source_target_pairs={{0,8},{2,10},{4,12},{6,14},{8,0},{10,2},{12,4},{14,6},{16,24},{18,... | collective-permute-start | bytes 491528 | tf_op jit(solution)/shard_map/ppermute | solution.py:476
  115.8 29.9 %collective-permute-start.19 = (bf16[4,80,1024]{2,1,0:T(8,128)(2,1)S(1)}, bf16[4,80,1024]{2,1,0:T(8,128)(2,1)S(1)}, u32[]{:S(2)}, u32[]{:S(2)}) collective-permute-start(bf16[4,80,1024]{2,1,0:T(8,128)(2,1)S(1)} %pad_maximum_fusion.refs_16_.refs_1_), channel_id=1, source_target_pairs={{0,4},{2,6},{4,0},{6,2},{8,12},{10,14},{12,8},{14,10},{16,20},{18,... | collective-permute-start | bytes 1966088 | tf_op jit(solution)/shard_map/ppermute | solution.py:476
  117.0 28.8 %collective-permute-start.18 = (bf16[4,80,1024]{2,1,0:T(8,128)(2,1)S(1)}, bf16[4,80,1024]{2,1,0:T(8,128)(2,1)S(1)}, u32[]{:S(2)}, u32[]{:S(2)}) collective-permute-start(bf16[4,80,1024]{2,1,0:T(8,128)(2,1)S(1)} %pad_maximum_fusion.refs_16_.refs_1_), channel_id=1, source_target_pairs={{0,2},{2,0},{4,6},{6,4},{8,10},{10,8},{12,14},{14,12},{16,18},{18,... | collective-permute-start | bytes 1966088 | tf_op jit(solution)/shard_map/ppermute | solution.py:476
  167.6 170.1 %all-to-all-start.2 = ((bf16[16,4,16,1024]{3,2,1,0:T(8,128)(2,1)}), bf16[16,4,16,1024]{3,2,1,0:T(8,128)(2,1)S(1)}, u32[]{:S(2)}, u32[]{:S(2)}) async-start(bf16[16,4,16,1024]{3,2,1,0:T(8,128)(2,1)} %bitcast.16), calls=%async_computation.2 | async-start | bytes 4194304 | tf_op jit(solution)/shard_map/all_to_all | solution.py:514
  179.4 43.4 %collective-permute-start.2 = (bf16[8,16,1024]{2,1,0:T(8,128)(2,1)}, bf16[8,16,1024]{2,1,0:T(8,128)(2,1)S(1)}, u32[]{:S(2)}, u32[]{:S(2)}) collective-permute-start(bf16[8,16,1024]{2,1,0:T(8,128)(2,1)} %get-tuple-element.46), channel_id=1, source_target_pairs={{0,6},{2,4},{4,2},{6,0},{8,14},{10,12},{12,10},{14,8},{16,22},{18,... | collective-permute-start | bytes 786440 | tf_op jit(solution)/shard_map/ppermute | solution.py:476
  181.1 43.4 %collective-permute-start.3 = (bf16[8,16,1024]{2,1,0:T(8,128)(2,1)}, bf16[8,16,1024]{2,1,0:T(8,128)(2,1)S(1)}, u32[]{:S(2)}, u32[]{:S(2)}) collective-permute-start(bf16[8,16,1024]{2,1,0:T(8,128)(2,1)} %get-tuple-element.47), channel_id=1, source_target_pairs={{0,8},{2,10},{4,12},{6,14},{8,0},{10,2},{12,4},{14,6},{16,24},{18,... | collective-permute-start | bytes 786440 | tf_op jit(solution)/shard_map/ppermute | solution.py:476
  182.3 44.0 %collective-permute-start.4 = (bf16[8,16,1024]{2,1,0:T(8,128)(2,1)}, bf16[8,16,1024]{2,1,0:T(8,128)(2,1)S(1)}, u32[]{:S(2)}, u32[]{:S(2)}) collective-permute-start(bf16[8,16,1024]{2,1,0:T(8,128)(2,1)} %get-tuple-element.48), channel_id=1, source_target_pairs={{0,10},{2,8},{4,14},{6,12},{8,2},{10,0},{12,6},{14,4},{16,26},{18,... | collective-permute-start | bytes 786440 | tf_op jit(solution)/shard_map/ppermute | solution.py:476
  182.9 46.4 %collective-permute-start.5 = (bf16[8,16,1024]{2,1,0:T(8,128)(2,1)}, bf16[8,16,1024]{2,1,0:T(8,128)(2,1)}, u32[]{:S(2)}, u32[]{:S(2)}) collective-permute-start(bf16[8,16,1024]{2,1,0:T(8,128)(2,1)} %get-tuple-element.49), channel_id=1, source_target_pairs={{0,12},{2,14},{4,8},{6,10},{8,4},{10,6},{12,0},{14,2},{16,28},{18,... | collective-permute-start | bytes 786440 | tf_op jit(solution)/shard_map/ppermute | solution.py:476
  222.8 35.2 %collective-permute-start.7 = (bf16[8,16,1024]{2,1,0:T(8,128)(2,1)}, bf16[8,16,1024]{2,1,0:T(8,128)(2,1)}, u32[]{:S(2)}, u32[]{:S(2)}) collective-permute-start(bf16[8,16,1024]{2,1,0:T(8,128)(2,1)} %get-tuple-element.51), channel_id=1, source_target_pairs={{0,16},{2,18},{4,20},{6,22},{8,24},{10,26},{12,28},{14,30},{16,0},... | collective-permute-start | bytes 786440 | tf_op jit(solution)/shard_map/ppermute | solution.py:476
  224.5 39.1 %collective-permute-start.8 = (bf16[8,16,1024]{2,1,0:T(8,128)(2,1)}, bf16[8,16,1024]{2,1,0:T(8,128)(2,1)}, u32[]{:S(2)}, u32[]{:S(2)}) collective-permute-start(bf16[8,16,1024]{2,1,0:T(8,128)(2,1)} %get-tuple-element.52), channel_id=1, source_target_pairs={{0,18},{2,16},{4,22},{6,20},{8,26},{10,24},{12,30},{14,28},{16,2},... | collective-permute-start | bytes 786440 | tf_op jit(solution)/shard_map/ppermute | solution.py:476
  226.3 48.5 %collective-permute-start.9 = (bf16[8,16,1024]{2,1,0:T(8,128)(2,1)}, bf16[8,16,1024]{2,1,0:T(8,128)(2,1)}, u32[]{:S(2)}, u32[]{:S(2)}) collective-permute-start(bf16[8,16,1024]{2,1,0:T(8,128)(2,1)} %get-tuple-element.53), channel_id=1, source_target_pairs={{0,20},{2,22},{4,16},{6,18},{8,28},{10,30},{12,24},{14,26},{16,4},... | collective-permute-start | bytes 786440 | tf_op jit(solution)/shard_map/ppermute | solution.py:476
  229.2 56.8 %collective-permute-start.10 = (bf16[8,16,1024]{2,1,0:T(8,128)(2,1)}, bf16[8,16,1024]{2,1,0:T(8,128)(2,1)}, u32[]{:S(2)}, u32[]{:S(2)}) collective-permute-start(bf16[8,16,1024]{2,1,0:T(8,128)(2,1)} %get-tuple-element.54), channel_id=1, source_target_pairs={{0,22},{2,20},{4,18},{6,16},{8,30},{10,28},{12,26},{14,24},{16,6},... | collective-permute-start | bytes 786440 | tf_op jit(solution)/shard_map/ppermute | solution.py:476
  229.3 70.3 %collective-permute-start.11 = (bf16[8,16,1024]{2,1,0:T(8,128)(2,1)}, bf16[8,16,1024]{2,1,0:T(8,128)(2,1)}, u32[]{:S(2)}, u32[]{:S(2)}) collective-permute-start(bf16[8,16,1024]{2,1,0:T(8,128)(2,1)} %get-tuple-element.55), channel_id=1, source_target_pairs={{0,24},{2,26},{4,28},{6,30},{8,16},{10,18},{12,20},{14,22},{16,8},... | collective-permute-start | bytes 786440 | tf_op jit(solution)/shard_map/ppermute | solution.py:476
  258.0 47.3 %collective-permute-start.12 = (bf16[8,16,1024]{2,1,0:T(8,128)(2,1)}, bf16[8,16,1024]{2,1,0:T(8,128)(2,1)}, u32[]{:S(2)}, u32[]{:S(2)}) collective-permute-start(bf16[8,16,1024]{2,1,0:T(8,128)(2,1)} %get-tuple-element.56), channel_id=1, source_target_pairs={{0,26},{2,24},{4,30},{6,28},{8,18},{10,16},{12,22},{14,20},{16,10}... | collective-permute-start | bytes 786440 | tf_op jit(solution)/shard_map/ppermute | solution.py:476
  263.6 49.0 %collective-permute-start.13 = (bf16[8,16,1024]{2,1,0:T(8,128)(2,1)}, bf16[8,16,1024]{2,1,0:T(8,128)(2,1)}, u32[]{:S(2)}, u32[]{:S(2)}) collective-permute-start(bf16[8,16,1024]{2,1,0:T(8,128)(2,1)} %get-tuple-element.57), channel_id=1, source_target_pairs={{0,28},{2,30},{4,24},{6,26},{8,20},{10,22},{12,16},{14,18},{16,12}... | collective-permute-start | bytes 786440 | tf_op jit(solution)/shard_map/ppermute | solution.py:476
  274.8 43.4 %collective-permute-start.14 = (bf16[8,16,1024]{2,1,0:T(8,128)(2,1)}, bf16[8,16,1024]{2,1,0:T(8,128)(2,1)}, u32[]{:S(2)}, u32[]{:S(2)}) collective-permute-start(bf16[8,16,1024]{2,1,0:T(8,128)(2,1)} %get-tuple-element.58), channel_id=1, source_target_pairs={{0,30},{2,28},{4,26},{6,24},{8,22},{10,20},{12,18},{14,16},{16,14}... | collective-permute-start | bytes 786440 | tf_op jit(solution)/shard_map/ppermute | solution.py:476
  339.0 237.1 %all-to-all-start = ((bf16[32,4,16,1024]{3,2,1,0:T(8,128)(2,1)}), bf16[32,4,16,1024]{3,2,1,0:T(8,128)(2,1)}, u32[]{:S(2)}, u32[]{:S(2)}) async-start(bf16[32,4,16,1024]{3,2,1,0:T(8,128)(2,1)} %bitcast.14), calls=%async_computation | async-start | bytes 8388608 | tf_op jit(solution)/shard_map/all_to_all | solution.py:480
  346.7 92.1 %collective-permute-start.37 = (bf16[4,256,1024]{2,1,0:T(8,128)(2,1)S(1)}, bf16[4,256,1024]{2,1,0:T(8,128)(2,1)S(1)}, u32[]{:S(2)}, u32[]{:S(2)}) collective-permute-start(bf16[4,256,1024]{2,1,0:T(8,128)(2,1)S(1)} %bitcast.17), channel_id=1, source_target_pairs={{0,1},{1,0},{2,3},{3,2},{4,5},{5,4},{6,7},{7,6},{8,9},{9,8},{10,11... | collective-permute-start | bytes 6291464 | tf_op jit(solution)/shard_map/ppermute | solution.py:476
  348.0 138.4 %collective-permute-start.38 = (bf16[4,256,1024]{2,1,0:T(8,128)(2,1)S(1)}, bf16[4,256,1024]{2,1,0:T(8,128)(2,1)S(1)}, u32[]{:S(2)}, u32[]{:S(2)}) collective-permute-start(bf16[4,256,1024]{2,1,0:T(8,128)(2,1)S(1)} %bitcast.18), channel_id=1, source_target_pairs={{0,1},{1,0},{2,3},{3,2},{4,5},{5,4},{6,7},{7,6},{8,9},{9,8},{10,11... | collective-permute-start | bytes 6291464 | tf_op jit(solution)/shard_map/ppermute | solution.py:476
  349.1 137.3 %collective-permute-start.21 = (bf16[4,16,1024]{2,1,0:T(8,128)(2,1)S(1)}, bf16[4,16,1024]{2,1,0:T(8,128)(2,1)S(1)}, u32[]{:S(2)}, u32[]{:S(2)}) collective-permute-start(bf16[4,16,1024]{2,1,0:T(8,128)(2,1)S(1)} %copy-done.47), channel_id=1, source_target_pairs={{0,16},{1,17},{2,18},{3,19},{4,20},{5,21},{6,22},{7,23},{8,24},{9,... | collective-permute-start | bytes 393224 | tf_op jit(solution)/shard_map/ppermute | solution.py:530
  349.4 140.0 %collective-permute-start.22 = (bf16[4,16,1024]{2,1,0:T(8,128)(2,1)S(1)}, bf16[4,16,1024]{2,1,0:T(8,128)(2,1)S(1)}, u32[]{:S(2)}, u32[]{:S(2)}) collective-permute-start(bf16[4,16,1024]{2,1,0:T(8,128)(2,1)S(1)} %copy-done.46), channel_id=1, source_target_pairs={{0,17},{1,16},{2,19},{3,18},{4,21},{5,20},{6,23},{7,22},{8,25},{9,... | collective-permute-start | bytes 393224 | tf_op jit(solution)/shard_map/ppermute | solution.py:530
  351.6 139.3 %collective-permute-start.23 = (bf16[4,16,1024]{2,1,0:T(8,128)(2,1)S(1)}, bf16[4,16,1024]{2,1,0:T(8,128)(2,1)S(1)}, u32[]{:S(2)}, u32[]{:S(2)}) collective-permute-start(bf16[4,16,1024]{2,1,0:T(8,128)(2,1)S(1)} %copy-done.45), channel_id=1, source_target_pairs={{0,18},{1,19},{2,16},{3,17},{4,22},{5,23},{6,20},{7,21},{8,26},{9,... | collective-permute-start | bytes 393224 | tf_op jit(solution)/shard_map/ppermute | solution.py:530
  438.8 55.6 %collective-permute-start.24 = (bf16[4,16,1024]{2,1,0:T(8,128)(2,1)S(1)}, bf16[4,16,1024]{2,1,0:T(8,128)(2,1)S(1)}, u32[]{:S(2)}, u32[]{:S(2)}) collective-permute-start(bf16[4,16,1024]{2,1,0:T(8,128)(2,1)S(1)} %copy-done.44), channel_id=1, source_target_pairs={{0,19},{1,18},{2,17},{3,16},{4,23},{5,22},{6,21},{7,20},{8,27},{9,... | collective-permute-start | bytes 393224 | tf_op jit(solution)/shard_map/ppermute | solution.py:530
  494.4 29.9 %collective-permute-start.29 = (bf16[4,16,1024]{2,1,0:T(8,128)(2,1)S(1)}, bf16[4,16,1024]{2,1,0:T(8,128)(2,1)S(1)}, u32[]{:S(2)}, u32[]{:S(2)}) collective-permute-start(bf16[4,16,1024]{2,1,0:T(8,128)(2,1)S(1)} %copy-done.39), channel_id=1, source_target_pairs={{0,24},{1,25},{2,26},{3,27},{4,28},{5,29},{6,30},{7,31},{8,16},{9,... | collective-permute-start | bytes 393224 | tf_op jit(solution)/shard_map/ppermute | solution.py:530
  505.6 37.4 %collective-permute-start.31 = (bf16[4,16,1024]{2,1,0:T(8,128)(2,1)S(1)}, bf16[4,16,1024]{2,1,0:T(8,128)(2,1)S(1)}, u32[]{:S(2)}, u32[]{:S(2)}) collective-permute-start(bf16[4,16,1024]{2,1,0:T(8,128)(2,1)S(1)} %copy-done.37), channel_id=1, source_target_pairs={{0,26},{1,27},{2,24},{3,25},{4,30},{5,31},{6,28},{7,29},{8,18},{9,... | collective-permute-start | bytes 393224 | tf_op jit(solution)/shard_map/ppermute | solution.py:530
  508.9 37.2 %collective-permute-start.32 = (bf16[4,16,1024]{2,1,0:T(8,128)(2,1)S(1)}, bf16[4,16,1024]{2,1,0:T(8,128)(2,1)S(1)}, u32[]{:S(2)}, u32[]{:S(2)}) collective-permute-start(bf16[4,16,1024]{2,1,0:T(8,128)(2,1)S(1)} %copy-done.36), channel_id=1, source_target_pairs={{0,27},{1,26},{2,25},{3,24},{4,31},{5,30},{6,29},{7,28},{8,19},{9,... | collective-permute-start | bytes 393224 | tf_op jit(solution)/shard_map/ppermute | solution.py:530
  516.8 33.5 %collective-permute-start.33 = (bf16[4,16,1024]{2,1,0:T(8,128)(2,1)S(1)}, bf16[4,16,1024]{2,1,0:T(8,128)(2,1)S(1)}, u32[]{:S(2)}, u32[]{:S(2)}) collective-permute-start(bf16[4,16,1024]{2,1,0:T(8,128)(2,1)S(1)} %copy-done.35), channel_id=1, source_target_pairs={{0,28},{1,29},{2,30},{3,31},{4,24},{5,25},{6,26},{7,27},{8,20},{9,... | collective-permute-start | bytes 393224 | tf_op jit(solution)/shard_map/ppermute | solution.py:530
  524.3 29.0 %collective-permute-start.34 = (bf16[4,16,1024]{2,1,0:T(8,128)(2,1)S(1)}, bf16[4,16,1024]{2,1,0:T(8,128)(2,1)S(1)}, u32[]{:S(2)}, u32[]{:S(2)}) collective-permute-start(bf16[4,16,1024]{2,1,0:T(8,128)(2,1)S(1)} %copy-done.34), channel_id=1, source_target_pairs={{0,29},{1,28},{2,31},{3,30},{4,25},{5,24},{6,27},{7,26},{8,21},{9,... | collective-permute-start | bytes 393224 | tf_op jit(solution)/shard_map/ppermute | solution.py:530
  527.3 28.6 %collective-permute-start.35 = (bf16[4,16,1024]{2,1,0:T(8,128)(2,1)S(1)}, bf16[4,16,1024]{2,1,0:T(8,128)(2,1)S(1)}, u32[]{:S(2)}, u32[]{:S(2)}) collective-permute-start(bf16[4,16,1024]{2,1,0:T(8,128)(2,1)S(1)} %copy-done.33), channel_id=1, source_target_pairs={{0,30},{1,31},{2,28},{3,29},{4,26},{5,27},{6,24},{7,25},{8,22},{9,... | collective-permute-start | bytes 393224 | tf_op jit(solution)/shard_map/ppermute | solution.py:530
  (58 other events, 3598.8 us)

commit v4 on v2

--- a/solution.py
+++ b/solution.py
@@ -13,6 +13,7 @@
 LANES = 256
 CHUNKS = 2
 STEP = 16
+LAST = 1
 
 
 class Plan:
@@ -29,6 +30,7 @@
         self.out_rows = self.rows // self.ch
         self.channels = self.local * self.ch
         self.mix = mix_weight.shape[1]
+        self.half = self.seq // 2
         self.near = 1
         while self.near * self.near < self.seq:
             self.near *= 2
@@ -50,6 +52,7 @@
             and self.rows % 8 == 0
             and STEP % self.rows == 0
             and self.rows % c == 0
+            and self.out_rows > LAST
             and self.all_rows % STEP == 0
             and self.right_rows % 16 == 0
             and self.width % LANES == 0
@@ -141,11 +144,14 @@
     return part.transpose(1, 0, 2, 3).reshape(plan.out_rows, plan.chunk, plan.width)
 
 
-def sections_kernel(plan, count, *refs):
+def sections_kernel(plan, count, full, *refs):
     near, far, own = plan.near, plan.seq // plan.near, plan.own
     pieces, gathered, left = refs[:count], refs[count : count + near], refs[count + near]
-    out, x, right, twiddle, first, mixed, sem_x, sem_r, sem_t = refs[count + near + 1 :]
-    me = lax.axis_index("seq")
+    parts = 1 + plan.half * plan.ch * (2 if full else 1)
+    outs = refs[count + near + 1 : count + near + 1 + parts]
+    x, right, twiddle, first, mixed, out = refs[count + near + 1 + parts : -5]
+    sem_x, sem_r, sem_t, sem_o, sem_l = refs[-5:]
+    me, y = lax.axis_index("seq"), lax.axis_index("ch")
     if count == 1:
         copies = [pltpu.make_async_copy(pieces[0], x, sem_x.at[0])]
     else:
@@ -201,30 +207,56 @@
     def turn(t, carry):
         at = pl.ds(pl.multiple_of(t * STEP, STEP), STEP)
         value = jnp.swapaxes(mixed[:, at, :], 0, 1)
-        out[pl.ds(t * STEP, STEP)] = value.astype(jnp.bfloat16)
+        out[pl.ds(t * STEP, STEP), :, ks] = value.astype(jnp.bfloat16)
         return carry
 
     lax.fori_loop(0, plan.all_rows // STEP, turn, 0)
 
-
-def sections(plan, pieces, gathered, left):
+    @pl.when(kt == plan.width // LANES - 1)
+    def _():
+        half, ways, rows = plan.half, plan.half * plan.ch, plan.out_rows
+        stores = []
+        low = 0 if full else half
+        for m in range((plan.seq - low) * plan.ch):
+            row = jnp.bitwise_xor(me, low + m // plan.ch) * plan.rows
+            row = row + jnp.bitwise_xor(y, m % plan.ch) * rows
+            at = pl.ds(row + full, rows - full)
+            stores.append(pltpu.make_async_copy(out.at[at], outs[1 + m], sem_o.at[m]))
+        for m in range(2 * ways if full else ways):
+            row = m * rows if full else (me // half) * (half * plan.rows) + m * rows
+            at = pl.ds(row, full if full else rows)
+            stores.append(pltpu.make_async_copy(out.at[at], outs[0].at[m], sem_l.at[m]))
+        for store in stores:
+            store.start()
+        for store in stores:
+            store.wait()
+
+
+def sections(plan, pieces, gathered, left, full):
     s, own, width, bf16 = plan.seq, plan.own, plan.width, jnp.bfloat16
     flops = 2 * plan.all_rows * own * width * (width + plan.all_rows)
+    ways = plan.half * plan.ch
+    count = 2 * ways if full else ways
+    shapes = [jax.ShapeDtypeStruct((count, full if full else plan.out_rows, own, width), bf16)]
+    shapes += [jax.ShapeDtypeStruct((plan.out_rows - full, own, width), bf16)] * count
     return pl.pallas_call(
-        functools.partial(sections_kernel, plan, len(pieces)),
-        out_shape=jax.ShapeDtypeStruct((plan.all_rows, own, width), bf16),
+        functools.partial(sections_kernel, plan, len(pieces), full),
+        out_shape=shapes,
         grid=(width // LANES,),
         in_specs=[ANY] * (len(pieces) + len(gathered)) + [VMEM],
-        out_specs=pl.BlockSpec((plan.all_rows, own, LANES), lambda k: (0, 0, k)),
+        out_specs=[ANY] * len(shapes),
         scratch_shapes=[
             pltpu.VMEM((plan.all_rows, own, width), bf16),
             pltpu.VMEM((s * plan.right_rows, width), bf16),
             pltpu.VMEM((s, plan.rows, width), bf16),
             pltpu.VMEM((own, plan.all_rows, LANES), bf16),
             pltpu.VMEM((own, plan.all_rows, LANES), jnp.float32),
+            pltpu.VMEM((plan.all_rows, own, width), bf16),
             pltpu.SemaphoreType.DMA((s,)),
             pltpu.SemaphoreType.DMA((s,)),
             pltpu.SemaphoreType.DMA((s,)),
+            pltpu.SemaphoreType.DMA((2 * ways,)),
+            pltpu.SemaphoreType.DMA((2 * ways,)),
         ],
         cost_estimate=pl.CostEstimate(
             flops=flops,
@@ -236,12 +268,38 @@
 
 
 def load_piece(plan, piece, mixed, sem):
-    for r in range(plan.out_rows):
+    for r in range(piece.shape[1]):
         for m in range(plan.seq * plan.ch):
             row = (m % plan.ch) * plan.chunk + (m // plan.ch) * plan.own
             pltpu.make_async_copy(
                 piece.at[m, r], mixed.at[r, pl.ds(row, plan.own)], sem.at[r]
             ).start()
+
+
+def load_halves(plan, block, pieces, mixed, sem):
+    me, y = lax.axis_index("seq"), lax.axis_index("ch")
+    half, own = plan.half, plan.own
+    for r in range(block.shape[1]):
+        for m in range(half * plan.ch):
+            row = (m % plan.ch) * plan.chunk + ((me // half) * half + m // plan.ch) * own
+            pltpu.make_async_copy(
+                block.at[m, r], mixed.at[r, pl.ds(pl.multiple_of(row, own), own)], sem.at[r]
+            ).start()
+            who = jnp.bitwise_xor(me, half + m // plan.ch)
+            row = jnp.bitwise_xor(y, m % plan.ch) * plan.chunk + who * own
+            pltpu.make_async_copy(
+                pieces[m].at[r], mixed.at[r, pl.ds(pl.multiple_of(row, own), own)], sem.at[r]
+            ).start()
+
+
+def load_pieces(plan, pieces, mixed, sem):
+    me, y = lax.axis_index("seq"), lax.axis_index("ch")
+    for r in range(pieces[0].shape[0]):
+        for m, piece in enumerate(pieces):
+            row = jnp.bitwise_xor(y, m % plan.ch) * plan.chunk
+            row = row + jnp.bitwise_xor(me, m // plan.ch) * plan.own
+            at = pl.ds(pl.multiple_of(row, plan.own), plan.own)
+            pltpu.make_async_copy(piece.at[r], mixed.at[r, at], sem.at[r]).start()
 
 
 def load_shares(plan, shares, inputs, sem):
@@ -273,16 +331,18 @@
 
 def gate_kernel(plan, *refs):
     c = plan.ch
-    piece, shares, later = refs[0], refs[1 : 1 + c], refs[1 + c : 1 + 2 * c]
-    gain, weight, out, gates, totals = refs[1 + 2 * c : 6 + 2 * c]
-    mixed, inputs, after, sem_m, sem_i, sem_a = refs[6 + 2 * c :]
+    count = 1 + plan.half * c
+    block, pieces, refs = refs[0], refs[1:count], refs[count:]
+    shares, later = refs[:c], refs[c : 2 * c]
+    gain, weight, out, gates, totals = refs[2 * c : 5 + 2 * c]
+    mixed, inputs, after, sem_m, sem_i, sem_a = refs[5 + 2 * c :]
     i = pl.program_id(0)
 
     @pl.when(i == 0)
     def _():
         load_shares(plan, later, after, sem_a)
         load_shares(plan, shares, inputs, sem_i)
-        load_piece(plan, piece, mixed, sem_m)
+        load_halves(plan, block, pieces, mixed, sem_m)
 
     wait_row(after, sem_a, i)
     wait_row(inputs, sem_i, i)
@@ -307,24 +367,28 @@
     lax.fori_loop(0, plan.width // LANES, tile, 0)
 
 
-def final_kernel(plan, *refs):
-    piece, gates, held, before, gain, weight, result = refs[:7]
-    mixed, inputs, left, out, sem_m, sem_i, sem_h, sem_o = refs[7:]
+def final_kernel(plan, count, base, rows, *refs):
+    pieces, gates, held, before, gain, weight = refs[:count], *refs[count : count + 5]
+    result = refs[-9]
+    mixed, inputs, left, out, sem_m, sem_i, sem_h, sem_o = refs[-8:]
     c, width = plan.ch, plan.width
-    for r in range(plan.out_rows):
-        pltpu.make_async_copy(gates.at[r], inputs.at[r], sem_i.at[r]).start()
-        at = pl.ds(r * width, width)
+    for r in range(rows):
+        pltpu.make_async_copy(gates.at[base + r], inputs.at[r], sem_i.at[r]).start()
+        at = pl.ds((base + r) * width, width)
         pltpu.make_async_copy(held.at[at], left.at[r], sem_h.at[r]).start()
-    load_piece(plan, piece, mixed, sem_m)
+    if count == 1:
+        load_piece(plan, pieces[0], mixed, sem_m)
+    else:
+        load_pieces(plan, pieces, mixed, sem_m)
     stores = []
-    for r in range(plan.out_rows):
+    for r in range(rows):
         wait_row(mixed, sem_m, r)
         wait_row(inputs, sem_i, r)
         wait_row(left, sem_h, r)
 
         def tile(kt, carry):
             ks = pl.ds(pl.multiple_of(kt * LANES, LANES), LANES)
-            total = before[r, pl.ds(0, 1), ks]
+            total = before[base + r, pl.ds(0, 1), ks]
             parts = []
             for j in range(plan.chunk * c // plan.mix):
                 rs = pl.ds(j * plan.mix, plan.mix)
@@ -348,14 +412,14 @@
 
         lax.fori_loop(0, width // LANES, tile, 0)
         stores.append(
-            pltpu.make_async_copy(out.at[r], result.at[pl.ds(r * width, width)], sem_o.at[r])
+            pltpu.make_async_copy(out.at[r], result.at[pl.ds((base + r) * width, width)], sem_o.at[r])
         )
         stores[-1].start()
     for store in stores:
         store.wait()
 
 
-def gate(plan, piece, shares, later, gain, weight):
+def gate(plan, pieces, shares, later, gain, weight):
     size, part = plan.out_rows * plan.width, plan.chunk * plan.ch
     shape, bf16 = (plan.out_rows, part, plan.width), jnp.bfloat16
     sem = pltpu.SemaphoreType.DMA((plan.out_rows,))
@@ -367,7 +431,7 @@
             jax.ShapeDtypeStruct((plan.out_rows, 8, plan.width), jnp.float32),
         ],
         grid=(plan.out_rows,),
-        in_specs=[ANY] * (1 + 2 * plan.ch) + [VMEM, VMEM],
+        in_specs=[ANY] * (len(pieces) + 2 * plan.ch) + [VMEM, VMEM],
         out_specs=[
             pl.BlockSpec((plan.width, part), lambda i: (i, 0)),
             pl.BlockSpec((1, part, plan.width), lambda i: (i, 0, 0)),
@@ -380,23 +444,29 @@
             transcendentals=2 * size * part,
         ),
         name="gate",
-    )(piece, *shares, *later, gain, weight)
-
-
-def final(plan, piece, gates, held, before, gain, weight):
-    size, part = plan.out_rows * plan.width, plan.chunk * plan.ch
-    shape, bf16 = (plan.out_rows, part, plan.width), jnp.bfloat16
-    sem = pltpu.SemaphoreType.DMA((plan.out_rows,))
+    )(*pieces, *shares, *later, gain, weight)
+
+
+def final(plan, pieces, gates, held, before, gain, weight, base, rows, result=None):
+    size, part = rows * plan.width, plan.chunk * plan.ch
+    shape, bf16 = (rows, part, plan.width), jnp.bfloat16
+    sem = pltpu.SemaphoreType.DMA((rows,))
+    args = [*pieces, gates, held, before, gain, weight]
+    aliases = {}
+    if result is not None:
+        aliases[len(args)] = 0
+        args.append(result)
     return pl.pallas_call(
-        functools.partial(final_kernel, plan),
-        out_shape=jax.ShapeDtypeStruct((size, plan.channels), bf16),
-        in_specs=[ANY] * 3 + [VMEM] * 3,
+        functools.partial(final_kernel, plan, len(pieces), base, rows),
+        out_shape=jax.ShapeDtypeStruct((plan.out_rows * plan.width, plan.channels), bf16),
+        in_specs=[ANY] * (len(pieces) + 2) + [VMEM] * 3 + [ANY] * len(aliases),
         out_specs=ANY,
+        input_output_aliases=aliases,
         scratch_shapes=[
             pltpu.VMEM(shape, bf16),
             pltpu.VMEM(shape, bf16),
-            pltpu.VMEM((plan.out_rows, plan.width, part), bf16),
-            pltpu.VMEM((plan.out_rows, plan.width, plan.channels), bf16),
+            pltpu.VMEM((rows, plan.width, part), bf16),
+            pltpu.VMEM((rows, plan.width, plan.channels), bf16),
         ]
         + [sem] * 4,
         cost_estimate=pl.CostEstimate(
@@ -405,7 +475,7 @@
             transcendentals=0,
         ),
         name="final",
-    )(piece, gates, held, before, gain, weight)
+    )(*args)
 
 
 def swap(value, mask, axis):
@@ -443,13 +513,33 @@
         shares.append([share[0]])
         for n in range(1, c):
             shares[k].append(swap(share[n], n, "ch"))
+    half, ways = plan.half, plan.half * c
+    groups = [[h * ways + i for i in range(ways)] for h in range(2)]
+    first = plan.out_rows - LAST
     landed = []
     for k in range(CHUNKS):
-        out = sections(plan, arrived[k], gathered, left_block)
-        out = out.reshape(s * c, plan.out_rows, own, plan.width)
-        landed.append(exchange(out, ("seq", "ch")))
+        block, *pieces = sections(plan, arrived[k], gathered, left_block, k * first)
+        low = 0 if k else half
+        if k:
+            block = exchange(block, ("seq", "ch"))
+        else:
+            block = lax.all_to_all(block, ("seq", "ch"), 0, 0, axis_index_groups=groups, tiled=True)
+        landed.append([block])
+        for m in range(low, s):
+            for n in range(c):
+                piece = pieces[(m - low) * c + n]
+                if m or n:
+                    piece = cross(piece, m, n, s, c)
+                landed[k].append(piece)
     held, gates, before = gate(plan, landed[0], *shares, gain, mix_weight)
-    return final(plan, landed[1], gates, held, before, gain, mix_weight)
+    rest = (gates, held, before, gain, mix_weight)
+    result = final(plan, landed[1][:1], *rest, 0, first)
+    return final(plan, landed[1][1:], *rest, first, LAST, result)
+
+
+def cross(value, seq_mask, ch_mask, s, c):
+    pairs = [(i * c + j, (i ^ seq_mask) * c + (j ^ ch_mask)) for i in range(s) for j in range(c)]
+    return lax.ppermute(value, ("seq", "ch"), pairs)
 
 
 def plain_body(tokens, right_block, twiddle, left_block, gain, mix_weight):

time: 550 us -> 652 us (1.19)
  starting transfers between devices: 65.3 us -> 171 us
  waiting for transfers between devices: 400 us -> 384 us
  Pallas kernels: 75.5 us -> 83.4 us
    ppermute x23, waiting for transfers between devices: 400 us -> 224 us  [swap(): return lax.ppermute(value, axis, [(i, i ^ mask) for i in range(count)])]
    ppermute x0 -> x47, waiting for transfers between devices: none -> 161 us  [cross(): return lax.ppermute(value, ('seq', 'ch'), pairs)]
    ppermute x0 -> x47, starting transfers between devices: none -> 99.1 us  [cross(): return lax.ppermute(value, ('seq', 'ch'), pairs)]
    pallas_call x3 -> x4, Pallas kernels: 51.2 us -> 58.8 us  [the longest x2 42.3 us: sections(): pl.pallas_call(functools.partial(sections_kernel, plan, len(pieces), full...]
    all_to_all x3 -> x2, starting transfers between devices: 36.2 us -> 35 us  [exchange(): return lax.all_to_all(value, axes, split_axis=0, concat_axis=0, tiled=True)]
  transfers between devices with their start and end apart: 26 -> 73, of which waited for: 16 -> 28; matrix products, arithmetic and copies ran while one was open for 1% -> 1% of each run, Pallas kernels for 7% -> 8%
where the time goes in v4:
time: 652 us
  waiting for transfers between devices  384 us (59%)
  starting transfers between devices  171 us (26%)
  Pallas kernels  83.4 us (13%)
  local copies, waits for them, and re-layouts  11.6 us (2%)
    ppermute x23, waiting for transfers between devices, swap(): return lax.ppermute(value, axis, [(i, i ^ mask) for i in range(count)])  224 us
    ppermute x47, waiting for transfers between devices, cross(): return lax.ppermute(value, ('seq', 'ch'), pairs)  161 us
    ppermute x47, starting transfers between devices, cross(): return lax.ppermute(value, ('seq', 'ch'), pairs)  99.1 us
    pallas_call x2, Pallas kernels, sections(): pl.pallas_call(functools.partial(sections_kernel, plan, len(pieces), full...  42.3 us
    all_to_all x2, starting transfers between devices, exchange(): return lax.all_to_all(value, axes, split_axis=0, concat_axis=0, tiled=True)  35 us
    ppermute x23, starting transfers between devices, swap(): return lax.ppermute(value, axis, [(i, i ^ mask) for i in range(count)])  33 us
    pallas_call x2, Pallas kernels, final(): pl.pallas_call(functools.partial(final_kernel, plan, len(pieces), base, r...  16.6 us
    pallas_call x1, Pallas kernels, gate(): pl.pallas_call(functools.partial(gate_kernel, plan), out_shape=[jax.Shape...  15.8 us
  transfers between devices with their start and end apart: 73, of which 28 were waited for; matrix products, arithmetic and copies ran while one was open for 1% of the time, Pallas kernels for 8%

profile of v4, /device:TPU:0, one launch (start us, length us, event | category | flops | bytes accessed | tf_op | source)
XLA Modules:
  0.0 651.7 jit_solution(4626881908729033150)
XLA Ops:
  0.0 3.7 prep.3
  3.7 7.6 %all-to-all-start = ((bf16[16,8,16,1024]{3,2,1,0:T(8,128)(2,1)}), bf16[16,8,16,1024]{3,2,1,0:T(8,128)(2,1)}, u32[]{:S(2)}, u32[]{:S(2)}) async-start(bf16[16,8,16,1024]{3,2,1,0:T(8,128)(2,1)} %prep.3), calls=%async_computation | async-start | bytes 8388608 | tf_op jit(solution)/shard_map/all_to_all | solution.py:487
  11.5 3.7 collective-permute-start.17
  15.9 72.0 %collective-permute-done.17 = bf16[1,80,1024]{2,1,0:T(8,128)(2,1)S(1)} collective-permute-done((bf16[1,80,1024]{2,1,0:T(8,128)(2,1)S(1)}, bf16[1,80,1024]{2,1,0:T(8,128)(2,1)S(1)}, u32[]{:S(2)}, u32[]{:S(2)}) %collective-permute-start.17) | collective-permute-done | bytes 163872 | tf_op jit(solution)/shard_map/ppermute | solution.py:483
  87.9 31.4 %collective-permute-done.16 = bf16[1,80,1024]{2,1,0:T(8,128)(2,1)S(1)} collective-permute-done((bf16[1,80,1024]{2,1,0:T(8,128)(2,1)S(1)}, bf16[1,80,1024]{2,1,0:T(8,128)(2,1)S(1)}, u32[]{:S(2)}, u32[]{:S(2)}) %collective-permute-start.16) | collective-permute-done | bytes 163872 | tf_op jit(solution)/shard_map/ppermute | solution.py:483
  121.3 15.1 %collective-permute-done.20.refs_19_.refs_4_ = bf16[4,80,1024]{2,1,0:T(8,128)(2,1)S(1)} collective-permute-done((bf16[4,80,1024]{2,1,0:T(8,128)(2,1)S(1)}, bf16[4,80,1024]{2,1,0:T(8,128)(2,1)S(1)}, u32[]{:S(2)}, u32[]{:S(2)}) %collective-permute-start.20) | collective-permute-done | bytes 655392 | tf_op jit(solution)/shard_map/ppermute | solution.py:483
  136.5 14.1 %collective-permute-done.19.refs_18_.refs_3_ = bf16[4,80,1024]{2,1,0:T(8,128)(2,1)S(1)} collective-permute-done((bf16[4,80,1024]{2,1,0:T(8,128)(2,1)S(1)}, bf16[4,80,1024]{2,1,0:T(8,128)(2,1)S(1)}, u32[]{:S(2)}, u32[]{:S(2)}) %collective-permute-start.19) | collective-permute-done | bytes 655392 | tf_op jit(solution)/shard_map/ppermute | solution.py:483
  151.6 21.2 %sections.3 = (bf16[16,4,16,1024]{3,2,1,0:T(8,128)(2,1)}, bf16[4,16,1024]{2,1,0:T(8,128)(2,1)}, bf16[4,16,1024]{2,1,0:T(8,128)(2,1)}, bf16[4,16,1024]{2,1,0:T(8,...) custom-call(bf16[128,16,1024]{2,1,0:T(8,128)(2,1)} %bitcast.1.refs_0, ...), custom_call_target="tpu_custom_call" | custom-call | flops 4831838208 | bytes 10485760 | tf_op jit(solution)/shard_map/sections/pallas_call | solution.py:242
  172.8 3.7 all-to-all-start.1
  176.6 5.2 prep.2
  188.2 23.9 %collective-permute-done.1.refs_2_ = bf16[8,16,1024]{2,1,0:T(8,128)(2,1)S(1)} collective-permute-done((bf16[8,16,1024]{2,1,0:T(8,128)(2,1)}, bf16[8,16,1024]{2,1,0:T(8,128)(2,1)S(1)}, u32[]{:S(2)}, u32[]{:S(2)}) %collective-permute-start.1) | collective-permute-done | bytes 262176 | tf_op jit(solution)/shard_map/ppermute | solution.py:483
  212.1 15.7 %collective-permute-done.2.refs_3_ = bf16[8,16,1024]{2,1,0:T(8,128)(2,1)S(1)} collective-permute-done((bf16[8,16,1024]{2,1,0:T(8,128)(2,1)}, bf16[8,16,1024]{2,1,0:T(8,128)(2,1)S(1)}, u32[]{:S(2)}, u32[]{:S(2)}) %collective-permute-start.2) | collective-permute-done | bytes 262176 | tf_op jit(solution)/shard_map/ppermute | solution.py:483
  236.0 30.4 %collective-permute-done.7.refs_8_ = bf16[8,16,1024]{2,1,0:T(8,128)(2,1)} collective-permute-done((bf16[8,16,1024]{2,1,0:T(8,128)(2,1)}, bf16[8,16,1024]{2,1,0:T(8,128)(2,1)}, u32[]{:S(2)}, u32[]{:S(2)}) %collective-permute-start.7) | collective-permute-done | bytes 262176 | tf_op jit(solution)/shard_map/ppermute | solution.py:483
  266.8 9.6 %collective-permute-done.8.refs_9_ = bf16[8,16,1024]{2,1,0:T(8,128)(2,1)} collective-permute-done((bf16[8,16,1024]{2,1,0:T(8,128)(2,1)}, bf16[8,16,1024]{2,1,0:T(8,128)(2,1)}, u32[]{:S(2)}, u32[]{:S(2)}) %collective-permute-start.8) | collective-permute-done | bytes 262176 | tf_op jit(solution)/shard_map/ppermute | solution.py:483
  277.5 4.9 collective-permute-done.9.refs_10_
  282.5 7.7 %collective-permute-start.14 = (bf16[8,16,1024]{2,1,0:T(8,128)(2,1)}, bf16[8,16,1024]{2,1,0:T(8,128)(2,1)}, u32[]{:S(2)}, u32[]{:S(2)}) collective-permute-start(bf16[8,16,1024]{2,1,0:T(8,128)(2,1)} %get-tuple-element.91), channel_id=1, source_target_pairs={{0,30},{2,28},{4,26},{6,24},{8,22},{10,20},{12,18},{14,16},{16,14}... | collective-permute-start | bytes 786440 | tf_op jit(solution)/shard_map/ppermute | solution.py:483
  291.6 5.3 collective-permute-done.14.refs_15_
  297.0 21.1 %sections.2 = (bf16[32,3,16,1024]{3,2,1,0:T(8,128)(2,1)}, bf16[1,16,1024]{2,1,0:T(8,128)(2,1)}, bf16[1,16,1024]{2,1,0:T(8,128)(2,1)}, bf16[1,16,1024]{2,1,0:T(8,...) custom-call(bf16[8,16,1024]{2,1,0:T(8,128)(2,1)} %get-tuple-element., ...), custom_call_target="tpu_custom_call" | custom-call | flops 4831838208 | bytes 10485760 | tf_op jit(solution)/shard_map/sections/pallas_call | solution.py:242
  319.4 27.4 %all-to-all-start.2 = ((bf16[32,3,16,1024]{3,2,1,0:T(8,128)(2,1)}), bf16[32,3,16,1024]{3,2,1,0:T(8,128)(2,1)S(1)}, u32[]{:S(2)}, u32[]{:S(2)}) async-start(bf16[32,3,16,1024]{3,2,1,0:T(8,128)(2,1)} %get-tuple-element.146), calls=%async_computation.2 | async-start | bytes 6291456 | tf_op jit(solution)/shard_map/all_to_all | solution.py:487
  355.2 119.0 %collective-permute-done.21.refs_1_ = bf16[1,16,1024]{2,1,0:T(8,128)(2,1)S(1)} collective-permute-done((bf16[1,16,1024]{2,1,0:T(8,128)(2,1)S(1)}, bf16[1,16,1024]{2,1,0:T(8,128)(2,1)S(1)}, u32[]{:S(2)}, u32[]{:S(2)}) %collective-permute-start.21) | collective-permute-done | bytes 32800 | tf_op jit(solution)/shard_map/ppermute | solution.py:542
  498.9 5.3 collective-permute-done.36.refs_16_
  520.2 3.8 collective-permute-start.56
  526.2 10.5 %collective-permute-done.54.refs_3_ = bf16[4,16,1024]{2,1,0:T(8,128)(2,1)S(1)} collective-permute-done((bf16[4,16,1024]{2,1,0:T(8,128)(2,1)S(1)}, bf16[4,16,1024]{2,1,0:T(8,128)(2,1)S(1)}, u32[]{:S(2)}, u32[]{:S(2)}) %collective-permute-start.54) | collective-permute-done | bytes 131104 | tf_op jit(solution)/shard_map/ppermute | solution.py:542
  536.6 3.9 collective-permute-start.59
  540.5 7.6 %collective-permute-start.60 = (bf16[4,16,1024]{2,1,0:T(8,128)(2,1)S(1)}, bf16[4,16,1024]{2,1,0:T(8,128)(2,1)S(1)}, u32[]{:S(2)}, u32[]{:S(2)}) collective-permute-start(bf16[4,16,1024]{2,1,0:T(8,128)(2,1)S(1)} %copy-done.66), channel_id=1, source_target_pairs={{0,24},{1,25},{2,26},{3,27},{4,28},{5,29},{6,30},{7,31},{8,16},{9,... | collective-permute-start | bytes 393224 | tf_op jit(solution)/shard_map/ppermute | solution.py:542
  551.8 5.6 collective-permute-done.57.refs_6_
  557.4 5.5 collective-permute-start.63
  563.0 4.2 collective-permute-done.59.refs_8_
  579.0 14.1 %collective-permute-start.42 = (bf16[1,16,1024]{2,1,0:T(8,128)(2,1)}, bf16[1,16,1024]{2,1,0:T(8,128)(2,1)}, u32[]{:S(2)}, u32[]{:S(2)}) collective-permute-start(bf16[1,16,1024]{2,1,0:T(8,128)(2,1)} %get-tuple-element.114), channel_id=1, source_target_pairs={{0,22},{1,23},{2,20},{3,21},{4,18},{5,19},{6,16},{7,17},{8,30},{9,... | collective-permute-start | bytes 98312 | tf_op jit(solution)/shard_map/ppermute | solution.py:542
  605.0 15.8 %gate.1 = (bf16[4096,512]{1,0:T(8,128)(2,1)}, bf16[4,512,1024]{2,1,0:T(8,128)(2,1)}, f32[4,8,1024]{2,1,0:T(8,128)}) custom-call(bf16[16,4,16,1024]{3,2,1,0:T(8,128)(2,1)} %copy-done.1, bf16[4,16,1024]{2,1,0:T(8,128)(2,1)} %copy-done.5, bf16[4,16,1024]{2,1,0:T(8,128)(2,1)} %copy-done.6, bf16[4,16,1024]{2,1,0:T(8,128)(2,1)} %copy-done.7, ...), custom_call_target="tpu_custom_call" | custom-call | flops 1073741824 | bytes 20971520 | tf_op jit(solution)/shard_map/gate/pallas_call | solution.py:426
  634.3 10.2 %final.2.refs_37_ = bf16[4096,1024]{1,0:T(8,128)(2,1)} custom-call(bf16[32,3,16,1024]{3,2,1,0:T(8,128)(2,1)} %copy-done, bf16[4,512,1024]{2,1,0:T(8,128)(2,1)} %get-tuple-element.143.refs_1_.refs_32_, bf16[4096,512]{1,0:T(8,128)(2,1)} %get-tuple-element.144.refs_2_.refs_33_, f32[4,8,1024]{2,1,0:T(8,128)} %get-tuple-element.145.refs_3_.refs_34_, ...), custom_call_target="tpu_custom_call" | custom-call | flops 805306368 | bytes 15728640 | tf_op jit(solution)/shard_map/final/pallas_call | solution.py:459
  645.2 6.3 final.3
  (321 shorter events, 115.0 us)
Async XLA Ops:
  3.7 146.9 %all-to-all-start = ((bf16[16,8,16,1024]{3,2,1,0:T(8,128)(2,1)}), bf16[16,8,16,1024]{3,2,1,0:T(8,128)(2,1)}, u32[]{:S(2)}, u32[]{:S(2)}) async-start(bf16[16,8,16,1024]{3,2,1,0:T(8,128)(2,1)} %prep.3), calls=%async_computation | async-start | bytes 8388608 | tf_op jit(solution)/shard_map/all_to_all | solution.py:487
  11.5 76.4 %collective-permute-start.17 = (bf16[1,80,1024]{2,1,0:T(8,128)(2,1)S(1)}, bf16[1,80,1024]{2,1,0:T(8,128)(2,1)S(1)}, u32[]{:S(2)}, u32[]{:S(2)}) collective-permute-start(bf16[1,80,1024]{2,1,0:T(8,128)(2,1)S(1)} %maximum_bitcast_fusion), channel_id=1, source_target_pairs={{0,24},{2,26},{4,28},{6,30},{8,16},{10,18},{12,20},{14,22},{16,8},... | collective-permute-start | bytes 491528 | tf_op jit(solution)/shard_map/ppermute | solution.py:483
  15.2 104.1 %collective-permute-start.16 = (bf16[1,80,1024]{2,1,0:T(8,128)(2,1)S(1)}, bf16[1,80,1024]{2,1,0:T(8,128)(2,1)S(1)}, u32[]{:S(2)}, u32[]{:S(2)}) collective-permute-start(bf16[1,80,1024]{2,1,0:T(8,128)(2,1)S(1)} %maximum_bitcast_fusion), channel_id=1, source_target_pairs={{0,16},{2,18},{4,20},{6,22},{8,24},{10,26},{12,28},{14,30},{16,0},... | collective-permute-start | bytes 491528 | tf_op jit(solution)/shard_map/ppermute | solution.py:483
  15.2 104.1 %collective-permute-start.15 = (bf16[1,80,1024]{2,1,0:T(8,128)(2,1)S(1)}, bf16[1,80,1024]{2,1,0:T(8,128)(2,1)S(1)}, u32[]{:S(2)}, u32[]{:S(2)}) collective-permute-start(bf16[1,80,1024]{2,1,0:T(8,128)(2,1)S(1)} %maximum_bitcast_fusion), channel_id=1, source_target_pairs={{0,8},{2,10},{4,12},{6,14},{8,0},{10,2},{12,4},{14,6},{16,24},{18,... | collective-permute-start | bytes 491528 | tf_op jit(solution)/shard_map/ppermute | solution.py:483
  120.1 30.5 %collective-permute-start.19 = (bf16[4,80,1024]{2,1,0:T(8,128)(2,1)S(1)}, bf16[4,80,1024]{2,1,0:T(8,128)(2,1)S(1)}, u32[]{:S(2)}, u32[]{:S(2)}) collective-permute-start(bf16[4,80,1024]{2,1,0:T(8,128)(2,1)S(1)} %pad_maximum_fusion.refs_16_.refs_1_), channel_id=1, source_target_pairs={{0,4},{2,6},{4,0},{6,2},{8,12},{10,14},{12,8},{14,10},{16,20},{18,... | collective-permute-start | bytes 1966088 | tf_op jit(solution)/shard_map/ppermute | solution.py:483
  121.0 29.5 %collective-permute-start.18 = (bf16[4,80,1024]{2,1,0:T(8,128)(2,1)S(1)}, bf16[4,80,1024]{2,1,0:T(8,128)(2,1)S(1)}, u32[]{:S(2)}, u32[]{:S(2)}) collective-permute-start(bf16[4,80,1024]{2,1,0:T(8,128)(2,1)S(1)} %pad_maximum_fusion.refs_16_.refs_1_), channel_id=1, source_target_pairs={{0,2},{2,0},{4,6},{6,4},{8,10},{10,8},{12,14},{14,12},{16,18},{18,... | collective-permute-start | bytes 1966088 | tf_op jit(solution)/shard_map/ppermute | solution.py:483
  172.8 145.3 %all-to-all-start.1 = ((bf16[16,4,16,1024]{3,2,1,0:T(8,128)(2,1)}), bf16[16,4,16,1024]{3,2,1,0:T(8,128)(2,1)S(1)}, u32[]{:S(2)}, u32[]{:S(2)}) async-start(bf16[16,4,16,1024]{3,2,1,0:T(8,128)(2,1)} %get-tuple-element.124), calls=%async_computation.1 | async-start | bytes 4194304 | tf_op jit(solution)/shard_map/all_to_all | solution.py:526
  182.1 30.1 %collective-permute-start.1 = (bf16[8,16,1024]{2,1,0:T(8,128)(2,1)}, bf16[8,16,1024]{2,1,0:T(8,128)(2,1)S(1)}, u32[]{:S(2)}, u32[]{:S(2)}) collective-permute-start(bf16[8,16,1024]{2,1,0:T(8,128)(2,1)} %get-tuple-element.78), channel_id=1, source_target_pairs={{0,4},{2,6},{4,0},{6,2},{8,12},{10,14},{12,8},{14,10},{16,20},{18,... | collective-permute-start | bytes 786440 | tf_op jit(solution)/shard_map/ppermute | solution.py:483
  183.7 44.1 %collective-permute-start.2 = (bf16[8,16,1024]{2,1,0:T(8,128)(2,1)}, bf16[8,16,1024]{2,1,0:T(8,128)(2,1)S(1)}, u32[]{:S(2)}, u32[]{:S(2)}) collective-permute-start(bf16[8,16,1024]{2,1,0:T(8,128)(2,1)} %get-tuple-element.79), channel_id=1, source_target_pairs={{0,6},{2,4},{4,2},{6,0},{8,14},{10,12},{12,10},{14,8},{16,22},{18,... | collective-permute-start | bytes 786440 | tf_op jit(solution)/shard_map/ppermute | solution.py:483
  183.7 45.0 %collective-permute-start.3 = (bf16[8,16,1024]{2,1,0:T(8,128)(2,1)}, bf16[8,16,1024]{2,1,0:T(8,128)(2,1)S(1)}, u32[]{:S(2)}, u32[]{:S(2)}) collective-permute-start(bf16[8,16,1024]{2,1,0:T(8,128)(2,1)} %get-tuple-element.80), channel_id=1, source_target_pairs={{0,8},{2,10},{4,12},{6,14},{8,0},{10,2},{12,4},{14,6},{16,24},{18,... | collective-permute-start | bytes 786440 | tf_op jit(solution)/shard_map/ppermute | solution.py:483
  185.5 45.0 %collective-permute-start.4 = (bf16[8,16,1024]{2,1,0:T(8,128)(2,1)}, bf16[8,16,1024]{2,1,0:T(8,128)(2,1)S(1)}, u32[]{:S(2)}, u32[]{:S(2)}) collective-permute-start(bf16[8,16,1024]{2,1,0:T(8,128)(2,1)} %get-tuple-element.81), channel_id=1, source_target_pairs={{0,10},{2,8},{4,14},{6,12},{8,2},{10,0},{12,6},{14,4},{16,26},{18,... | collective-permute-start | bytes 786440 | tf_op jit(solution)/shard_map/ppermute | solution.py:483
  185.6 45.0 %collective-permute-start.5 = (bf16[8,16,1024]{2,1,0:T(8,128)(2,1)}, bf16[8,16,1024]{2,1,0:T(8,128)(2,1)}, u32[]{:S(2)}, u32[]{:S(2)}) collective-permute-start(bf16[8,16,1024]{2,1,0:T(8,128)(2,1)} %get-tuple-element.82), channel_id=1, source_target_pairs={{0,12},{2,14},{4,8},{6,10},{8,4},{10,6},{12,0},{14,2},{16,28},{18,... | collective-permute-start | bytes 786440 | tf_op jit(solution)/shard_map/ppermute | solution.py:483
  227.8 38.5 %collective-permute-start.7 = (bf16[8,16,1024]{2,1,0:T(8,128)(2,1)}, bf16[8,16,1024]{2,1,0:T(8,128)(2,1)}, u32[]{:S(2)}, u32[]{:S(2)}) collective-permute-start(bf16[8,16,1024]{2,1,0:T(8,128)(2,1)} %get-tuple-element.84), channel_id=1, source_target_pairs={{0,16},{2,18},{4,20},{6,22},{8,24},{10,26},{12,28},{14,30},{16,0},... | collective-permute-start | bytes 786440 | tf_op jit(solution)/shard_map/ppermute | solution.py:483
  228.8 47.6 %collective-permute-start.8 = (bf16[8,16,1024]{2,1,0:T(8,128)(2,1)}, bf16[8,16,1024]{2,1,0:T(8,128)(2,1)}, u32[]{:S(2)}, u32[]{:S(2)}) collective-permute-start(bf16[8,16,1024]{2,1,0:T(8,128)(2,1)} %get-tuple-element.85), channel_id=1, source_target_pairs={{0,18},{2,16},{4,22},{6,20},{8,26},{10,24},{12,30},{14,28},{16,2},... | collective-permute-start | bytes 786440 | tf_op jit(solution)/shard_map/ppermute | solution.py:483
  230.5 52.0 %collective-permute-start.9 = (bf16[8,16,1024]{2,1,0:T(8,128)(2,1)}, bf16[8,16,1024]{2,1,0:T(8,128)(2,1)}, u32[]{:S(2)}, u32[]{:S(2)}) collective-permute-start(bf16[8,16,1024]{2,1,0:T(8,128)(2,1)} %get-tuple-element.86), channel_id=1, source_target_pairs={{0,20},{2,22},{4,16},{6,18},{8,28},{10,30},{12,24},{14,26},{16,4},... | collective-permute-start | bytes 786440 | tf_op jit(solution)/shard_map/ppermute | solution.py:483
  230.5 61.1 %collective-permute-start.10 = (bf16[8,16,1024]{2,1,0:T(8,128)(2,1)}, bf16[8,16,1024]{2,1,0:T(8,128)(2,1)}, u32[]{:S(2)}, u32[]{:S(2)}) collective-permute-start(bf16[8,16,1024]{2,1,0:T(8,128)(2,1)} %get-tuple-element.87), channel_id=1, source_target_pairs={{0,22},{2,20},{4,18},{6,16},{8,30},{10,28},{12,26},{14,24},{16,6},... | collective-permute-start | bytes 786440 | tf_op jit(solution)/shard_map/ppermute | solution.py:483
  234.1 57.6 %collective-permute-start.11 = (bf16[8,16,1024]{2,1,0:T(8,128)(2,1)}, bf16[8,16,1024]{2,1,0:T(8,128)(2,1)}, u32[]{:S(2)}, u32[]{:S(2)}) collective-permute-start(bf16[8,16,1024]{2,1,0:T(8,128)(2,1)} %get-tuple-element.88), channel_id=1, source_target_pairs={{0,24},{2,26},{4,28},{6,30},{8,16},{10,18},{12,20},{14,22},{16,8},... | collective-permute-start | bytes 786440 | tf_op jit(solution)/shard_map/ppermute | solution.py:483
  319.4 313.1 %all-to-all-start.2 = ((bf16[32,3,16,1024]{3,2,1,0:T(8,128)(2,1)}), bf16[32,3,16,1024]{3,2,1,0:T(8,128)(2,1)S(1)}, u32[]{:S(2)}, u32[]{:S(2)}) async-start(bf16[32,3,16,1024]{3,2,1,0:T(8,128)(2,1)} %get-tuple-element.146), calls=%async_computation.2 | async-start | bytes 6291456 | tf_op jit(solution)/shard_map/all_to_all | solution.py:487
  350.3 167.2 %collective-permute-start.68 = (bf16[4,256,1024]{2,1,0:T(8,128)(2,1)S(1)}, bf16[4,256,1024]{2,1,0:T(8,128)(2,1)S(1)}, u32[]{:S(2)}, u32[]{:S(2)}) collective-permute-start(bf16[4,256,1024]{2,1,0:T(8,128)(2,1)S(1)} %bitcast.13), channel_id=1, source_target_pairs={{0,1},{1,0},{2,3},{3,2},{4,5},{5,4},{6,7},{7,6},{8,9},{9,8},{10,11... | collective-permute-start | bytes 6291464 | tf_op jit(solution)/shard_map/ppermute | solution.py:483
  352.0 168.2 %collective-permute-start.69 = (bf16[4,256,1024]{2,1,0:T(8,128)(2,1)S(1)}, bf16[4,256,1024]{2,1,0:T(8,128)(2,1)S(1)}, u32[]{:S(2)}, u32[]{:S(2)}) collective-permute-start(bf16[4,256,1024]{2,1,0:T(8,128)(2,1)S(1)} %bitcast.14), channel_id=1, source_target_pairs={{0,1},{1,0},{2,3},{3,2},{4,5},{5,4},{6,7},{7,6},{8,9},{9,8},{10,11... | collective-permute-start | bytes 6291464 | tf_op jit(solution)/shard_map/ppermute | solution.py:483
  353.1 121.1 %collective-permute-start.21 = (bf16[1,16,1024]{2,1,0:T(8,128)(2,1)S(1)}, bf16[1,16,1024]{2,1,0:T(8,128)(2,1)S(1)}, u32[]{:S(2)}, u32[]{:S(2)}) collective-permute-start(bf16[1,16,1024]{2,1,0:T(8,128)(2,1)S(1)} %copy-done.95), channel_id=1, source_target_pairs={{0,1},{1,0},{2,3},{3,2},{4,5},{5,4},{6,7},{7,6},{8,9},{9,8},{10,11... | collective-permute-start | bytes 98312 | tf_op jit(solution)/shard_map/ppermute | solution.py:542
  354.0 121.4 %collective-permute-start.22 = (bf16[1,16,1024]{2,1,0:T(8,128)(2,1)S(1)}, bf16[1,16,1024]{2,1,0:T(8,128)(2,1)S(1)}, u32[]{:S(2)}, u32[]{:S(2)}) collective-permute-start(bf16[1,16,1024]{2,1,0:T(8,128)(2,1)S(1)} %copy-done.94), channel_id=1, source_target_pairs={{0,2},{1,3},{2,0},{3,1},{4,6},{5,7},{6,4},{7,5},{8,10},{9,11},{10,... | collective-permute-start | bytes 98312 | tf_op jit(solution)/shard_map/ppermute | solution.py:542
  354.0 122.1 %collective-permute-start.23 = (bf16[1,16,1024]{2,1,0:T(8,128)(2,1)S(1)}, bf16[1,16,1024]{2,1,0:T(8,128)(2,1)S(1)}, u32[]{:S(2)}, u32[]{:S(2)}) collective-permute-start(bf16[1,16,1024]{2,1,0:T(8,128)(2,1)S(1)} %copy-done.93), channel_id=1, source_target_pairs={{0,3},{1,2},{2,1},{3,0},{4,7},{5,6},{6,5},{7,4},{8,11},{9,10},{10,... | collective-permute-start | bytes 98312 | tf_op jit(solution)/shard_map/ppermute | solution.py:542
  493.5 30.6 %collective-permute-start.52 = (bf16[4,16,1024]{2,1,0:T(8,128)(2,1)S(1)}, bf16[4,16,1024]{2,1,0:T(8,128)(2,1)S(1)}, u32[]{:S(2)}, u32[]{:S(2)}) collective-permute-start(bf16[4,16,1024]{2,1,0:T(8,128)(2,1)S(1)} %copy-done.74), channel_id=1, source_target_pairs={{0,16},{1,17},{2,18},{3,19},{4,20},{5,21},{6,22},{7,23},{8,24},{9,... | collective-permute-start | bytes 393224 | tf_op jit(solution)/shard_map/ppermute | solution.py:542
  520.2 31.5 %collective-permute-start.56 = (bf16[4,16,1024]{2,1,0:T(8,128)(2,1)S(1)}, bf16[4,16,1024]{2,1,0:T(8,128)(2,1)S(1)}, u32[]{:S(2)}, u32[]{:S(2)}) collective-permute-start(bf16[4,16,1024]{2,1,0:T(8,128)(2,1)S(1)} %copy-done.70), channel_id=1, source_target_pairs={{0,20},{1,21},{2,22},{3,23},{4,16},{5,17},{6,18},{7,19},{8,28},{9,... | collective-permute-start | bytes 393224 | tf_op jit(solution)/shard_map/ppermute | solution.py:542
  524.1 33.3 %collective-permute-start.57 = (bf16[4,16,1024]{2,1,0:T(8,128)(2,1)S(1)}, bf16[4,16,1024]{2,1,0:T(8,128)(2,1)S(1)}, u32[]{:S(2)}, u32[]{:S(2)}) collective-permute-start(bf16[4,16,1024]{2,1,0:T(8,128)(2,1)S(1)} %copy-done.69), channel_id=1, source_target_pairs={{0,21},{1,20},{2,23},{3,22},{4,17},{5,16},{6,19},{7,18},{8,29},{9,... | collective-permute-start | bytes 393224 | tf_op jit(solution)/shard_map/ppermute | solution.py:542
  524.9 32.6 %collective-permute-start.58 = (bf16[4,16,1024]{2,1,0:T(8,128)(2,1)S(1)}, bf16[4,16,1024]{2,1,0:T(8,128)(2,1)S(1)}, u32[]{:S(2)}, u32[]{:S(2)}) collective-permute-start(bf16[4,16,1024]{2,1,0:T(8,128)(2,1)S(1)} %copy-done.68), channel_id=1, source_target_pairs={{0,22},{1,23},{2,20},{3,21},{4,18},{5,19},{6,16},{7,17},{8,30},{9,... | collective-permute-start | bytes 393224 | tf_op jit(solution)/shard_map/ppermute | solution.py:542
  536.6 30.5 %collective-permute-start.59 = (bf16[4,16,1024]{2,1,0:T(8,128)(2,1)S(1)}, bf16[4,16,1024]{2,1,0:T(8,128)(2,1)S(1)}, u32[]{:S(2)}, u32[]{:S(2)}) collective-permute-start(bf16[4,16,1024]{2,1,0:T(8,128)(2,1)S(1)} %copy-done.67), channel_id=1, source_target_pairs={{0,23},{1,22},{2,21},{3,20},{4,19},{5,18},{6,17},{7,16},{8,31},{9,... | collective-permute-start | bytes 393224 | tf_op jit(solution)/shard_map/ppermute | solution.py:542
  579.0 41.8 %collective-permute-start.42 = (bf16[1,16,1024]{2,1,0:T(8,128)(2,1)}, bf16[1,16,1024]{2,1,0:T(8,128)(2,1)}, u32[]{:S(2)}, u32[]{:S(2)}) collective-permute-start(bf16[1,16,1024]{2,1,0:T(8,128)(2,1)} %get-tuple-element.114), channel_id=1, source_target_pairs={{0,22},{1,23},{2,20},{3,21},{4,18},{5,19},{6,16},{7,17},{8,30},{9,... | collective-permute-start | bytes 98312 | tf_op jit(solution)/shard_map/ppermute | solution.py:542
  593.2 29.3 %collective-permute-start.43 = (bf16[1,16,1024]{2,1,0:T(8,128)(2,1)}, bf16[1,16,1024]{2,1,0:T(8,128)(2,1)}, u32[]{:S(2)}, u32[]{:S(2)}) collective-permute-start(bf16[1,16,1024]{2,1,0:T(8,128)(2,1)} %get-tuple-element.115), channel_id=1, source_target_pairs={{0,23},{1,22},{2,21},{3,20},{4,19},{5,18},{6,17},{7,16},{8,31},{9,... | collective-permute-start | bytes 98312 | tf_op jit(solution)/shard_map/ppermute | solution.py:542
  597.9 28.9 %collective-permute-start.45 = (bf16[1,16,1024]{2,1,0:T(8,128)(2,1)}, bf16[1,16,1024]{2,1,0:T(8,128)(2,1)}, u32[]{:S(2)}, u32[]{:S(2)}) collective-permute-start(bf16[1,16,1024]{2,1,0:T(8,128)(2,1)} %get-tuple-element.117), channel_id=1, source_target_pairs={{0,25},{1,24},{2,27},{3,26},{4,29},{5,28},{6,31},{7,30},{8,17},{9,... | collective-permute-start | bytes 98312 | tf_op jit(solution)/shard_map/ppermute | solution.py:542
  600.5 29.8 %collective-permute-start.46 = (bf16[1,16,1024]{2,1,0:T(8,128)(2,1)}, bf16[1,16,1024]{2,1,0:T(8,128)(2,1)}, u32[]{:S(2)}, u32[]{:S(2)}) collective-permute-start(bf16[1,16,1024]{2,1,0:T(8,128)(2,1)} %get-tuple-element.118), channel_id=1, source_target_pairs={{0,26},{1,27},{2,24},{3,25},{4,30},{5,31},{6,28},{7,29},{8,18},{9,... | collective-permute-start | bytes 98312 | tf_op jit(solution)/shard_map/ppermute | solution.py:542
  (137 other events, 9634.8 us)
